TPU v7x, 1024 devices: a whole 8x8x8 slice. The times are simulated.
1024 devices in a mesh: gx: 8 (over y), gy: 8 (over x), gz: 16 (over z, core).
Axes of the slice: x: 8, y: 8, z: 8, core: 2. Of those that a mesh axis runs over, the one named last changes fastest.
Arguments:
- fields: float32 [5, 256, 128, 1024], P(None, 'gz', 'gx', 'gy'), may hold values from -6 to 6
- tile_writer: int32 [8, 8, 1280, 1], P('gx', 'gy', 'gz'), may hold values from 0 to 63; in each aligned block of 80 rows (0 to 79, 80 to 159, ..., all dimensions but the last counted through in order) at most 2 rows name the same one
Outputs:
- coarse_bands: float32 [5, 32, 16, 128], P(None, None, 'gx', 'gy')
- received: float32 [8192, 32768], P(('gx', 'gy'), 'gz')
Inputs may be any that keep to these rules, and one draw needn't show every extreme that they name: `tile_writer`: within each device's 80 entries, no destination is named more than 2 times, a bound that some block reaches.
All inputs are finite; a program needn't handle non-finite values.
Results may differ from a plain program's by a relative error of at most 0.00014.
Values sent between devices are 32-bit elements; how exact they have to be, the bound alone decides.
No kernel may reach another device: no remote copies, remote signals or barrier semaphores. Data moves between devices by JAX's collectives and lax.ppermute only.
A program may use at most 64 MiB of HBM per device.

v0:
```python
import jax
import jax.numpy as jnp
from jax import lax
from jax.sharding import PartitionSpec as P

TILE_ROWS = 16


PREDICT_ONE = -1.586134342059924
UPDATE_ONE = -0.052980118572961
PREDICT_TWO = 0.882911075530934
UPDATE_TWO = 0.443506852043971
LOW_SCALE = 1.0 / 1.149604398860241
HIGH_SCALE = 1.149604398860241


def with_halo(block, sides, width):
    for axis, dim in sides:
        count = lax.axis_size(axis)
        forward = [(i, i + 1) for i in range(count - 1)]
        forward.append((count - 1, 0))
        backward = [(target, source) for source, target in forward]
        low = lax.ppermute(
            lax.slice_in_dim(block, block.shape[dim] - width, None, axis=dim), axis, forward
        )
        high = lax.ppermute(lax.slice_in_dim(block, 0, width, axis=dim), axis, backward)
        block = jnp.concatenate([low, block, high], axis=dim)
    return block


def lifting(values, along):
    length = values.shape[along]
    low_band = lax.slice_in_dim(values, 0, length, 2, along)
    high_band = lax.slice_in_dim(values, 1, length, 2, along)
    high_band = high_band + PREDICT_ONE * (low_band + jnp.roll(low_band, -1, along))
    low_band = low_band + UPDATE_ONE * (jnp.roll(high_band, 1, along) + high_band)
    high_band = high_band + PREDICT_TWO * (low_band + jnp.roll(low_band, -1, along))
    low_band = low_band + UPDATE_TWO * (jnp.roll(high_band, 1, along) + high_band)
    low_band = low_band * LOW_SCALE
    high_band = high_band * HIGH_SCALE
    joined = jnp.stack([low_band, high_band], axis=along + 1)
    return joined.reshape(values.shape)


def transform_matrix(length):
    identity = jnp.eye(length + 8, dtype=jnp.float32)
    return lifting(identity, 1)[:, 4:-4]


def apply_along(values, length, dim):
    matrix = transform_matrix(length)
    if dim == 1:
        return jnp.einsum("fzxy,zk->fkxy", values, matrix, precision=lax.Precision.HIGHEST)
    if dim == 2:
        return jnp.einsum("fzxy,xk->fzky", values, matrix, precision=lax.Precision.HIGHEST)
    return jnp.einsum("fzxy,yk->fzxk", values, matrix, precision=lax.Precision.HIGHEST)


def one_level(bricks):
    depth_z = bricks.shape[1]
    depth_x = bricks.shape[2]
    depth_y = bricks.shape[3]
    padded = with_halo(bricks, (("gx", 2), ("gy", 3), ("gz", 1)), 4)
    result = apply_along(padded, depth_y, 3)
    result = apply_along(result, depth_x, 2)
    return apply_along(result, depth_z, 1)


def body(fields, tile_writer):
    results = []
    current = fields
    for depth in range(3):
        result = one_level(current)
        results.append(result)
        current = result[:, ::2, ::2, ::2]
    merged = results[2]
    for depth in (1, 0):
        merged = results[depth].at[:, ::2, ::2, ::2].set(merged)
    gathered = lax.all_gather(current, "gz", axis=1, tiled=True)
    level_four = lifting(gathered, 1)
    level_five = lifting(level_four[:, ::2], 1)
    coarse_bands = level_four.at[:, ::2].set(level_five)
    width = TILE_ROWS * merged.shape[3]
    tile_rows = merged.reshape(-1, width)
    count = tile_rows.shape[0]
    groups = lax.axis_size("gx") * lax.axis_size("gy")
    capacity = max(2, 7 * count // (5 * groups) + 1)
    writers = tile_writer.reshape(count)
    onehot = (writers[:, None] == jnp.arange(groups, dtype=jnp.int32)[None, :]).astype(jnp.int32)
    slots = jnp.sum((jnp.cumsum(onehot, axis=0) - onehot) * onehot, axis=1)
    targets = writers * capacity + slots
    outbox = jnp.zeros((groups * capacity, width), jnp.float32).at[targets].set(tile_rows)
    inbox = lax.all_to_all(outbox, ("gx", "gy"), split_axis=0, concat_axis=0, tiled=True)
    return (coarse_bands, inbox)


def solution(mesh):
    return jax.shard_map(
        body,
        mesh=mesh,
        in_specs=(P(None, "gz", "gx", "gy"), P("gx", "gy", "gz", None)),
        out_specs=(P(None, None, "gx", "gy"), P(("gx", "gy"), "gz")),
        check_vma=False,
    )
```

profile of v0, /device:TPU:2, one launch (start us, length us, event | category | flops | bytes accessed | tf_op | source)
XLA Modules:
  0.0 241.7 jit_solution(2018079191838892674)
XLA Ops:
  0.7 1.2 fusion.133
  1.9 3.6 %collective-permute-start = (f32[5,16,4,128]{3,2,1,0:T(4,128)S(1)}, f32[5,16,4,128]{3,2,1,0:T(4,128)S(1)}, u32[]{:S(2)}, u32[]{:S(2)}) collective-permute-start(f32[5,16,4,128]{3,2,1,0:T(4,128)S(1)} %get-tuple-element.28), channel_id=1, source_target_pairs={{0,128},{128,256},{256,384},{384,512},{512,640},{640,768},{768,896... | collective-permute-start | bytes 491528 | tf_op jit(solution)/shard_map/ppermute | solution.py:23
  5.5 4.5 %collective-permute-start.1 = (f32[5,16,4,128]{3,2,1,0:T(4,128)S(1)}, f32[5,16,4,128]{3,2,1,0:T(4,128)S(1)}, u32[]{:S(2)}, u32[]{:S(2)}) collective-permute-start(f32[5,16,4,128]{3,2,1,0:T(4,128)S(1)} %get-tuple-element.29), channel_id=1, source_target_pairs={{128,0},{256,128},{384,256},{512,384},{640,512},{768,640},{896,768... | collective-permute-start | bytes 491528 | tf_op jit(solution)/shard_map/ppermute | solution.py:26
  10.0 1.3 slice.452
  11.3 1.3 slice.453
  14.0 0.6 broadcast_multiply_fusion.2
  14.6 0.6 multiply_bitcast_fusion.3
  15.3 0.6 multiply_bitcast_fusion.4
  16.1 0.6 fusion.97
  16.7 0.6 fusion.119
  17.3 0.6 fusion.109
  18.1 0.7 or_select_fusion
  19.0 0.7 fusion.33
  20.1 0.6 copy.51
  20.7 3.4 %collective-permute-start.2 = (f32[5,16,24,4]{2,1,3,0:T(8,128)S(1)}, f32[5,16,24,4]{2,1,3,0:T(8,128)S(1)}, u32[]{:S(2)}, u32[]{:S(2)}) collective-permute-start(f32[5,16,24,4]{2,1,3,0:T(8,128)S(1)} %copy.51), channel_id=1, source_target_pairs={{0,16},{16,32},{32,48},{48,64},{64,80},{80,96},{96,112},{112,0},{1... | collective-permute-start | bytes 92168 | tf_op jit(solution)/shard_map/ppermute | solution.py:23
  24.1 0.6 copy.52
  24.7 12.6 %collective-permute-start.3 = (f32[5,16,24,4]{2,1,3,0:T(8,128)S(1)}, f32[5,16,24,4]{2,1,3,0:T(8,128)S(1)}, u32[]{:S(2)}, u32[]{:S(2)}) collective-permute-start(f32[5,16,24,4]{2,1,3,0:T(8,128)S(1)} %copy.52), channel_id=1, source_target_pairs={{16,0},{32,16},{48,32},{64,48},{80,64},{96,80},{112,96},{0,112},{1... | collective-permute-start | bytes 92168 | tf_op jit(solution)/shard_map/ppermute | solution.py:26
  37.3 1.3 select_reduce_fusion
  38.6 0.7 copy.50
  39.3 0.7 stack.88
  40.0 0.5 copy.53
  40.6 0.5 copy.54
  41.1 1.6 pad_maximum_fusion.6
  42.7 4.5 %collective-permute-start.5 = (f32[5,4,24,136]{3,2,1,0:T(8,128)}, f32[5,4,24,136]{3,2,1,0:T(8,128)}, u32[]{:S(2)}, u32[]{:S(2)}) collective-permute-start(f32[5,4,24,136]{3,2,1,0:T(8,128)} %get-tuple-element.25), channel_id=1, source_target_pairs={{1,0},{2,1},{3,2},{4,3},{5,4},{6,5},{7,6},{8,7},{9,8},{10,9},{11,1... | collective-permute-start | bytes 783368 | tf_op jit(solution)/shard_map/ppermute | solution.py:26
  47.5 6.5 %collective-permute-done.4 = f32[5,4,24,136]{3,2,1,0:T(8,128)} collective-permute-done((f32[5,4,24,136]{3,2,1,0:T(8,128)}, f32[5,4,24,136]{3,2,1,0:T(8,128)}, u32[]{:S(2)}, u32[]{:S(2)}) %collective-permute-start.4) | collective-permute-done | bytes 261152 | tf_op jit(solution)/shard_map/ppermute | solution.py:23
  54.0 4.1 %fusion = f32[5,24,24,128]{3,2,1,0:T(8,128)S(1)} fusion(f32[5,4,24,136]{3,2,1,0:T(8,128)} %collective-permute-done.5, f32[5,16,24,4]{3,2,1,0:T(8,128)S(1)} %copy.54, f32[5,16,4,128]{3,2,1,0:T(4,128)S(1)} %collective-permute-done.1, f32[5,16,16,128]{3,2,1,0:T(8,128)S(1)} %copy-done, f32[5,16,4,128]{3,2,1,0:T(4,128)S(1)} %collective-permute-done, ...), kind=kOutput, calls=%fused_computation.4 | convolution fusion | flops 603970560 | bytes 5076992 | tf_op jit(solution)/shard_map/fzxy,yk->fzxk/dot_general | solution.py:56
  58.2 1.0 convolution_bitcast_fusion
  59.1 0.9 fusion.14
  60.1 5.9 %slice.463 = f32[5,8,8,64]{3,1,2,0:T(8,128)S(1)} slice(f32[5,16,16,128]{3,1,2,0:T(8,128)S(1)} %bitcast.136), slice={[0:5:1], [0:16:2], [0:16:2], [0:128:2]} | slice | bytes 163840 | tf_op jit(solution)/shard_map/slice | solution.py:75
  66.0 1.9 collective-permute-start.6
  68.0 5.1 %collective-permute-start.7 = (f32[5,8,4,64]{3,1,2,0:T(8,128)S(1)}, f32[5,8,4,64]{3,1,2,0:T(8,128)S(1)}, u32[]{:S(2)}, u32[]{:S(2)}) collective-permute-start(f32[5,8,4,64]{3,1,2,0:T(8,128)S(1)} %get-tuple-element.35), channel_id=1, source_target_pairs={{128,0},{256,128},{384,256},{512,384},{640,512},{768,640},{896,768... | collective-permute-start | bytes 122888 | tf_op jit(solution)/shard_map/ppermute | solution.py:26
  73.1 0.4 collective-permute-done.6
  73.6 1.6 collective-permute-done.7
  75.3 4.9 %collective-permute-start.8 = (f32[5,8,16,4]{3,1,2,0:T(8,128)S(1)}, f32[5,8,16,4]{3,1,2,0:T(8,128)S(1)}, u32[]{:S(2)}, u32[]{:S(2)}) collective-permute-start(f32[5,8,16,4]{3,1,2,0:T(8,128)S(1)} %get-tuple-element.32), channel_id=1, source_target_pairs={{0,16},{16,32},{32,48},{48,64},{64,80},{80,96},{96,112},{112,0},{1... | collective-permute-start | bytes 30728 | tf_op jit(solution)/shard_map/ppermute | solution.py:23
  80.3 2.1 collective-permute-start.9
  82.5 2.3 collective-permute-done.8
  84.9 4.7 %collective-permute-done.9 = f32[5,8,16,4]{3,1,2,0:T(8,128)S(1)} collective-permute-done((f32[5,8,16,4]{3,1,2,0:T(8,128)S(1)}, f32[5,8,16,4]{3,1,2,0:T(8,128)S(1)}, u32[]{:S(2)}, u32[]{:S(2)}) %collective-permute-start.9) | collective-permute-done | bytes 10272 | tf_op jit(solution)/shard_map/ppermute | solution.py:26
  90.0 2.9 %collective-permute-start.11 = (f32[5,4,16,72]{3,1,2,0:T(4,128)S(1)}, f32[5,4,16,72]{3,1,2,0:T(4,128)S(1)}, u32[]{:S(2)}, u32[]{:S(2)}) collective-permute-start(f32[5,4,16,72]{3,1,2,0:T(4,128)S(1)} %get-tuple-element.31), channel_id=1, source_target_pairs={{1,0},{2,1},{3,2},{4,3},{5,4},{6,5},{7,6},{8,7},{9,8},{10,9},{11,1... | collective-permute-start | bytes 276488 | tf_op jit(solution)/shard_map/ppermute | solution.py:26
  93.0 2.9 %collective-permute-done.10 = f32[5,4,16,72]{3,1,2,0:T(4,128)S(1)} collective-permute-done((f32[5,4,16,72]{3,1,2,0:T(4,128)S(1)}, f32[5,4,16,72]{3,1,2,0:T(4,128)S(1)}, u32[]{:S(2)}, u32[]{:S(2)}) %collective-permute-start.10) | collective-permute-done | bytes 92192 | tf_op jit(solution)/shard_map/ppermute | solution.py:23
  96.3 0.8 fusion.19
  97.9 2.3 slice.481
  100.2 2.7 %collective-permute-start.12 = (f32[5,4,4,32]{3,1,2,0:T(4,128)S(1)}, f32[5,4,4,32]{3,1,2,0:T(4,128)S(1)}, u32[]{:S(2)}, u32[]{:S(2)}) collective-permute-start(f32[5,4,4,32]{3,1,2,0:T(4,128)S(1)} %slice.481), channel_id=1, source_target_pairs={{0,128},{128,256},{256,384},{384,512},{512,640},{640,768},{768,896... | collective-permute-start | bytes 30728 | tf_op jit(solution)/shard_map/ppermute | solution.py:23
  103.0 4.7 %collective-permute-start.13 = (f32[5,4,4,32]{3,1,2,0:T(4,128)S(1)}, f32[5,4,4,32]{3,1,2,0:T(4,128)S(1)}, u32[]{:S(2)}, u32[]{:S(2)}) collective-permute-start(f32[5,4,4,32]{3,1,2,0:T(4,128)S(1)} %slice.481), channel_id=1, source_target_pairs={{128,0},{256,128},{384,256},{512,384},{640,512},{768,640},{896,768... | collective-permute-start | bytes 30728 | tf_op jit(solution)/shard_map/ppermute | solution.py:26
  107.7 2.1 collective-permute-done.13
  110.0 3.9 %collective-permute-start.14 = (f32[5,4,12,4]{3,1,2,0:T(4,128)S(1)}, f32[5,4,12,4]{3,1,2,0:T(4,128)S(1)}, u32[]{:S(2)}, u32[]{:S(2)}) collective-permute-start(f32[5,4,12,4]{3,1,2,0:T(4,128)S(1)} %get-tuple-element.36), channel_id=1, source_target_pairs={{0,16},{16,32},{32,48},{48,64},{64,80},{80,96},{96,112},{112,0},{1... | collective-permute-start | bytes 11528 | tf_op jit(solution)/shard_map/ppermute | solution.py:23
  113.9 1.9 collective-permute-start.15
  115.9 0.9 collective-permute-done.14
  116.7 4.0 %collective-permute-done.15 = f32[5,4,12,4]{3,1,2,0:T(4,128)S(1)} collective-permute-done((f32[5,4,12,4]{3,1,2,0:T(4,128)S(1)}, f32[5,4,12,4]{3,1,2,0:T(4,128)S(1)}, u32[]{:S(2)}, u32[]{:S(2)}) %collective-permute-start.15) | collective-permute-done | bytes 3872 | tf_op jit(solution)/shard_map/ppermute | solution.py:26
  121.0 2.9 %collective-permute-start.17 = (f32[5,4,12,40]{3,1,2,0:T(4,128)S(1)}, f32[5,4,12,40]{3,1,2,0:T(4,128)S(1)}, u32[]{:S(2)}, u32[]{:S(2)}) collective-permute-start(f32[5,4,12,40]{3,1,2,0:T(4,128)S(1)} %pad_maximum_fusion.13), channel_id=1, source_target_pairs={{1,0},{2,1},{3,2},{4,3},{5,4},{6,5},{7,6},{8,7},{9,8},{10,9},{11,1... | collective-permute-start | bytes 115208 | tf_op jit(solution)/shard_map/ppermute | solution.py:26
  124.1 8.6 %copy.82 = f32[16,16,128,5]{3,2,1,0:T(8,128)} copy(f32[16,16,128,5]{2,0,1,3:T(8,128)S(1)} %bitcast.137) | data formatting | bytes 1310720
  132.8 0.7 copy.71
  133.9 0.6 fusion.22
  135.2 31.2 %scatter_fusion.1 = f32[5,8,8,64]{0,3,2,1:T(8,128)S(1)} fusion(f32[5,8,8,64]{0,3,2,1:T(8,128)S(1)} %copy.71, s32[512]{0:T(512)S(1)} %reshape.94, f32[512,5]{1,0:T(8,128)S(1)} %bitcast.148), kind=kCustom, calls=%fused_computation.1 | custom fusion | bytes 36864 | tf_op jit(solution)/shard_map/scatter | solution.py:78
  166.4 22.0 %scatter_fusion.2 = f32[32768,5]{1,0:T(8,128)} fusion(f32[32768,5]{1,0:T(8,128)} %bitcast.134, s32[4096]{0:T(1024)S(1)} %reshape.108, f32[4096,5]{1,0:T(8,128)S(1)} %bitcast.138), kind=kCustom, calls=%fused_computation.3 | custom fusion | bytes 262144
  188.5 10.0 %copy.74 = f32[16,16,128,5]{2,1,0,3:T(8,128)S(1)} copy(f32[16,16,128,5]{3,2,1,0:T(8,128)} %bitcast.135) | data formatting | bytes 1310720
  198.5 1.5 scatter_custom_fusion.2
  200.0 1.6 all_to_all.8
  201.6 10.7 %all-to-all-start = ((f32[64,2,2048]{2,1,0:T(2,128)}), f32[64,2,2048]{2,1,0:T(2,128)S(1)}, u32[]{:S(2)}, u32[]{:S(2)}) async-start(f32[64,2,2048]{2,1,0:T(2,128)} %all_to_all.8), calls=%async_computation | async-start | bytes 2097152 | tf_op jit(solution)/shard_map/all_to_all | solution.py:93
  212.3 1.1 slice.495
  213.4 16.8 %all_gather.3 = f32[5,32,2,16]{3,2,0,1:T(2,128)S(1)} all-gather(f32[5,2,2,16]{3,2,0,1:T(2,128)S(1)} %copy.64), channel_id=1, replica_groups=mesh['gx'=8,'gy'=8,'gz'=16] {'gz'}, dimensions={1}, use_global_device_ids=true | all-gather | bytes 21760 | tf_op jit(solution)/shard_map/all_gather | solution.py:79
  231.9 1.4 scatter_fusion
  233.3 0.7 copy.75
  234.1 5.9 %all-to-all-done = f32[64,2,2048]{2,1,0:T(2,128)S(1)} async-done(((f32[64,2,2048]{2,1,0:T(2,128)}), f32[64,2,2048]{2,1,0:T(2,128)S(1)}, u32[]{:S(2)}, u32[]{:S(2)}) %all-to-all-start) | async-done | bytes 1048608 | tf_op jit(solution)/shard_map/all_to_all | solution.py:93
  240.0 1.7 all_to_all.10
  (186 shorter events, 7.4 us)
Async XLA Ops:
  0.6 17.4 %copy-start.10 = (s32[3]{0:T(128)S(1)}, s32[3]{0:T(128)}, u32[]{:S(2)}) copy-start(s32[3]{0:T(128)} %constant.4) | copy-start | bytes 40
  0.6 18.3 %copy-start.9 = (s32[3]{0:T(128)S(1)}, s32[3]{0:T(128)}, u32[]{:S(2)}) copy-start(s32[3]{0:T(128)} %constant.7) | copy-start | bytes 40
  0.7 19.0 %copy-start = (f32[5,16,16,128]{3,2,1,0:T(8,128)S(1)}, f32[5,16,16,128]{3,2,1,0:T(8,128)}, u32[]{:S(2)}) copy-start(f32[5,16,16,128]{3,2,1,0:T(8,128)} %param.2) | copy-start | bytes 1966084
  0.7 15.2 %copy-start.7 = (s32[1,1,80,1]{2,3,1,0:T(1,128)S(1)}, s32[1,1,80,1]{2,3,1,0:T(1,128)}, u32[]{:S(2)}) copy-start(s32[1,1,80,1]{2,3,1,0:T(1,128)} %param.3) | copy-start | bytes 964
  1.9 17.8 %collective-permute-start = (f32[5,16,4,128]{3,2,1,0:T(4,128)S(1)}, f32[5,16,4,128]{3,2,1,0:T(4,128)S(1)}, u32[]{:S(2)}, u32[]{:S(2)}) collective-permute-start(f32[5,16,4,128]{3,2,1,0:T(4,128)S(1)} %get-tuple-element.28), channel_id=1, source_target_pairs={{0,128},{128,256},{256,384},{384,512},{512,640},{640,768},{768,896... | collective-permute-start | bytes 491528 | tf_op jit(solution)/shard_map/ppermute | solution.py:23
  5.5 14.2 %collective-permute-start.1 = (f32[5,16,4,128]{3,2,1,0:T(4,128)S(1)}, f32[5,16,4,128]{3,2,1,0:T(4,128)S(1)}, u32[]{:S(2)}, u32[]{:S(2)}) collective-permute-start(f32[5,16,4,128]{3,2,1,0:T(4,128)S(1)} %get-tuple-element.29), channel_id=1, source_target_pairs={{128,0},{256,128},{384,256},{512,384},{640,512},{768,640},{896,768... | collective-permute-start | bytes 491528 | tf_op jit(solution)/shard_map/ppermute | solution.py:26
  20.7 19.3 %collective-permute-start.2 = (f32[5,16,24,4]{2,1,3,0:T(8,128)S(1)}, f32[5,16,24,4]{2,1,3,0:T(8,128)S(1)}, u32[]{:S(2)}, u32[]{:S(2)}) collective-permute-start(f32[5,16,24,4]{2,1,3,0:T(8,128)S(1)} %copy.51), channel_id=1, source_target_pairs={{0,16},{16,32},{32,48},{48,64},{64,80},{80,96},{96,112},{112,0},{1... | collective-permute-start | bytes 92168 | tf_op jit(solution)/shard_map/ppermute | solution.py:23
  24.7 15.9 %collective-permute-start.3 = (f32[5,16,24,4]{2,1,3,0:T(8,128)S(1)}, f32[5,16,24,4]{2,1,3,0:T(8,128)S(1)}, u32[]{:S(2)}, u32[]{:S(2)}) collective-permute-start(f32[5,16,24,4]{2,1,3,0:T(8,128)S(1)} %copy.52), channel_id=1, source_target_pairs={{16,0},{32,16},{48,32},{64,48},{80,64},{96,80},{112,96},{0,112},{1... | collective-permute-start | bytes 92168 | tf_op jit(solution)/shard_map/ppermute | solution.py:26
  40.6 6.9 %copy-start.2 = (pred[8,8,64]{2,1,0:T(8,128)(4,1)S(1)}, pred[8,8,64]{2,1,0:T(8,128)(4,1)}, u32[]{:S(2)}) copy-start(pred[8,8,64]{2,1,0:T(8,128)(4,1)} %fusion.33) | copy-start | bytes 12292
  42.7 11.3 %collective-permute-start.4 = (f32[5,4,24,136]{3,2,1,0:T(8,128)}, f32[5,4,24,136]{3,2,1,0:T(8,128)}, u32[]{:S(2)}, u32[]{:S(2)}) collective-permute-start(f32[5,4,24,136]{3,2,1,0:T(8,128)} %get-tuple-element.24), channel_id=1, source_target_pairs={{0,1},{1,2},{2,3},{3,4},{4,5},{5,6},{6,7},{7,8},{8,9},{9,10},{10,1... | collective-permute-start | bytes 783368 | tf_op jit(solution)/shard_map/ppermute | solution.py:23
  42.7 11.3 %collective-permute-start.5 = (f32[5,4,24,136]{3,2,1,0:T(8,128)}, f32[5,4,24,136]{3,2,1,0:T(8,128)}, u32[]{:S(2)}, u32[]{:S(2)}) collective-permute-start(f32[5,4,24,136]{3,2,1,0:T(8,128)} %get-tuple-element.25), channel_id=1, source_target_pairs={{1,0},{2,1},{3,2},{4,3},{5,4},{6,5},{7,6},{8,7},{9,8},{10,9},{11,1... | collective-permute-start | bytes 783368 | tf_op jit(solution)/shard_map/ppermute | solution.py:26
  58.1 15.0 %copy-start.8 = (s32[1,1,80,1]{2,3,1,0:T(1,128)S(1)}, s32[1,1,80,1]{2,3,1,0:T(1,128)}, u32[]{:S(2)}) copy-start(s32[1,1,80,1]{2,3,1,0:T(1,128)} %param.3) | copy-start | bytes 964
  58.1 15.0 %copy-start.11 = (s32[80]{0:T(128)S(1)}, s32[80]{0:T(128)}, u32[]{:S(2)}) copy-start(s32[80]{0:T(128)} %select_reduce_fusion) | copy-start | bytes 964
  58.1 24.3 %copy-start.5 = (f32[16,8,1]{0,1,2:T(8,128)S(1)}, f32[16,8,1]{0,1,2:T(8,128)}, u32[]{:S(2)}) copy-start(f32[16,8,1]{0,1,2:T(8,128)} %get-tuple-element.16) | copy-start | bytes 1540
  58.2 24.3 %copy-start.6 = (f32[16,8,1]{0,1,2:T(8,128)S(1)}, f32[16,8,1]{0,1,2:T(8,128)}, u32[]{:S(2)}) copy-start(f32[16,8,1]{0,1,2:T(8,128)} %fusion.119) | copy-start | bytes 1540
  66.0 7.5 %collective-permute-start.6 = (f32[5,8,4,64]{3,1,2,0:T(8,128)S(1)}, f32[5,8,4,64]{3,1,2,0:T(8,128)S(1)}, u32[]{:S(2)}, u32[]{:S(2)}) collective-permute-start(f32[5,8,4,64]{3,1,2,0:T(8,128)S(1)} %get-tuple-element.34), channel_id=1, source_target_pairs={{0,128},{128,256},{256,384},{384,512},{512,640},{640,768},{768,896... | collective-permute-start | bytes 122888 | tf_op jit(solution)/shard_map/ppermute | solution.py:23
  68.0 7.2 %collective-permute-start.7 = (f32[5,8,4,64]{3,1,2,0:T(8,128)S(1)}, f32[5,8,4,64]{3,1,2,0:T(8,128)S(1)}, u32[]{:S(2)}, u32[]{:S(2)}) collective-permute-start(f32[5,8,4,64]{3,1,2,0:T(8,128)S(1)} %get-tuple-element.35), channel_id=1, source_target_pairs={{128,0},{256,128},{384,256},{512,384},{640,512},{768,640},{896,768... | collective-permute-start | bytes 122888 | tf_op jit(solution)/shard_map/ppermute | solution.py:26
  75.3 9.5 %collective-permute-start.8 = (f32[5,8,16,4]{3,1,2,0:T(8,128)S(1)}, f32[5,8,16,4]{3,1,2,0:T(8,128)S(1)}, u32[]{:S(2)}, u32[]{:S(2)}) collective-permute-start(f32[5,8,16,4]{3,1,2,0:T(8,128)S(1)} %get-tuple-element.32), channel_id=1, source_target_pairs={{0,16},{16,32},{32,48},{48,64},{64,80},{80,96},{96,112},{112,0},{1... | collective-permute-start | bytes 30728 | tf_op jit(solution)/shard_map/ppermute | solution.py:23
  80.3 9.3 %collective-permute-start.9 = (f32[5,8,16,4]{3,1,2,0:T(8,128)S(1)}, f32[5,8,16,4]{3,1,2,0:T(8,128)S(1)}, u32[]{:S(2)}, u32[]{:S(2)}) collective-permute-start(f32[5,8,16,4]{3,1,2,0:T(8,128)S(1)} %get-tuple-element.33), channel_id=1, source_target_pairs={{16,0},{32,16},{48,32},{64,48},{80,64},{96,80},{112,96},{0,112},{1... | collective-permute-start | bytes 30728 | tf_op jit(solution)/shard_map/ppermute | solution.py:26
  89.9 25.9 %copy-start.3 = (f32[12,6,1]{0,1,2:T(8,128)S(1)}, f32[12,6,1]{0,1,2:T(8,128)}, u32[]{:S(2)}) copy-start(f32[12,6,1]{0,1,2:T(8,128)} %get-tuple-element.12) | copy-start | bytes 868
  89.9 25.9 %copy-start.4 = (f32[12,6,1]{0,1,2:T(8,128)S(1)}, f32[12,6,1]{0,1,2:T(8,128)}, u32[]{:S(2)}) copy-start(f32[12,6,1]{0,1,2:T(8,128)} %fusion.109) | copy-start | bytes 868
  89.9 6.0 %collective-permute-start.10 = (f32[5,4,16,72]{3,1,2,0:T(4,128)S(1)}, f32[5,4,16,72]{3,1,2,0:T(4,128)S(1)}, u32[]{:S(2)}, u32[]{:S(2)}) collective-permute-start(f32[5,4,16,72]{3,1,2,0:T(4,128)S(1)} %get-tuple-element.30), channel_id=1, source_target_pairs={{0,1},{1,2},{2,3},{3,4},{4,5},{5,6},{6,7},{7,8},{8,9},{9,10},{10,1... | collective-permute-start | bytes 276488 | tf_op jit(solution)/shard_map/ppermute | solution.py:23
  90.0 5.9 %collective-permute-start.11 = (f32[5,4,16,72]{3,1,2,0:T(4,128)S(1)}, f32[5,4,16,72]{3,1,2,0:T(4,128)S(1)}, u32[]{:S(2)}, u32[]{:S(2)}) collective-permute-start(f32[5,4,16,72]{3,1,2,0:T(4,128)S(1)} %get-tuple-element.31), channel_id=1, source_target_pairs={{1,0},{2,1},{3,2},{4,3},{5,4},{6,5},{7,6},{8,7},{9,8},{10,9},{11,1... | collective-permute-start | bytes 276488 | tf_op jit(solution)/shard_map/ppermute | solution.py:26
  92.9 31.0 %copy-start.1 = (s32[4,4,32,1]{2,1,0,3:T(4,128)S(1)}, s32[4,4,32,1]{2,1,0,3:T(4,128)}, u32[]{:S(2)}) copy-start(s32[4,4,32,1]{2,1,0,3:T(4,128)} %or_select_fusion) | copy-start | bytes 6148
  100.2 7.5 %collective-permute-start.12 = (f32[5,4,4,32]{3,1,2,0:T(4,128)S(1)}, f32[5,4,4,32]{3,1,2,0:T(4,128)S(1)}, u32[]{:S(2)}, u32[]{:S(2)}) collective-permute-start(f32[5,4,4,32]{3,1,2,0:T(4,128)S(1)} %slice.481), channel_id=1, source_target_pairs={{0,128},{128,256},{256,384},{384,512},{512,640},{640,768},{768,896... | collective-permute-start | bytes 30728 | tf_op jit(solution)/shard_map/ppermute | solution.py:23
  103.0 6.8 %collective-permute-start.13 = (f32[5,4,4,32]{3,1,2,0:T(4,128)S(1)}, f32[5,4,4,32]{3,1,2,0:T(4,128)S(1)}, u32[]{:S(2)}, u32[]{:S(2)}) collective-permute-start(f32[5,4,4,32]{3,1,2,0:T(4,128)S(1)} %slice.481), channel_id=1, source_target_pairs={{128,0},{256,128},{384,256},{512,384},{640,512},{768,640},{896,768... | collective-permute-start | bytes 30728 | tf_op jit(solution)/shard_map/ppermute | solution.py:26
  110.0 6.8 %collective-permute-start.14 = (f32[5,4,12,4]{3,1,2,0:T(4,128)S(1)}, f32[5,4,12,4]{3,1,2,0:T(4,128)S(1)}, u32[]{:S(2)}, u32[]{:S(2)}) collective-permute-start(f32[5,4,12,4]{3,1,2,0:T(4,128)S(1)} %get-tuple-element.36), channel_id=1, source_target_pairs={{0,16},{16,32},{32,48},{48,64},{64,80},{80,96},{96,112},{112,0},{1... | collective-permute-start | bytes 11528 | tf_op jit(solution)/shard_map/ppermute | solution.py:23
  113.9 6.9 %collective-permute-start.15 = (f32[5,4,12,4]{3,1,2,0:T(4,128)S(1)}, f32[5,4,12,4]{3,1,2,0:T(4,128)S(1)}, u32[]{:S(2)}, u32[]{:S(2)}) collective-permute-start(f32[5,4,12,4]{3,1,2,0:T(4,128)S(1)} %get-tuple-element.37), channel_id=1, source_target_pairs={{16,0},{32,16},{48,32},{64,48},{80,64},{96,80},{112,96},{0,112},{1... | collective-permute-start | bytes 11528 | tf_op jit(solution)/shard_map/ppermute | solution.py:26
  121.0 12.5 %collective-permute-start.16 = (f32[5,4,12,40]{3,1,2,0:T(4,128)S(1)}, f32[5,4,12,40]{3,1,2,0:T(4,128)S(1)}, u32[]{:S(2)}, u32[]{:S(2)}) collective-permute-start(f32[5,4,12,40]{3,1,2,0:T(4,128)S(1)} %pad_maximum_fusion.13), channel_id=1, source_target_pairs={{0,1},{1,2},{2,3},{3,4},{4,5},{5,6},{6,7},{7,8},{8,9},{9,10},{10,1... | collective-permute-start | bytes 115208 | tf_op jit(solution)/shard_map/ppermute | solution.py:23
  121.0 12.5 %collective-permute-start.17 = (f32[5,4,12,40]{3,1,2,0:T(4,128)S(1)}, f32[5,4,12,40]{3,1,2,0:T(4,128)S(1)}, u32[]{:S(2)}, u32[]{:S(2)}) collective-permute-start(f32[5,4,12,40]{3,1,2,0:T(4,128)S(1)} %pad_maximum_fusion.13), channel_id=1, source_target_pairs={{1,0},{2,1},{3,2},{4,3},{5,4},{6,5},{7,6},{8,7},{9,8},{10,9},{11,1... | collective-permute-start | bytes 115208 | tf_op jit(solution)/shard_map/ppermute | solution.py:26
  201.6 38.4 %all-to-all-start = ((f32[64,2,2048]{2,1,0:T(2,128)}), f32[64,2,2048]{2,1,0:T(2,128)S(1)}, u32[]{:S(2)}, u32[]{:S(2)}) async-start(f32[64,2,2048]{2,1,0:T(2,128)} %all_to_all.8), calls=%async_computation | async-start | bytes 2097152 | tf_op jit(solution)/shard_map/all_to_all | solution.py:93
where the time goes:
time: 242 us
  local copies, waits for them, and re-layouts  99.2 us (41%)
  starting transfers between devices  72.6 us (30%)
  waiting for transfers between devices  31.5 us (13%)
  blocking collectives  16.8 us (7%)
  other arithmetic  11 us (5%)
  matrix products  8.71 us (4%)
    unnamed x29, local copies, waits for them, and re-layouts  41.6 us
    ppermute x9, starting transfers between devices, with_halo(): lax.ppermute(lax.slice_in_dim(block, 0, width, axis=dim), axis, backward)  41.3 us
    scatter x1, local copies, waits for them, and re-layouts, body(): merged = results[depth].at[:, ::2, ::2, ::2].set(merged)  31.2 us
    ppermute x9, starting transfers between devices, with_halo(): lax.ppermute(lax.slice_in_dim(block, block.shape[dim] - width, None, axis...  20.6 us
    all_gather x1, blocking collectives, body(): gathered = lax.all_gather(current, 'gz', axis=1, tiled=True)  16.8 us
    ppermute x9, waiting for transfers between devices, with_halo(): lax.ppermute(lax.slice_in_dim(block, block.shape[dim] - width, None, axis...  13.1 us
    ppermute x9, waiting for transfers between devices, with_halo(): lax.ppermute(lax.slice_in_dim(block, 0, width, axis=dim), axis, backward)  12.4 us
    all_to_all x1, starting transfers between devices, body(): lax.all_to_all(outbox, ('gx', 'gy'), split_axis=0, concat_axis=0, tiled=T...  10.7 us
  transfers between devices with their start and end apart: 19, of which 10 were waited for; matrix products, arithmetic and copies ran while one was open for 11% of the time, Pallas kernels for 0%

commit v1 on v0

v1 whole, which is shorter than its diff:
```python
import jax
import jax.numpy as jnp
import ml_dtypes
import numpy as np
from jax import lax
from jax.experimental import pallas as pl
from jax.experimental.pallas import tpu as pltpu
from jax.sharding import PartitionSpec as P

PREDICT_ONE = -1.586134342059924
UPDATE_ONE = -0.052980118572961
PREDICT_TWO = 0.882911075530934
UPDATE_TWO = 0.443506852043971
LOW_SCALE = 1.0 / 1.149604398860241
HIGH_SCALE = 1.149604398860241

F = 5
NB = 16
LN = 128
ROWS = F * NB * NB
TILES = F * NB

LOW_SIDE = (4, 6, 6)
HIGH_SIDE = (3, 5, 7)


def lift_np(values):
    low = values[0::2].copy()
    high = values[1::2].copy()
    high += PREDICT_ONE * (low + np.roll(low, -1, 0))
    low += UPDATE_ONE * (np.roll(high, 1, 0) + high)
    high += PREDICT_TWO * (low + np.roll(low, -1, 0))
    low += UPDATE_TWO * (np.roll(high, 1, 0) + high)
    joined = np.empty_like(values)
    joined[0::2] = low * LOW_SCALE
    joined[1::2] = high * HIGH_SCALE
    return joined


def split(matrix):
    matrix = np.asarray(matrix, np.float32)
    upper = matrix.astype(ml_dtypes.bfloat16)
    lower = (matrix - upper.astype(np.float32)).astype(ml_dtypes.bfloat16)
    return upper, lower


def y_matrices():
    total, start = 8 * LN, 4 * LN
    level = np.eye(total)
    maps = []
    for _ in range(3):
        level = lift_np(level)
        maps.append(level)
        level = level[0::2]
    own = np.zeros((LN, 2 * LN))
    send = np.zeros((32, LN))
    place = np.zeros((32, 2 * LN))
    columns = [lambda j: j, lambda j: LN + 2 * j, lambda j: LN + 4 * j + 1]
    at_low, at_high = 0, 16
    for depth in range(3):
        count = LN >> depth
        first = start >> depth
        block = maps[depth][:, start : start + LN]
        low, high = LOW_SIDE[depth], HIGH_SIDE[depth]
        assert not block[: first - low].any() and not block[first + count + high :].any()
        for j in range(count):
            own[:, columns[depth](j)] = block[first + j]
        for j in range(low):
            send[at_low] = block[first - low + j]
            place[at_low, columns[depth](count - low + j)] = 1
            at_low += 1
        for j in range(high):
            send[at_high] = block[first + count + j]
            place[at_high, columns[depth](j)] = 1
            at_high += 1
    return send, own, place


def lift(values):
    low = {i // 2: v for i, v in values.items() if i % 2 == 0}
    high = {i // 2: v for i, v in values.items() if i % 2 != 0}

    def add(target, source, factor, offsets):
        span = range(min(source) - 1, max(source) + 2)
        result = dict(target)
        for i in span:
            terms = [source[i + o] for o in offsets if i + o in source]
            if terms:
                step = factor * (terms[0] + terms[1] if len(terms) == 2 else terms[0])
                result[i] = result[i] + step if i in result else step
        return result

    high = add(high, low, PREDICT_ONE, (0, 1))
    low = add(low, high, UPDATE_ONE, (-1, 0))
    high = add(high, low, PREDICT_TWO, (0, 1))
    low = add(low, high, UPDATE_TWO, (-1, 0))
    joined = {2 * i: v * LOW_SCALE for i, v in low.items()}
    joined.update({2 * i + 1: v * HIGH_SCALE for i, v in high.items()})
    return joined


def lows(values):
    return {i // 2: v for i, v in values.items() if i % 2 == 0}


def lane_of(shape):
    return lax.broadcasted_iota(jnp.int32, shape, len(shape) - 1)


def dot(a, b, dims):
    return lax.dot_general(a, b, (dims, ((), ())), preferred_element_type=jnp.float32)


def halves(x):
    upper = x.astype(jnp.bfloat16)
    return upper, (x - upper.astype(jnp.float32)).astype(jnp.bfloat16)


def share_y_kernel(fields, send_hi, send_lo, to_low, to_high):
    cells_hi, cells_lo = halves(fields[...])
    dims = ((1,), (1,))
    shares = dot(send_hi[...], cells_hi, dims) + dot(send_hi[...], cells_lo, dims) + dot(send_lo[...], cells_hi, dims)
    to_low[...] = shares[:16]
    to_high[...] = shares[16:]


def fine_shares(values):
    return lift(values)


def coarse_shares(values):
    second = lift(lows(lift(values)))
    third = lift(lows(second))
    return second, third


def send_rows(second, third, second_lane, third_lane, third_far, roll):
    near_low = []
    for i in range(6):
        row = second[i - 6]
        near_low.append(jnp.where(second_lane, row, third[i - 4]) if i < 4 else row)
    near_high = []
    for i in range(5):
        row = second[8 + i]
        near_high.append(jnp.where(second_lane, row, third[4 + i]) if i < 4 else row)
    far_low = jnp.where(third_lane, third[-6], roll(third[-5], 1))
    far_high = jnp.where(third_lane, third[8], jnp.where(third_far, roll(third[10], 2), roll(third[9], 1)))
    return near_low, near_high, far_low, far_high


def share_z_kernel(
    fields, own_hi, own_lo, place, from_low, from_high, fine, coarse, to_low, to_high, to_low_far, to_high_far, work
):
    cells_hi, cells_lo = halves(fields[...])
    dims = ((1,), (0,))
    low_hi, low_lo = halves(from_high[...])
    high_hi, high_lo = halves(from_low[...])
    turned = ((0,), (0,))
    work[...] = (
        dot(cells_hi, own_hi[...], dims)
        + dot(cells_lo, own_hi[...], dims)
        + dot(cells_hi, own_lo[...], dims)
        + dot(low_hi, place[:16], turned)
        + dot(low_lo, place[:16], turned)
        + dot(high_hi, place[16:], turned)
        + dot(high_lo, place[16:], turned)
    )
    shape = (8, LN)
    lane = lane_of(shape)
    second_lane = lane % 2 == 0
    third_lane = lane % 4 == 1
    third_far = lane % 4 == 3

    def roll(x, by):
        return pltpu.roll(x, by, 1)

    for f in range(F):
        for half in (0, 8):
            rows = slice(half, half + 8)
            at = [f * 256 + z * 16 + half for z in range(NB)]
            done = fine_shares({z: work[at[z] : at[z] + 8, :LN] for z in range(NB)})
            for z in range(NB):
                fine[at[z] : at[z] + 8] = done[z]
            for i in range(4):
                to_low[f, i, rows] = done[i - 4]
            for i in range(3):
                to_high[f, i, rows] = done[16 + i]
            second, third = coarse_shares({z: work[at[z] : at[z] + 8, LN:] for z in range(NB)})
            for z in range(8):
                row = jnp.where(second_lane, second[z], third[z // 2]) if z % 2 == 0 else second[z]
                coarse[f * 128 + z * 16 + half : f * 128 + z * 16 + half + 8] = row
            near_low, near_high, far_low, far_high = send_rows(second, third, second_lane, third_lane, third_far, roll)
            for i in range(6):
                to_low[f, 4 + i, rows] = near_low[i]
            for i in range(5):
                to_high[f, 3 + i, rows] = near_high[i]
            to_low_far[f, rows] = far_low
            to_high_far[f, rows] = far_high


def add_coarse(base, near_low, near_high, far_low, far_high, second_lane, third_lane, roll):
    zero = jnp.zeros_like(base[0])
    rows = list(base)
    for i in range(6):
        rows[2 + i] = rows[2 + i] + jnp.where(second_lane, near_low[i], zero)
    for i in range(5):
        rows[i] = rows[i] + jnp.where(second_lane, near_high[i], zero)
    third = [near_low[r] + near_high[r] for r in range(4)]
    third[2] = third[2] + far_low
    third[3] = third[3] + roll(far_low, LN - 1)
    third[0] = third[0] + far_high
    third[1] = third[1] + roll(far_high, LN - 1)
    third[2] = third[2] + roll(far_high, LN - 2)
    for r in range(4):
        rows[2 * r] = rows[2 * r] + jnp.where(third_lane, third[r], zero)
    return rows


def share_x_kernel(
    fine, coarse, from_high, from_low, from_high_far, from_low_far,
    own_fine, own_coarse, to_low, to_high, to_low_far, to_high_far, work, work_coarse,
):
    shape = (8, LN)
    lane = lane_of(shape)
    second_lane = lane % 2 == 0
    third_lane = lane % 4 == 1
    third_far = lane % 4 == 3

    def roll(x, by):
        return pltpu.roll(x, by, 1)

    for f in range(F):
        at = f * 256
        work[at : at + 48] = fine[at : at + 48] + from_low[f, :3].reshape(48, LN)
        work[at + 48 : at + 192] = fine[at + 48 : at + 192]
        work[at + 192 : at + 256] = fine[at + 192 : at + 256] + from_high[f, :4].reshape(64, LN)
        for half in (0, 8):
            rows = slice(half, half + 8)
            at = [f * 128 + z * 16 + half for z in range(8)]
            added = add_coarse(
                [coarse[at[z] : at[z] + 8] for z in range(8)],
                [from_high[f, 4 + i, rows] for i in range(6)],
                [from_low[f, 3 + i, rows] for i in range(5)],
                from_high_far[f, rows],
                from_low_far[f, rows],
                second_lane,
                third_lane,
                roll,
            )
            for z in range(8):
                work_coarse[at[z] : at[z] + 8] = added[z]
    for g in range(10):
        rows = slice(g * 8, g * 8 + 8)
        done = fine_shares({x: work[pl.ds(g * 128 + x, 8, stride=16), :] for x in range(NB)})
        for x in range(NB):
            own_fine[x, rows] = done[x]
        for i in range(4):
            to_low[i * 80 + g * 8 : i * 80 + g * 8 + 8] = done[i - 4]
        for i in range(3):
            to_high[i * 80 + g * 8 : i * 80 + g * 8 + 8] = done[16 + i]
    for g in range(5):
        rows = slice(g * 8, g * 8 + 8)
        second, third = coarse_shares({x: work_coarse[pl.ds(g * 128 + x, 8, stride=16), :] for x in range(NB)})
        for x in range(8):
            own_coarse[x, rows] = jnp.where(second_lane, second[x], third[x // 2]) if x % 2 == 0 else second[x]
        near_low, near_high, far_low, far_high = send_rows(second, third, second_lane, third_lane, third_far, roll)
        for i in range(6):
            to_low[320 + i * 40 + g * 8 : 320 + i * 40 + g * 8 + 8] = near_low[i]
        for i in range(5):
            to_high[240 + i * 40 + g * 8 : 240 + i * 40 + g * 8 + 8] = near_high[i]
        to_low_far[rows] = far_low
        to_high_far[rows] = far_high


def route_kernel(
    writers, fine, coarse, from_high, from_low, from_high_far, from_low_far, pick,
    outbox, low_band, tiles, spread, counts,
):
    shape = (8, LN)
    lane = lane_of(shape)
    second_lane = lane % 2 == 0
    third_lane = lane % 4 == 1
    replaced = (lane % 4 == 0) & (lax.broadcasted_iota(jnp.int32, shape, 0) % 2 == 0)

    def roll(x, by):
        return pltpu.roll(x, by, 1)

    outbox[...] = jnp.zeros_like(outbox)
    for g in range(5):
        rows = slice(g * 8, g * 8 + 8)
        added = add_coarse(
            [coarse[x, rows] for x in range(8)],
            [from_high[320 + i * 40 + g * 8 : 320 + i * 40 + g * 8 + 8] for i in range(6)],
            [from_low[240 + i * 40 + g * 8 : 240 + i * 40 + g * 8 + 8] for i in range(5)],
            from_high_far[rows],
            from_low_far[rows],
            second_lane,
            third_lane,
            roll,
        )
        for i, x in ((0, 0), (1, 4)):
            upper, lower = halves(added[x])
            rest = (added[x] - upper.astype(jnp.float32) - lower.astype(jnp.float32)).astype(jnp.bfloat16)
            dims = ((1,), (0,))
            low_band[i, rows] = dot(upper, pick[...], dims) + dot(lower, pick[...], dims) + dot(rest, pick[...], dims)
        for x in range(8):
            row = added[x]
            if x % 2 == 0:
                row = jnp.where(replaced, roll(row, LN - 1), row)
            spread[pl.ds(x * 80 + g * 16, 8, stride=2), :] = row
            spread[pl.ds(x * 80 + g * 16 + 1, 8, stride=2), :] = row
    merged = (lane % 2 == 0) & (lax.broadcasted_iota(jnp.int32, shape, 0) % 2 == 0)
    for g in range(10):
        rows = slice(g * 8, g * 8 + 8)
        for x in range(NB):
            row = fine[x, rows]
            if x < 3:
                row = row + from_low[x * 80 + g * 8 : x * 80 + g * 8 + 8]
            if x >= 12:
                i = x - 12
                row = row + from_high[i * 80 + g * 8 : i * 80 + g * 8 + 8]
            if x % 2 == 0:
                row = jnp.where(merged, spread[x // 2 * 80 + g * 8 : x // 2 * 80 + g * 8 + 8], row)
            tiles[pl.ds(g * 128 + x, 8, stride=16), :] = row

    def clear(i, carry):
        counts[i] = 0
        return carry

    lax.fori_loop(0, 64, clear, 0)

    def send(t, carry):
        writer = writers[t]
        slot = counts[writer]
        counts[writer] = slot + 1
        to = pl.multiple_of((writer * 2 + slot) * 16, 16)
        outbox[pl.ds(to, 16), :] = tiles[pl.ds(pl.multiple_of(t * 16, 16), 16), :]
        return carry

    lax.fori_loop(0, TILES, send, 0)


VM = pl.BlockSpec(memory_space=pltpu.VMEM)
SM = pl.BlockSpec(memory_space=pltpu.SMEM)


def f32(*shape):
    return jax.ShapeDtypeStruct(shape, jnp.float32)


def call(kernel, outs, ins, scratch=(), specs=None, flops=1 << 20):
    moved = sum(4 * int(np.prod(a.shape)) for a in list(outs) + list(ins))
    return pl.pallas_call(
        kernel,
        out_shape=list(outs),
        in_specs=specs or [VM] * len(ins),
        out_specs=[VM] * len(outs),
        scratch_shapes=list(scratch),
        compiler_params=pltpu.CompilerParams(vmem_limit_bytes=32 << 20),
        cost_estimate=pl.CostEstimate(flops=flops, bytes_accessed=moved, transcendentals=0),
    )(*ins)


def shift(array, axis, by):
    count = lax.axis_size(axis)
    return lax.ppermute(array, axis, [(i, (i + by) % count) for i in range(count)])


def coarse_matrix(length):
    level_four = lift_np(np.eye(length))
    level_five = lift_np(level_four[0::2])
    level_four[0::2] = level_five
    return level_four.astype(np.float32)


def body(fields, tile_writer):
    send, own, place = y_matrices()
    send_hi, send_lo = (jnp.asarray(m) for m in split(send))
    own_hi, own_lo = (jnp.asarray(m) for m in split(own))
    place = jnp.asarray(place.astype(ml_dtypes.bfloat16))
    pick = np.zeros((LN, 16), ml_dtypes.bfloat16)
    for j in range(16):
        pick[8 * j + 1, j] = 1
    cells = fields.reshape(ROWS, LN)

    to_low, to_high = call(share_y_kernel, [f32(16, ROWS)] * 2, [cells, send_hi, send_lo])
    from_high = shift(to_low, "gy", -1)
    from_low = shift(to_high, "gy", 1)

    fine, coarse, to_low, to_high, to_low_far, to_high_far = call(
        share_z_kernel,
        [f32(ROWS, LN), f32(ROWS // 2, LN), f32(F, 10, 16, LN), f32(F, 8, 16, LN), f32(F, 16, LN), f32(F, 16, LN)],
        [cells, own_hi, own_lo, place, from_low, from_high],
        [pltpu.VMEM((ROWS, 2 * LN), jnp.float32)],
    )
    from_high = shift(to_low, "gz", -1)
    from_low = shift(to_high, "gz", 1)
    from_high_far = shift(to_low_far, "gz", -2)
    from_low_far = shift(to_high_far, "gz", 2)

    fine, coarse, to_low, to_high, to_low_far, to_high_far = call(
        share_x_kernel,
        [f32(16, 80, LN), f32(8, 40, LN), f32(560, LN), f32(440, LN), f32(40, LN), f32(40, LN)],
        [fine, coarse, from_high, from_low, from_high_far, from_low_far],
        [pltpu.VMEM((ROWS, LN), jnp.float32), pltpu.VMEM((ROWS // 2, LN), jnp.float32)],
    )
    from_high = shift(to_low, "gx", -1)
    from_low = shift(to_high, "gx", 1)
    from_high_far = shift(to_low_far, "gx", -2)
    from_low_far = shift(to_high_far, "gx", 2)

    outbox, low_band = call(
        route_kernel,
        [f32(2048, LN), f32(2, 40, 16)],
        [tile_writer.reshape(TILES), fine, coarse, from_high, from_low, from_high_far, from_low_far, jnp.asarray(pick)],
        [pltpu.VMEM((ROWS, LN), jnp.float32), pltpu.VMEM((640, LN), jnp.float32), pltpu.SMEM((64,), jnp.int32)],
        [SM] + [VM] * 7,
    )
    inbox = lax.all_to_all(outbox.reshape(64, 32, LN), ("gx", "gy"), split_axis=0, concat_axis=0, tiled=True)

    band = low_band.reshape(2, F, 8, 16)[:, :, ::4].transpose(2, 1, 0, 3).reshape(2, F * 32)
    band = lax.all_gather(band, "gz", axis=0, tiled=True)
    turn = jnp.asarray(coarse_matrix(band.shape[0]))
    bands = jnp.dot(turn, band, precision=lax.Precision.HIGHEST)
    bands = bands.reshape(-1, F, 2, 16).transpose(1, 0, 2, 3)
    return (bands, inbox.reshape(128, 2048))


def solution(mesh):
    return jax.shard_map(
        body,
        mesh=mesh,
        in_specs=(P(None, "gz", "gx", "gy"), P("gx", "gy", "gz", None)),
        out_specs=(P(None, None, "gx", "gy"), P(("gx", "gy"), "gz")),
        check_vma=False,
    )
```

time: 242 us -> 106 us (0.44)
  local copies, waits for them, and re-layouts: 99.2 us -> 5.16 us
  starting transfers between devices: 72.6 us -> 52.7 us
  other arithmetic: 11 us -> 0 us
  matrix products: 8.71 us -> 0.97 us
  waiting for transfers between devices: 31.5 us -> 24.7 us
  Pallas kernels: 0 us -> 6.34 us
  blocking collectives: 16.8 us -> 14.2 us
    unnamed x29 -> x21, local copies, waits for them, and re-layouts: 41.6 us -> 3.94 us
    scatter x3 -> x0, local copies, waits for them, and re-layouts: 34.1 us -> none  [the longest x1 31.2 us: body(): merged = results[depth].at[:, ::2, ::2, ::2].set(merged)]
    ppermute x18 -> x10, starting transfers between devices: 61.8 us -> 42.3 us  [shift(): lax.ppermute(array, axis, [(i, (i + by) % count) for i in range(count)])]
    slice x76 -> x1, local copies, waits for them, and re-layouts: 16 us -> 0.09 us  [body(): low_band.reshape(2, F, 8, 16)[:, :, ::4].transpose(2, 1, 0, 3)]
    ppermute x18 -> x10, waiting for transfers between devices: 25.6 us -> 12.9 us  [shift(): lax.ppermute(array, axis, [(i, (i + by) % count) for i in range(count)])]
    dot_general x9 -> x1, matrix products: 8.71 us -> 0.97 us  [body(): bands = jnp.dot(turn, band, precision=lax.Precision.HIGHEST)]
    pallas_call x0 -> x4, Pallas kernels: none -> 6.34 us  [call(): pl.pallas_call(kernel, out_shape=list(outs), in_specs=specs or [VM] * len...]
    all_to_all x1, waiting for transfers between devices: 5.93 us -> 11.8 us  [body(): lax.all_to_all(outbox.reshape(64, 32, LN), ('gx', 'gy'), split_axis=0, co...]
  transfers between devices with their start and end apart: 19 -> 11, of which waited for: 10 -> 5; matrix products, arithmetic and copies ran while one was open for 11% -> 1% of each run, Pallas kernels for 0% -> 0%
where the time goes in v1:
time: 106 us; the launch traced here: 105 us
  starting transfers between devices  52.7 us (50%)
  waiting for transfers between devices  24.7 us (23%)
  blocking collectives  14.2 us (13%)
  Pallas kernels  6.34 us (6%)
  local copies, waits for them, and re-layouts  5.16 us (5%)
    ppermute x10, starting transfers between devices, shift(): lax.ppermute(array, axis, [(i, (i + by) % count) for i in range(count)])  42.3 us
    all_gather x1, blocking collectives, body(): band = lax.all_gather(band, 'gz', axis=0, tiled=True)  14.2 us
    ppermute x10, waiting for transfers between devices, shift(): lax.ppermute(array, axis, [(i, (i + by) % count) for i in range(count)])  12.9 us
    all_to_all x1, waiting for transfers between devices, body(): lax.all_to_all(outbox.reshape(64, 32, LN), ('gx', 'gy'), split_axis=0, co...  11.8 us
    all_to_all x1, starting transfers between devices, body(): lax.all_to_all(outbox.reshape(64, 32, LN), ('gx', 'gy'), split_axis=0, co...  10.5 us
    pallas_call x4, Pallas kernels, call(): pl.pallas_call(kernel, out_shape=list(outs), in_specs=specs or [VM] * len...  6.34 us
    unnamed x21, local copies, waits for them, and re-layouts  3.94 us
  transfers between devices with their start and end apart: 11, of which 5 were waited for; matrix products, arithmetic and copies ran while one was open for 1% of the time, Pallas kernels for 0%

profile of v1, /device:TPU:2, one launch (start us, length us, event | category | flops | bytes accessed | tf_op | source)
XLA Modules:
  0.0 104.9 jit_solution(5920882040319793378)
XLA Ops:
  0.6 0.0 copy-start.5
  0.6 0.7 copy-done.5
  1.3 0.0 copy-start
  1.3 1.1 %copy-done = f32[5,16,16,128]{3,2,1,0:T(8,128)S(1)} copy-done((f32[5,16,16,128]{3,2,1,0:T(8,128)S(1)}, f32[5,16,16,128]{3,2,1,0:T(8,128)}, u32[]{:S(2)}) %copy-start) | copy-done | bytes 655384
  2.4 0.0 copy-start.6
  2.4 0.7 copy-done.6
  3.1 0.0 copy-start.1
  3.1 0.0 copy-start.2
  3.1 0.0 copy-start.4
  3.1 0.4 shard_map.104
  3.6 3.4 %collective-permute-start = (f32[16,1280]{1,0:T(8,128)S(1)}, f32[16,1280]{1,0:T(8,128)S(1)}, u32[]{:S(2)}, u32[]{:S(2)}) collective-permute-start(f32[16,1280]{1,0:T(8,128)S(1)} %get-tuple-element.18), channel_id=1, source_target_pairs={{0,16},{16,32},{32,48},{48,64},{64,80},{80,96},{96,112},{112,0},{1... | collective-permute-start | bytes 245768 | tf_op jit(solution)/shard_map/ppermute | solution.py:366
  7.0 13.6 %collective-permute-start.1 = (f32[16,1280]{1,0:T(8,128)S(1)}, f32[16,1280]{1,0:T(8,128)S(1)}, u32[]{:S(2)}, u32[]{:S(2)}) collective-permute-start(f32[16,1280]{1,0:T(8,128)S(1)} %get-tuple-element.19), channel_id=1, source_target_pairs={{0,112},{16,0},{32,16},{48,32},{64,48},{80,64},{96,80},{112,96},{1... | collective-permute-start | bytes 245768 | tf_op jit(solution)/shard_map/ppermute | solution.py:366
  20.6 0.5 collective-permute-done.from_low
  21.1 1.6 %collective-permute-done.1.from_high = f32[16,1280]{1,0:T(8,128)S(1)} collective-permute-done((f32[16,1280]{1,0:T(8,128)S(1)}, f32[16,1280]{1,0:T(8,128)S(1)}, u32[]{:S(2)}, u32[]{:S(2)}) %collective-permute-start.1) | collective-permute-done | bytes 81952 | tf_op jit(solution)/shard_map/ppermute | solution.py:366
  22.6 0.0 copy-done.1
  22.6 0.0 copy-done.2
  22.6 0.0 copy-done.4
  22.6 1.9 %shard_map.105 = (f32[1280,128]{1,0:T(8,128)S(1)}, f32[640,128]{1,0:T(8,128)S(1)}, f32[5,10,16,128]{3,2,1,0:T(8,128)S(1)}, f32[5,8,16,128]{3,2,1,0:T(8,128)S(1)}...) custom-call(f32[1280,128]{1,0:T(8,128)S(1)} %bitcast.13, bf16[128,256]{1,0:T(8,128)(2,1)S(1)} %copy-done.2, ...), custom_call_target="tpu_custom_call" | custom-call | flops 1048576 | bytes 2916352 | tf_op jit(solution)/shard_map/pallas_call | solution.py:353
  24.6 4.1 %collective-permute-start.2 = (f32[5,10,16,128]{3,2,1,0:T(8,128)S(1)}, f32[5,10,16,128]{3,2,1,0:T(8,128)S(1)}, u32[]{:S(2)}, u32[]{:S(2)}) collective-permute-start(f32[5,10,16,128]{3,2,1,0:T(8,128)S(1)} %get-tuple-element.22), channel_id=1, source_target_pairs={{0,15},{1,0},{2,1},{3,2},{4,3},{5,4},{6,5},{7,6},{8,7},{9,8},{10,9... | collective-permute-start | bytes 1228808 | tf_op jit(solution)/shard_map/ppermute | solution.py:366
  28.7 0.0 collective-permute-start.3
  28.7 4.4 %collective-permute-start.4 = (f32[5,16,128]{2,1,0:T(8,128)S(1)}, f32[5,16,128]{2,1,0:T(8,128)S(1)}, u32[]{:S(2)}, u32[]{:S(2)}) collective-permute-start(f32[5,16,128]{2,1,0:T(8,128)S(1)} %get-tuple-element.24), channel_id=1, source_target_pairs={{0,14},{1,15},{2,0},{3,1},{4,2},{5,3},{6,4},{7,5},{8,6},{9,7},{10,... | collective-permute-start | bytes 122888 | tf_op jit(solution)/shard_map/ppermute | solution.py:366
  33.1 1.9 %collective-permute-start.5 = (f32[5,16,128]{2,1,0:T(8,128)S(1)}, f32[5,16,128]{2,1,0:T(8,128)S(1)}, u32[]{:S(2)}, u32[]{:S(2)}) collective-permute-start(f32[5,16,128]{2,1,0:T(8,128)S(1)} %get-tuple-element.25), channel_id=1, source_target_pairs={{0,2},{1,3},{2,4},{3,5},{4,6},{5,7},{6,8},{7,9},{8,10},{9,11},{10,... | collective-permute-start | bytes 122888 | tf_op jit(solution)/shard_map/ppermute | solution.py:366
  35.0 0.0 collective-permute-done.4.from_high_far
  35.0 5.2 %collective-permute-done.5.from_low_far = f32[5,16,128]{2,1,0:T(8,128)S(1)} collective-permute-done((f32[5,16,128]{2,1,0:T(8,128)S(1)}, f32[5,16,128]{2,1,0:T(8,128)S(1)}, u32[]{:S(2)}, u32[]{:S(2)}) %collective-permute-start.5) | collective-permute-done | bytes 40992 | tf_op jit(solution)/shard_map/ppermute | solution.py:366
  40.2 0.0 collective-permute-done.3.from_low
  40.2 0.0 collective-permute-done.2.from_high
  40.2 0.0 copy-start.3
  40.2 0.9 shard_map.106
  41.1 6.2 %collective-permute-start.6 = (f32[560,128]{1,0:T(8,128)S(1)}, f32[560,128]{1,0:T(8,128)S(1)}, u32[]{:S(2)}, u32[]{:S(2)}) collective-permute-start(f32[560,128]{1,0:T(8,128)S(1)} %get-tuple-element.28), channel_id=1, source_target_pairs={{0,896},{128,0},{256,128},{384,256},{512,384},{640,512},{768,640},... | collective-permute-start | bytes 860168 | tf_op jit(solution)/shard_map/ppermute | solution.py:366
  47.3 1.9 %collective-permute-start.7 = (f32[440,128]{1,0:T(8,128)S(1)}, f32[440,128]{1,0:T(8,128)S(1)}, u32[]{:S(2)}, u32[]{:S(2)}) collective-permute-start(f32[440,128]{1,0:T(8,128)S(1)} %get-tuple-element.29), channel_id=1, source_target_pairs={{0,128},{128,256},{256,384},{384,512},{512,640},{640,768},{768,896... | collective-permute-start | bytes 675848 | tf_op jit(solution)/shard_map/ppermute | solution.py:366
  49.2 4.6 %collective-permute-start.8 = (f32[40,128]{1,0:T(8,128)S(1)}, f32[40,128]{1,0:T(8,128)S(1)}, u32[]{:S(2)}, u32[]{:S(2)}) collective-permute-start(f32[40,128]{1,0:T(8,128)S(1)} %get-tuple-element.30), channel_id=1, source_target_pairs={{0,768},{128,896},{256,0},{384,128},{512,256},{640,384},{768,512},... | collective-permute-start | bytes 61448 | tf_op jit(solution)/shard_map/ppermute | solution.py:366
  53.8 2.2 %collective-permute-start.9 = (f32[40,128]{1,0:T(8,128)S(1)}, f32[40,128]{1,0:T(8,128)S(1)}, u32[]{:S(2)}, u32[]{:S(2)}) collective-permute-start(f32[40,128]{1,0:T(8,128)S(1)} %get-tuple-element.31), channel_id=1, source_target_pairs={{0,256},{128,384},{256,512},{384,640},{512,768},{640,896},{768,0},... | collective-permute-start | bytes 61448 | tf_op jit(solution)/shard_map/ppermute | solution.py:366
  56.0 0.0 collective-permute-done.8.from_high_far
  56.0 5.6 %collective-permute-done.9.from_low_far = f32[40,128]{1,0:T(8,128)S(1)} collective-permute-done((f32[40,128]{1,0:T(8,128)S(1)}, f32[40,128]{1,0:T(8,128)S(1)}, u32[]{:S(2)}, u32[]{:S(2)}) %collective-permute-start.9) | collective-permute-done | bytes 20512 | tf_op jit(solution)/shard_map/ppermute | solution.py:366
  61.6 0.0 collective-permute-done.7.from_low
  61.6 0.0 collective-permute-done.6.from_high
  61.6 0.0 copy-start.7
  61.6 0.0 copy-done.3
  61.6 0.6 copy-done.7
  62.3 3.1 %shard_map.107 = (f32[2048,128]{1,0:T(8,128)}, f32[2,40,16]{2,1,0:T(8,128)S(1)}) custom-call(s32[80]{0:T(128)S(1)} %bitcast.15, f32[16,80,128]{2,1,0:T(8,128)S(1)} %get-tuple-element.26.fine, f32[8,40,128]{2,1,0:T(8,128)S(1)} %get-tuple-element.27.coarse, f32[560,128]{1,0:T(8,128)S(1)} %collective-permute-done.6.from_high, ...), custom_call_target="tpu_custom_call" | custom-call | flops 1048576 | bytes 2434368 | tf_op jit(solution)/shard_map/pallas_call | solution.py:353
  65.4 10.5 %all-to-all-start = ((f32[64,32,128]{2,1,0:T(8,128)}), f32[64,32,128]{2,1,0:T(8,128)S(1)}, u32[]{:S(2)}, u32[]{:S(2)}) async-start(f32[64,32,128]{2,1,0:T(8,128)} %bitcast.6), calls=%async_computation | async-start | bytes 2097152 | tf_op jit(solution)/shard_map/all_to_all | solution.py:419
  75.8 0.1 slice.3
  76.0 0.1 reshape.32
  76.0 14.2 %all-gather = f32[16,2,160]{2,1,0:T(2,128)S(1)} all-gather(f32[1,2,160]{2,1,0:T(2,128)S(1)} %reshape.32), channel_id=1, replica_groups=mesh['gx'=8,'gy'=8,'gz'=16] {'gz'}, dimensions={0}, use_global_device_ids=true | all-gather | bytes 21760 | tf_op jit(solution)/shard_map/all_gather | solution.py:422
  90.3 0.0 copy-start.8
  90.3 0.7 copy-done.8
  91.0 1.0 fusion
  91.9 11.8 %all-to-all-done = f32[64,32,128]{2,1,0:T(8,128)S(1)} async-done(((f32[64,32,128]{2,1,0:T(8,128)}), f32[64,32,128]{2,1,0:T(8,128)S(1)}, u32[]{:S(2)}, u32[]{:S(2)}) %all-to-all-start) | async-done | bytes 1048608 | tf_op jit(solution)/shard_map/all_to_all | solution.py:419
  103.8 1.1 %reshape.31 = f32[128,2048]{1,0:T(8,128)} reshape(f32[64,32,128]{2,1,0:T(8,128)S(1)} %all-to-all-done) | data formatting | bytes 2097152 | tf_op jit(solution)/shard_map/reshape | solution.py:426
  (2 shorter events, 0.0 us)
Async XLA Ops:
  0.6 0.7 copy-start.5
  1.3 1.1 %copy-start = (f32[5,16,16,128]{3,2,1,0:T(8,128)S(1)}, f32[5,16,16,128]{3,2,1,0:T(8,128)}, u32[]{:S(2)}) copy-start(f32[5,16,16,128]{3,2,1,0:T(8,128)} %param.9) | copy-start | bytes 1966084
  2.4 0.7 copy-start.6
  3.1 19.5 %copy-start.1 = (bf16[128,256]{1,0:T(8,128)(2,1)S(1)}, bf16[128,256]{1,0:T(8,128)(2,1)}, u32[]{:S(2)}) copy-start(bf16[128,256]{1,0:T(8,128)(2,1)} %constant.17.clone.own_lo) | copy-start | bytes 196612
  3.1 19.5 %copy-start.2 = (bf16[128,256]{1,0:T(8,128)(2,1)S(1)}, bf16[128,256]{1,0:T(8,128)(2,1)}, u32[]{:S(2)}) copy-start(bf16[128,256]{1,0:T(8,128)(2,1)} %constant.16.clone.own_hi) | copy-start | bytes 196612
  3.1 19.5 %copy-start.4 = (bf16[32,256]{1,0:T(8,128)(2,1)S(1)}, bf16[32,256]{1,0:T(8,128)(2,1)}, u32[]{:S(2)}) copy-start(bf16[32,256]{1,0:T(8,128)(2,1)} %constant.18.clone.place) | copy-start | bytes 49156
  3.6 17.5 %collective-permute-start = (f32[16,1280]{1,0:T(8,128)S(1)}, f32[16,1280]{1,0:T(8,128)S(1)}, u32[]{:S(2)}, u32[]{:S(2)}) collective-permute-start(f32[16,1280]{1,0:T(8,128)S(1)} %get-tuple-element.18), channel_id=1, source_target_pairs={{0,16},{16,32},{32,48},{48,64},{64,80},{80,96},{96,112},{112,0},{1... | collective-permute-start | bytes 245768 | tf_op jit(solution)/shard_map/ppermute | solution.py:366
  7.0 15.7 %collective-permute-start.1 = (f32[16,1280]{1,0:T(8,128)S(1)}, f32[16,1280]{1,0:T(8,128)S(1)}, u32[]{:S(2)}, u32[]{:S(2)}) collective-permute-start(f32[16,1280]{1,0:T(8,128)S(1)} %get-tuple-element.19), channel_id=1, source_target_pairs={{0,112},{16,0},{32,16},{48,32},{64,48},{80,64},{96,80},{112,96},{1... | collective-permute-start | bytes 245768 | tf_op jit(solution)/shard_map/ppermute | solution.py:366
  24.6 15.7 %collective-permute-start.2 = (f32[5,10,16,128]{3,2,1,0:T(8,128)S(1)}, f32[5,10,16,128]{3,2,1,0:T(8,128)S(1)}, u32[]{:S(2)}, u32[]{:S(2)}) collective-permute-start(f32[5,10,16,128]{3,2,1,0:T(8,128)S(1)} %get-tuple-element.22), channel_id=1, source_target_pairs={{0,15},{1,0},{2,1},{3,2},{4,3},{5,4},{6,5},{7,6},{8,7},{9,8},{10,9... | collective-permute-start | bytes 1228808 | tf_op jit(solution)/shard_map/ppermute | solution.py:366
  28.7 11.6 %collective-permute-start.3 = (f32[5,8,16,128]{3,2,1,0:T(8,128)S(1)}, f32[5,8,16,128]{3,2,1,0:T(8,128)S(1)}, u32[]{:S(2)}, u32[]{:S(2)}) collective-permute-start(f32[5,8,16,128]{3,2,1,0:T(8,128)S(1)} %get-tuple-element.23), channel_id=1, source_target_pairs={{0,1},{1,2},{2,3},{3,4},{4,5},{5,6},{6,7},{7,8},{8,9},{9,10},{10,1... | collective-permute-start | bytes 983048 | tf_op jit(solution)/shard_map/ppermute | solution.py:366
  28.7 6.4 %collective-permute-start.4 = (f32[5,16,128]{2,1,0:T(8,128)S(1)}, f32[5,16,128]{2,1,0:T(8,128)S(1)}, u32[]{:S(2)}, u32[]{:S(2)}) collective-permute-start(f32[5,16,128]{2,1,0:T(8,128)S(1)} %get-tuple-element.24), channel_id=1, source_target_pairs={{0,14},{1,15},{2,0},{3,1},{4,2},{5,3},{6,4},{7,5},{8,6},{9,7},{10,... | collective-permute-start | bytes 122888 | tf_op jit(solution)/shard_map/ppermute | solution.py:366
  33.1 7.1 %collective-permute-start.5 = (f32[5,16,128]{2,1,0:T(8,128)S(1)}, f32[5,16,128]{2,1,0:T(8,128)S(1)}, u32[]{:S(2)}, u32[]{:S(2)}) collective-permute-start(f32[5,16,128]{2,1,0:T(8,128)S(1)} %get-tuple-element.25), channel_id=1, source_target_pairs={{0,2},{1,3},{2,4},{3,5},{4,6},{5,7},{6,8},{7,9},{8,10},{9,11},{10,... | collective-permute-start | bytes 122888 | tf_op jit(solution)/shard_map/ppermute | solution.py:366
  40.2 21.4 %copy-start.3 = (bf16[128,16]{1,0:T(8,128)(2,1)S(1)}, bf16[128,16]{1,0:T(8,128)(2,1)}, u32[]{:S(2)}) copy-start(bf16[128,16]{1,0:T(8,128)(2,1)} %constant.19.clone.pick) | copy-start | bytes 12292
  41.1 20.5 %collective-permute-start.6 = (f32[560,128]{1,0:T(8,128)S(1)}, f32[560,128]{1,0:T(8,128)S(1)}, u32[]{:S(2)}, u32[]{:S(2)}) collective-permute-start(f32[560,128]{1,0:T(8,128)S(1)} %get-tuple-element.28), channel_id=1, source_target_pairs={{0,896},{128,0},{256,128},{384,256},{512,384},{640,512},{768,640},... | collective-permute-start | bytes 860168 | tf_op jit(solution)/shard_map/ppermute | solution.py:366
  47.3 14.3 %collective-permute-start.7 = (f32[440,128]{1,0:T(8,128)S(1)}, f32[440,128]{1,0:T(8,128)S(1)}, u32[]{:S(2)}, u32[]{:S(2)}) collective-permute-start(f32[440,128]{1,0:T(8,128)S(1)} %get-tuple-element.29), channel_id=1, source_target_pairs={{0,128},{128,256},{256,384},{384,512},{512,640},{640,768},{768,896... | collective-permute-start | bytes 675848 | tf_op jit(solution)/shard_map/ppermute | solution.py:366
  49.2 6.8 %collective-permute-start.8 = (f32[40,128]{1,0:T(8,128)S(1)}, f32[40,128]{1,0:T(8,128)S(1)}, u32[]{:S(2)}, u32[]{:S(2)}) collective-permute-start(f32[40,128]{1,0:T(8,128)S(1)} %get-tuple-element.30), channel_id=1, source_target_pairs={{0,768},{128,896},{256,0},{384,128},{512,256},{640,384},{768,512},... | collective-permute-start | bytes 61448 | tf_op jit(solution)/shard_map/ppermute | solution.py:366
  53.8 7.8 %collective-permute-start.9 = (f32[40,128]{1,0:T(8,128)S(1)}, f32[40,128]{1,0:T(8,128)S(1)}, u32[]{:S(2)}, u32[]{:S(2)}) collective-permute-start(f32[40,128]{1,0:T(8,128)S(1)} %get-tuple-element.31), channel_id=1, source_target_pairs={{0,256},{128,384},{256,512},{384,640},{512,768},{640,896},{768,0},... | collective-permute-start | bytes 61448 | tf_op jit(solution)/shard_map/ppermute | solution.py:366
  61.6 0.7 copy-start.7
  65.4 38.4 %all-to-all-start = ((f32[64,32,128]{2,1,0:T(8,128)}), f32[64,32,128]{2,1,0:T(8,128)S(1)}, u32[]{:S(2)}, u32[]{:S(2)}) async-start(f32[64,32,128]{2,1,0:T(8,128)} %bitcast.6), calls=%async_computation | async-start | bytes 2097152 | tf_op jit(solution)/shard_map/all_to_all | solution.py:419
  90.3 0.7 copy-start.8

commit v2 on v1

v2 whole, which is shorter than its diff:
```python
import jax
import jax.numpy as jnp
import ml_dtypes
import numpy as np
from jax import lax
from jax.experimental import pallas as pl
from jax.experimental.pallas import tpu as pltpu
from jax.sharding import PartitionSpec as P

PREDICT_ONE = -1.586134342059924
UPDATE_ONE = -0.052980118572961
PREDICT_TWO = 0.882911075530934
UPDATE_TWO = 0.443506852043971
LOW_SCALE = 1.0 / 1.149604398860241
HIGH_SCALE = 1.149604398860241

F = 5
NB = 16
LN = 128
ROWS = F * NB * NB
TILES = F * NB

LOW_SIDE = (4, 6, 6)
HIGH_SIDE = (3, 5, 7)


def lift_np(values):
    low = values[0::2].copy()
    high = values[1::2].copy()
    high += PREDICT_ONE * (low + np.roll(low, -1, 0))
    low += UPDATE_ONE * (np.roll(high, 1, 0) + high)
    high += PREDICT_TWO * (low + np.roll(low, -1, 0))
    low += UPDATE_TWO * (np.roll(high, 1, 0) + high)
    joined = np.empty_like(values)
    joined[0::2] = low * LOW_SCALE
    joined[1::2] = high * HIGH_SCALE
    return joined


def split(matrix):
    matrix = np.asarray(matrix, np.float32)
    upper = matrix.astype(ml_dtypes.bfloat16)
    lower = (matrix - upper.astype(np.float32)).astype(ml_dtypes.bfloat16)
    return upper, lower


def y_matrices():
    total, start = 8 * LN, 4 * LN
    level = np.eye(total)
    maps = []
    for _ in range(3):
        level = lift_np(level)
        maps.append(level)
        level = level[0::2]
    own = np.zeros((LN, 2 * LN))
    send = np.zeros((32, LN))
    place = np.zeros((32, 2 * LN))
    columns = [lambda j: j, lambda j: LN + 2 * j, lambda j: LN + 4 * j + 1]
    at_low, at_high = 0, 16
    for depth in range(3):
        count = LN >> depth
        first = start >> depth
        block = maps[depth][:, start : start + LN]
        low, high = LOW_SIDE[depth], HIGH_SIDE[depth]
        assert not block[: first - low].any() and not block[first + count + high :].any()
        for j in range(count):
            own[:, columns[depth](j)] = block[first + j]
        for j in range(low):
            send[at_low] = block[first - low + j]
            place[at_low, columns[depth](count - low + j)] = 1
            at_low += 1
        for j in range(high):
            send[at_high] = block[first + count + j]
            place[at_high, columns[depth](j)] = 1
            at_high += 1
    return send, own, place


def lift(values):
    low = {i // 2: v for i, v in values.items() if i % 2 == 0}
    high = {i // 2: v for i, v in values.items() if i % 2 != 0}

    def add(target, source, factor, offsets):
        span = range(min(source) - 1, max(source) + 2)
        result = dict(target)
        for i in span:
            terms = [source[i + o] for o in offsets if i + o in source]
            if terms:
                step = factor * (terms[0] + terms[1] if len(terms) == 2 else terms[0])
                result[i] = result[i] + step if i in result else step
        return result

    high = add(high, low, PREDICT_ONE, (0, 1))
    low = add(low, high, UPDATE_ONE, (-1, 0))
    high = add(high, low, PREDICT_TWO, (0, 1))
    low = add(low, high, UPDATE_TWO, (-1, 0))
    joined = {2 * i: v * LOW_SCALE for i, v in low.items()}
    joined.update({2 * i + 1: v * HIGH_SCALE for i, v in high.items()})
    return joined


def lows(values):
    return {i // 2: v for i, v in values.items() if i % 2 == 0}


def dot(a, b, dims):
    return lax.dot_general(a, b, (dims, ((), ())), preferred_element_type=jnp.float32)


def halves(x):
    upper = x.astype(jnp.bfloat16)
    return upper, (x - upper.astype(jnp.float32)).astype(jnp.bfloat16)


def share_y_kernel(fields, send, to_low, to_high, cells, matrix, sems):
    copies = [
        pltpu.make_async_copy(fields, cells, sems.at[0]),
        pltpu.make_async_copy(send, matrix, sems.at[1]),
    ]
    for copy in copies:
        copy.start()
    for copy in copies:
        copy.wait()
    cells_hi, cells_lo = halves(cells[...])
    send_hi, send_lo = matrix[:32], matrix[32:]
    dims = ((1,), (1,))
    shares = dot(send_hi, cells_hi, dims) + dot(send_hi, cells_lo, dims) + dot(send_lo, cells_hi, dims)
    to_low[...] = shares[:16]
    to_high[...] = shares[16:]


def slots_kernel(writers, targets, counts):
    for i in range(64):
        counts[i] = 0
    for t in range(TILES):
        writer = writers[t]
        slot = counts[writer]
        counts[writer] = slot + 1
        targets[t] = writer * 2 + slot


def fine_shares(values):
    return lift(values)


def coarse_shares(values):
    second = lift(lows(lift(values)))
    third = lift(lows(second))
    return second, third


class Lanes:
    def __init__(self):
        self.lane = lax.broadcasted_iota(jnp.int32, (8, LN), 1)
        self.second = self.lane % 2 == 0
        self.third = self.lane % 4 == 1
        self.ahead = [self.lane % 4 == (1 + i) % 4 for i in range(4)]

    @staticmethod
    def roll(x, by):
        return pltpu.roll(x, by % LN, 1) if by % LN else x

    def pack_second(self, rows):
        packed = []
        for i in range(0, len(rows), 2):
            odd = self.roll(rows[i + 1], 1) if i + 1 < len(rows) else rows[i]
            packed.append(jnp.where(self.second, rows[i], odd))
        return packed

    def pack_third(self, rows):
        packed = rows[0]
        for i in range(1, len(rows)):
            packed = jnp.where(self.ahead[i], self.roll(rows[i], i), packed)
        return packed


def send_rows(second, third, lanes):
    near_low = lanes.pack_second([second[i - 6] for i in range(6)]) + [lanes.pack_third([third[i - 4] for i in range(4)])]
    near_high = lanes.pack_second([second[8 + i] for i in range(5)]) + [lanes.pack_third([third[4 + i] for i in range(4)])]
    return near_low, near_high, lanes.pack_third([third[-6], third[-5]]), lanes.pack_third([third[8], third[9], third[10]])


def share_z_kernel(
    fields, maps, from_low, from_high, fine, coarse, to_low, to_high, to_low_far, to_high_far, work
):
    cells_hi, cells_lo = halves(fields[...])
    dims = ((1,), (0,))
    low_hi, low_lo = halves(from_high[...])
    high_hi, high_lo = halves(from_low[...])
    turned = ((0,), (0,))
    own_hi, own_lo, place_low, place_high = maps[:128], maps[128:256], maps[256:272], maps[272:]
    work[...] = (
        dot(cells_hi, own_hi, dims)
        + dot(cells_lo, own_hi, dims)
        + dot(cells_hi, own_lo, dims)
        + dot(low_hi, place_low, turned)
        + dot(low_lo, place_low, turned)
        + dot(high_hi, place_high, turned)
        + dot(high_lo, place_high, turned)
    )
    lanes = Lanes()
    for f in range(F):
        for half in (0, 8):
            rows = slice(half, half + 8)
            at = [f * 256 + z * 16 + half for z in range(NB)]
            done = fine_shares({z: work[at[z] : at[z] + 8, :LN] for z in range(NB)})
            for z in range(NB):
                fine[at[z] : at[z] + 8] = done[z]
            for i in range(4):
                to_low[f, i, rows] = done[i - 4]
            for i in range(3):
                to_high[f, i, rows] = done[16 + i]
            second, third = coarse_shares({z: work[at[z] : at[z] + 8, LN:] for z in range(NB)})
            for z in range(8):
                row = jnp.where(lanes.second, second[z], third[z // 2]) if z % 2 == 0 else second[z]
                coarse[f * 128 + z * 16 + half : f * 128 + z * 16 + half + 8] = row
            near_low, near_high, far_low, far_high = send_rows(second, third, lanes)
            for i in range(4):
                to_low[f, 4 + i, rows] = near_low[i]
                to_high[f, 3 + i, rows] = near_high[i]
            to_low_far[f, rows] = far_low
            to_high_far[f, rows] = far_high


def add_coarse(base, near_low, near_high, far_low, far_high, lanes):
    zero = jnp.zeros_like(base[0])
    extra = [zero] * 8
    for i in range(6):
        extra[2 + i] = extra[2 + i] + lanes.roll(near_low[i // 2], -(i % 2))
    for i in range(5):
        extra[i] = extra[i] + lanes.roll(near_high[i // 2], -(i % 2))
    near = near_low[3] + near_high[3]
    near = near + jnp.where(lanes.ahead[3], zero, far_high)
    third = [lanes.roll(near, -r) for r in range(4)]
    third[2] = third[2] + far_low
    third[3] = third[3] + lanes.roll(far_low, -1)
    rows = []
    for i in range(8):
        other = jnp.where(lanes.third, third[i // 2], zero) if i % 2 == 0 else zero
        rows.append(base[i] + jnp.where(lanes.second, extra[i], other))
    return rows


def share_x_kernel(
    fine, coarse, from_high, from_low, from_high_far, from_low_far,
    own_fine, own_coarse, to_low, to_high, to_low_far, to_high_far, work, work_coarse,
):
    lanes = Lanes()
    for f in range(F):
        at = f * 256
        work[at : at + 48] = fine[at : at + 48] + from_low[f, :3].reshape(48, LN)
        work[at + 48 : at + 192] = fine[at + 48 : at + 192]
        work[at + 192 : at + 256] = fine[at + 192 : at + 256] + from_high[f, :4].reshape(64, LN)
        for half in (0, 8):
            rows = slice(half, half + 8)
            at = [f * 128 + z * 16 + half for z in range(8)]
            added = add_coarse(
                [coarse[at[z] : at[z] + 8] for z in range(8)],
                [from_high[f, 4 + i, rows] for i in range(4)],
                [from_low[f, 3 + i, rows] for i in range(4)],
                from_high_far[f, rows],
                from_low_far[f, rows],
                lanes,
            )
            for z in range(8):
                work_coarse[at[z] : at[z] + 8] = added[z]
    for g in range(10):
        rows = slice(g * 8, g * 8 + 8)
        done = fine_shares({x: work[pl.ds(g * 128 + x, 8, stride=16), :] for x in range(NB)})
        for x in range(NB):
            own_fine[x, rows] = done[x]
        for i in range(4):
            to_low[i * 80 + g * 8 : i * 80 + g * 8 + 8] = done[i - 4]
        for i in range(3):
            to_high[i * 80 + g * 8 : i * 80 + g * 8 + 8] = done[16 + i]
    for g in range(5):
        rows = slice(g * 8, g * 8 + 8)
        second, third = coarse_shares({x: work_coarse[pl.ds(g * 128 + x, 8, stride=16), :] for x in range(NB)})
        for x in range(8):
            own_coarse[x, rows] = jnp.where(lanes.second, second[x], third[x // 2]) if x % 2 == 0 else second[x]
        near_low, near_high, far_low, far_high = send_rows(second, third, lanes)
        for i in range(4):
            to_low[320 + i * 40 + g * 8 : 320 + i * 40 + g * 8 + 8] = near_low[i]
            to_high[240 + i * 40 + g * 8 : 240 + i * 40 + g * 8 + 8] = near_high[i]
        to_low_far[rows] = far_low
        to_high_far[rows] = far_high


def route_kernel(
    targets, fine, coarse, from_high, from_low, from_high_far, from_low_far, outbox, low_band, tiles, spread
):
    shape = (8, LN)
    lanes = Lanes()
    lane = lanes.lane
    even_row = lax.broadcasted_iota(jnp.int32, shape, 0) % 2 == 0
    replaced = (lane % 4 == 0) & even_row
    merged = lanes.second & even_row
    picked = (LN, 16)
    pick = lax.broadcasted_iota(jnp.int32, picked, 0) == 8 * lax.broadcasted_iota(jnp.int32, picked, 1) + 1
    pick = jnp.where(pick, jnp.ones(picked, jnp.float32), jnp.zeros(picked, jnp.float32)).astype(jnp.bfloat16)
    outbox[...] = jnp.zeros_like(outbox)
    for g in range(5):
        rows = slice(g * 8, g * 8 + 8)
        added = add_coarse(
            [coarse[x, rows] for x in range(8)],
            [from_high[320 + i * 40 + g * 8 : 320 + i * 40 + g * 8 + 8] for i in range(4)],
            [from_low[240 + i * 40 + g * 8 : 240 + i * 40 + g * 8 + 8] for i in range(4)],
            from_high_far[rows],
            from_low_far[rows],
            lanes,
        )
        for i, x in ((0, 0), (1, 4)):
            upper, lower = halves(added[x])
            rest = (added[x] - upper.astype(jnp.float32) - lower.astype(jnp.float32)).astype(jnp.bfloat16)
            dims = ((1,), (0,))
            low_band[i, rows] = dot(upper, pick, dims) + dot(lower, pick, dims) + dot(rest, pick, dims)
        for x in range(8):
            row = added[x]
            if x % 2 == 0:
                row = jnp.where(replaced, lanes.roll(row, -1), row)
            spread[pl.ds(x * 80 + g * 16, 8, stride=2), :] = row
            spread[pl.ds(x * 80 + g * 16 + 1, 8, stride=2), :] = row
    for g in range(10):
        rows = slice(g * 8, g * 8 + 8)
        for x in range(NB):
            row = fine[x, rows]
            if x < 3:
                row = row + from_low[x * 80 + g * 8 : x * 80 + g * 8 + 8]
            if x >= 12:
                i = x - 12
                row = row + from_high[i * 80 + g * 8 : i * 80 + g * 8 + 8]
            if x % 2 == 0:
                row = jnp.where(merged, spread[x // 2 * 80 + g * 8 : x // 2 * 80 + g * 8 + 8], row)
            tiles[pl.ds(g * 128 + x, 8, stride=16), :] = row

    for t in range(TILES):
        to = pl.multiple_of(targets[t] * 16, 16)
        outbox[pl.ds(to, 16), :] = tiles[t * 16 : t * 16 + 16]


VM = pl.BlockSpec(memory_space=pltpu.VMEM)
SM = pl.BlockSpec(memory_space=pltpu.SMEM)
HB = pl.BlockSpec(memory_space=pltpu.HBM)


def f32(*shape):
    return jax.ShapeDtypeStruct(shape, jnp.float32)


def call(kernel, outs, ins, scratch=(), specs=None, out_specs=None, flops=1 << 20, grant=32 << 20):
    moved = sum(4 * int(np.prod(a.shape)) for a in list(outs) + list(ins))
    return pl.pallas_call(
        kernel,
        out_shape=list(outs),
        in_specs=specs or [VM] * len(ins),
        out_specs=out_specs or [VM] * len(outs),
        scratch_shapes=list(scratch),
        compiler_params=pltpu.CompilerParams(vmem_limit_bytes=grant),
        cost_estimate=pl.CostEstimate(flops=flops, bytes_accessed=moved, transcendentals=0),
    )(*ins)


def shift(array, axis, by):
    count = lax.axis_size(axis)
    return lax.ppermute(array, axis, [(i, (i + by) % count) for i in range(count)])


def coarse_matrix(length):
    level_four = lift_np(np.eye(length))
    level_five = lift_np(level_four[0::2])
    level_four[0::2] = level_five
    return level_four.astype(np.float32)


def body(fields, tile_writer):
    send, own, place = y_matrices()
    send = jnp.asarray(np.concatenate(split(send)))
    maps = jnp.asarray(np.concatenate([*split(own), place.astype(ml_dtypes.bfloat16)]))
    cells = fields.reshape(ROWS, LN)

    to_low, to_high = call(
        share_y_kernel,
        [f32(16, ROWS)] * 2,
        [cells, send],
        [pltpu.VMEM((ROWS, LN), jnp.float32), pltpu.VMEM((64, LN), jnp.bfloat16), pltpu.SemaphoreType.DMA((2,))],
        [HB, HB],
        grant=60 << 20,
    )
    from_high = shift(to_low, "gy", -1)
    from_low = shift(to_high, "gy", 1)

    (targets,) = call(
        slots_kernel,
        [jax.ShapeDtypeStruct((TILES,), jnp.int32)],
        [tile_writer.reshape(TILES)],
        [pltpu.SMEM((64,), jnp.int32)],
        [SM],
        [SM],
        flops=1 << 30,
    )
    fine, coarse, to_low, to_high, to_low_far, to_high_far = call(
        share_z_kernel,
        [f32(ROWS, LN), f32(ROWS // 2, LN), f32(F, 8, 16, LN), f32(F, 7, 16, LN), f32(F, 16, LN), f32(F, 16, LN)],
        [cells, maps, from_low, from_high],
        [pltpu.VMEM((ROWS, 2 * LN), jnp.float32)],
    )
    from_high = shift(to_low, "gz", -1)
    from_low = shift(to_high, "gz", 1)
    from_high_far = shift(to_low_far, "gz", -2)
    from_low_far = shift(to_high_far, "gz", 2)

    fine, coarse, to_low, to_high, to_low_far, to_high_far = call(
        share_x_kernel,
        [f32(16, 80, LN), f32(8, 40, LN), f32(480, LN), f32(400, LN), f32(40, LN), f32(40, LN)],
        [fine, coarse, from_high, from_low, from_high_far, from_low_far],
        [pltpu.VMEM((ROWS, LN), jnp.float32), pltpu.VMEM((ROWS // 2, LN), jnp.float32)],
    )
    from_high = shift(to_low, "gx", -1)
    from_low = shift(to_high, "gx", 1)
    from_high_far = shift(to_low_far, "gx", -2)
    from_low_far = shift(to_high_far, "gx", 2)

    outbox, low_band = call(
        route_kernel,
        [f32(2048, LN), f32(2, 40, 16)],
        [targets, fine, coarse, from_high, from_low, from_high_far, from_low_far],
        [pltpu.VMEM((ROWS, LN), jnp.float32), pltpu.VMEM((640, LN), jnp.float32)],
        [SM] + [VM] * 6,
    )
    inbox = lax.all_to_all(outbox.reshape(64, 32, LN), ("gx", "gy"), split_axis=0, concat_axis=0, tiled=True)

    band = low_band.reshape(2, F, 8, 16)[:, :, ::4].transpose(2, 1, 0, 3).reshape(2, F * 32)
    band = lax.all_gather(band, "gz", axis=0, tiled=True)
    turn = jnp.asarray(coarse_matrix(band.shape[0]))
    bands = jnp.dot(turn, band, precision=lax.Precision.HIGHEST)
    bands = bands.reshape(-1, F, 2, 16).transpose(1, 0, 2, 3)
    return (bands, inbox.reshape(128, 2048))


def solution(mesh):
    return jax.shard_map(
        body,
        mesh=mesh,
        in_specs=(P(None, "gz", "gx", "gy"), P("gx", "gy", "gz", None)),
        out_specs=(P(None, None, "gx", "gy"), P(("gx", "gy"), "gz")),
        check_vma=False,
    )
```

time: 106 us -> 104 us (0.981)
  Pallas kernels: 6.34 us -> 8.74 us
  local copies, waits for them, and re-layouts: 5.16 us -> 2.95 us
  waiting for transfers between devices: 24.7 us -> 23.4 us
    pallas_call x4 -> x5, Pallas kernels: 6.34 us -> 8.74 us  [call(): pl.pallas_call(kernel, out_shape=list(outs), in_specs=specs or [VM] * len...]
    unnamed x21 -> x11, local copies, waits for them, and re-layouts: 3.94 us -> 1.73 us
    ppermute x10, waiting for transfers between devices: 12.9 us -> 11.6 us  [shift(): lax.ppermute(array, axis, [(i, (i + by) % count) for i in range(count)])]
  transfers between devices with their start and end apart: 11 -> 11, of which waited for: 5 -> 5; matrix products, arithmetic and copies ran while one was open for 1% -> 1% of each run, Pallas kernels for 0% -> 1%
where the time goes in v2:
time: 104 us
  starting transfers between devices  52.6 us (51%)
  waiting for transfers between devices  23.4 us (22%)
  blocking collectives  14.2 us (14%)
  Pallas kernels  8.74 us (8%)
  local copies, waits for them, and re-layouts  2.95 us (3%)
    ppermute x10, starting transfers between devices, shift(): lax.ppermute(array, axis, [(i, (i + by) % count) for i in range(count)])  42.2 us
    all_gather x1, blocking collectives, body(): band = lax.all_gather(band, 'gz', axis=0, tiled=True)  14.2 us
    all_to_all x1, waiting for transfers between devices, body(): lax.all_to_all(outbox.reshape(64, 32, LN), ('gx', 'gy'), split_axis=0, co...  11.8 us
    ppermute x10, waiting for transfers between devices, shift(): lax.ppermute(array, axis, [(i, (i + by) % count) for i in range(count)])  11.6 us
    all_to_all x1, starting transfers between devices, body(): lax.all_to_all(outbox.reshape(64, 32, LN), ('gx', 'gy'), split_axis=0, co...  10.5 us
    pallas_call x5, Pallas kernels, call(): pl.pallas_call(kernel, out_shape=list(outs), in_specs=specs or [VM] * len...  8.74 us
  transfers between devices with their start and end apart: 11, of which 5 were waited for; matrix products, arithmetic and copies ran while one was open for 1% of the time, Pallas kernels for 1%

profile of v2, /device:TPU:2, one launch (start us, length us, event | category | flops | bytes accessed | tf_op | source)
XLA Modules:
  0.0 103.7 jit_solution(16534681445084235344)
XLA Ops:
  0.6 0.0 copy-start
  0.6 2.3 %shard_map.69 = (f32[16,1280]{1,0:T(8,128)}, f32[16,1280]{1,0:T(8,128)}) custom-call(f32[1280,128]{1,0:T(8,128)} %bitcast.12, bf16[64,128]{1,0:T(8,128)(2,1)} %constant.6.clone.send), custom_call_target="tpu_custom_call" | custom-call | flops 1048576 | bytes 851968 | tf_op jit(solution)/shard_map/pallas_call | solution.py:352
  2.9 3.4 %collective-permute-start = (f32[16,1280]{1,0:T(8,128)}, f32[16,1280]{1,0:T(8,128)S(1)}, u32[]{:S(2)}, u32[]{:S(2)}) collective-permute-start(f32[16,1280]{1,0:T(8,128)} %get-tuple-element.18), channel_id=1, source_target_pairs={{0,16},{16,32},{32,48},{48,64},{64,80},{80,96},{96,112},{112,0},{1... | collective-permute-start | bytes 245768 | tf_op jit(solution)/shard_map/ppermute | solution.py:365
  6.3 13.6 %collective-permute-start.1 = (f32[16,1280]{1,0:T(8,128)}, f32[16,1280]{1,0:T(8,128)S(1)}, u32[]{:S(2)}, u32[]{:S(2)}) collective-permute-start(f32[16,1280]{1,0:T(8,128)} %get-tuple-element.19), channel_id=1, source_target_pairs={{0,112},{16,0},{32,16},{48,32},{64,48},{80,64},{96,80},{112,96},{1... | collective-permute-start | bytes 245768 | tf_op jit(solution)/shard_map/ppermute | solution.py:365
  20.0 0.7 collective-permute-done.from_low
  20.7 1.7 %collective-permute-done.1.from_high = f32[16,1280]{1,0:T(8,128)S(1)} collective-permute-done((f32[16,1280]{1,0:T(8,128)}, f32[16,1280]{1,0:T(8,128)S(1)}, u32[]{:S(2)}, u32[]{:S(2)}) %collective-permute-start.1) | collective-permute-done | bytes 81952 | tf_op jit(solution)/shard_map/ppermute | solution.py:365
  22.3 0.0 copy-done
  22.3 0.0 copy-start.1
  22.3 0.9 copy-done.1
  23.2 2.0 %shard_map.70 = (f32[1280,128]{1,0:T(8,128)S(1)}, f32[640,128]{1,0:T(8,128)S(1)}, f32[5,8,16,128]{3,2,1,0:T(8,128)S(1)}, f32[5,7,16,128]{3,2,1,0:T(8,128)S(1)}, ...) custom-call(f32[1280,128]{1,0:T(8,128)S(1)} %bitcast.13, bf16[288,256]{1,0:T(8,128)(2,1)S(1)} %copy-done.1, ...), custom_call_target="tpu_custom_call" | custom-call | flops 1048576 | bytes 2793472 | tf_op jit(solution)/shard_map/pallas_call | solution.py:352
  25.2 4.0 %collective-permute-start.2 = (f32[5,8,16,128]{3,2,1,0:T(8,128)S(1)}, f32[5,8,16,128]{3,2,1,0:T(8,128)S(1)}, u32[]{:S(2)}, u32[]{:S(2)}) collective-permute-start(f32[5,8,16,128]{3,2,1,0:T(8,128)S(1)} %get-tuple-element.22), channel_id=1, source_target_pairs={{0,15},{1,0},{2,1},{3,2},{4,3},{5,4},{6,5},{7,6},{8,7},{9,8},{10,9... | collective-permute-start | bytes 983048 | tf_op jit(solution)/shard_map/ppermute | solution.py:365
  29.2 0.0 collective-permute-start.3
  29.2 4.4 %collective-permute-start.4 = (f32[5,16,128]{2,1,0:T(8,128)S(1)}, f32[5,16,128]{2,1,0:T(8,128)S(1)}, u32[]{:S(2)}, u32[]{:S(2)}) collective-permute-start(f32[5,16,128]{2,1,0:T(8,128)S(1)} %get-tuple-element.24), channel_id=1, source_target_pairs={{0,14},{1,15},{2,0},{3,1},{4,2},{5,3},{6,4},{7,5},{8,6},{9,7},{10,... | collective-permute-start | bytes 122888 | tf_op jit(solution)/shard_map/ppermute | solution.py:365
  33.6 1.9 %collective-permute-start.5 = (f32[5,16,128]{2,1,0:T(8,128)S(1)}, f32[5,16,128]{2,1,0:T(8,128)S(1)}, u32[]{:S(2)}, u32[]{:S(2)}) collective-permute-start(f32[5,16,128]{2,1,0:T(8,128)S(1)} %get-tuple-element.25), channel_id=1, source_target_pairs={{0,2},{1,3},{2,4},{3,5},{4,6},{5,7},{6,8},{7,9},{8,10},{9,11},{10,... | collective-permute-start | bytes 122888 | tf_op jit(solution)/shard_map/ppermute | solution.py:365
  35.5 0.0 collective-permute-done.4.from_high_far
  35.5 5.2 %collective-permute-done.5.from_low_far = f32[5,16,128]{2,1,0:T(8,128)S(1)} collective-permute-done((f32[5,16,128]{2,1,0:T(8,128)S(1)}, f32[5,16,128]{2,1,0:T(8,128)S(1)}, u32[]{:S(2)}, u32[]{:S(2)}) %collective-permute-start.5) | collective-permute-done | bytes 40992 | tf_op jit(solution)/shard_map/ppermute | solution.py:365
  40.7 0.0 collective-permute-done.3.from_low
  40.8 0.0 collective-permute-done.2.from_high
  40.8 1.0 shard_map.71
  41.7 6.2 %collective-permute-start.6 = (f32[480,128]{1,0:T(8,128)S(1)}, f32[480,128]{1,0:T(8,128)S(1)}, u32[]{:S(2)}, u32[]{:S(2)}) collective-permute-start(f32[480,128]{1,0:T(8,128)S(1)} %get-tuple-element.28), channel_id=1, source_target_pairs={{0,896},{128,0},{256,128},{384,256},{512,384},{640,512},{768,640},... | collective-permute-start | bytes 737288 | tf_op jit(solution)/shard_map/ppermute | solution.py:365
  47.9 1.9 %collective-permute-start.7 = (f32[400,128]{1,0:T(8,128)S(1)}, f32[400,128]{1,0:T(8,128)S(1)}, u32[]{:S(2)}, u32[]{:S(2)}) collective-permute-start(f32[400,128]{1,0:T(8,128)S(1)} %get-tuple-element.29), channel_id=1, source_target_pairs={{0,128},{128,256},{256,384},{384,512},{512,640},{640,768},{768,896... | collective-permute-start | bytes 614408 | tf_op jit(solution)/shard_map/ppermute | solution.py:365
  49.8 4.6 %collective-permute-start.8 = (f32[40,128]{1,0:T(8,128)S(1)}, f32[40,128]{1,0:T(8,128)S(1)}, u32[]{:S(2)}, u32[]{:S(2)}) collective-permute-start(f32[40,128]{1,0:T(8,128)S(1)} %get-tuple-element.30), channel_id=1, source_target_pairs={{0,768},{128,896},{256,0},{384,128},{512,256},{640,384},{768,512},... | collective-permute-start | bytes 61448 | tf_op jit(solution)/shard_map/ppermute | solution.py:365
  54.4 0.0 copy-start.2
  54.4 2.2 %collective-permute-start.9 = (f32[40,128]{1,0:T(8,128)S(1)}, f32[40,128]{1,0:T(8,128)S(1)}, u32[]{:S(2)}, u32[]{:S(2)}) collective-permute-start(f32[40,128]{1,0:T(8,128)S(1)} %get-tuple-element.31), channel_id=1, source_target_pairs={{0,256},{128,384},{256,512},{384,640},{512,768},{640,896},{768,0},... | collective-permute-start | bytes 61448 | tf_op jit(solution)/shard_map/ppermute | solution.py:365
  56.6 0.0 copy-done.2
  56.6 1.5 %shard_map.68.targets = s32[80]{0:T(128)S(1)} custom-call(s32[80]{0:T(128)S(1)} %bitcast.15), custom_call_target="tpu_custom_call" | custom-call | flops 1073741824 | bytes 640 | tf_op jit(solution)/shard_map/pallas_call | solution.py:352
  58.2 0.0 collective-permute-done.8.from_high_far
  58.2 4.1 %collective-permute-done.9.from_low_far = f32[40,128]{1,0:T(8,128)S(1)} collective-permute-done((f32[40,128]{1,0:T(8,128)S(1)}, f32[40,128]{1,0:T(8,128)S(1)}, u32[]{:S(2)}, u32[]{:S(2)}) %collective-permute-start.9) | collective-permute-done | bytes 20512 | tf_op jit(solution)/shard_map/ppermute | solution.py:365
  62.2 0.0 collective-permute-done.7.from_low
  62.2 0.0 collective-permute-done.6.from_high
  62.2 2.0 %shard_map.72 = (f32[2048,128]{1,0:T(8,128)}, f32[2,40,16]{2,1,0:T(8,128)S(1)}) custom-call(s32[80]{0:T(128)S(1)} %shard_map.68.targets, f32[16,80,128]{2,1,0:T(8,128)S(1)} %get-tuple-element.26.fine, f32[8,40,128]{2,1,0:T(8,128)S(1)} %get-tuple-element.27.coarse, f32[480,128]{1,0:T(8,128)S(1)} %collective-permute-done.6.from_high, ...), custom_call_target="tpu_custom_call" | custom-call | flops 1048576 | bytes 2364736 | tf_op jit(solution)/shard_map/pallas_call | solution.py:352
  64.2 10.5 %all-to-all-start = ((f32[64,32,128]{2,1,0:T(8,128)}), f32[64,32,128]{2,1,0:T(8,128)S(1)}, u32[]{:S(2)}, u32[]{:S(2)}) async-start(f32[64,32,128]{2,1,0:T(8,128)} %bitcast.6), calls=%async_computation | async-start | bytes 2097152 | tf_op jit(solution)/shard_map/all_to_all | solution.py:430
  74.7 0.1 slice.3
  74.8 0.1 reshape.32
  74.9 14.2 %all-gather = f32[16,2,160]{2,1,0:T(2,128)S(1)} all-gather(f32[1,2,160]{2,1,0:T(2,128)S(1)} %reshape.32), channel_id=1, replica_groups=mesh['gx'=8,'gy'=8,'gz'=16] {'gz'}, dimensions={0}, use_global_device_ids=true | all-gather | bytes 21760 | tf_op jit(solution)/shard_map/all_gather | solution.py:433
  89.1 0.0 copy-start.3
  89.1 0.7 copy-done.3
  89.8 1.0 fusion
  90.8 11.8 %all-to-all-done = f32[64,32,128]{2,1,0:T(8,128)S(1)} async-done(((f32[64,32,128]{2,1,0:T(8,128)}), f32[64,32,128]{2,1,0:T(8,128)S(1)}, u32[]{:S(2)}, u32[]{:S(2)}) %all-to-all-start) | async-done | bytes 1048608 | tf_op jit(solution)/shard_map/all_to_all | solution.py:430
  102.6 1.1 %reshape.31 = f32[128,2048]{1,0:T(8,128)} reshape(f32[64,32,128]{2,1,0:T(8,128)S(1)} %all-to-all-done) | data formatting | bytes 2097152 | tf_op jit(solution)/shard_map/reshape | solution.py:437
  (2 shorter events, 0.0 us)
Async XLA Ops:
  0.6 21.7 %copy-start = (f32[5,16,16,128]{3,2,1,0:T(8,128)S(1)}, f32[5,16,16,128]{3,2,1,0:T(8,128)}, u32[]{:S(2)}) copy-start(f32[5,16,16,128]{3,2,1,0:T(8,128)} %param.5) | copy-start | bytes 1966084
  2.9 17.7 %collective-permute-start = (f32[16,1280]{1,0:T(8,128)}, f32[16,1280]{1,0:T(8,128)S(1)}, u32[]{:S(2)}, u32[]{:S(2)}) collective-permute-start(f32[16,1280]{1,0:T(8,128)} %get-tuple-element.18), channel_id=1, source_target_pairs={{0,16},{16,32},{32,48},{48,64},{64,80},{80,96},{96,112},{112,0},{1... | collective-permute-start | bytes 245768 | tf_op jit(solution)/shard_map/ppermute | solution.py:365
  6.3 16.0 %collective-permute-start.1 = (f32[16,1280]{1,0:T(8,128)}, f32[16,1280]{1,0:T(8,128)S(1)}, u32[]{:S(2)}, u32[]{:S(2)}) collective-permute-start(f32[16,1280]{1,0:T(8,128)} %get-tuple-element.19), channel_id=1, source_target_pairs={{0,112},{16,0},{32,16},{48,32},{64,48},{80,64},{96,80},{112,96},{1... | collective-permute-start | bytes 245768 | tf_op jit(solution)/shard_map/ppermute | solution.py:365
  22.3 0.9 copy-start.1
  25.2 15.6 %collective-permute-start.2 = (f32[5,8,16,128]{3,2,1,0:T(8,128)S(1)}, f32[5,8,16,128]{3,2,1,0:T(8,128)S(1)}, u32[]{:S(2)}, u32[]{:S(2)}) collective-permute-start(f32[5,8,16,128]{3,2,1,0:T(8,128)S(1)} %get-tuple-element.22), channel_id=1, source_target_pairs={{0,15},{1,0},{2,1},{3,2},{4,3},{5,4},{6,5},{7,6},{8,7},{9,8},{10,9... | collective-permute-start | bytes 983048 | tf_op jit(solution)/shard_map/ppermute | solution.py:365
  29.2 11.6 %collective-permute-start.3 = (f32[5,7,16,128]{3,2,1,0:T(8,128)S(1)}, f32[5,7,16,128]{3,2,1,0:T(8,128)S(1)}, u32[]{:S(2)}, u32[]{:S(2)}) collective-permute-start(f32[5,7,16,128]{3,2,1,0:T(8,128)S(1)} %get-tuple-element.23), channel_id=1, source_target_pairs={{0,1},{1,2},{2,3},{3,4},{4,5},{5,6},{6,7},{7,8},{8,9},{9,10},{10,1... | collective-permute-start | bytes 860168 | tf_op jit(solution)/shard_map/ppermute | solution.py:365
  29.2 6.3 %collective-permute-start.4 = (f32[5,16,128]{2,1,0:T(8,128)S(1)}, f32[5,16,128]{2,1,0:T(8,128)S(1)}, u32[]{:S(2)}, u32[]{:S(2)}) collective-permute-start(f32[5,16,128]{2,1,0:T(8,128)S(1)} %get-tuple-element.24), channel_id=1, source_target_pairs={{0,14},{1,15},{2,0},{3,1},{4,2},{5,3},{6,4},{7,5},{8,6},{9,7},{10,... | collective-permute-start | bytes 122888 | tf_op jit(solution)/shard_map/ppermute | solution.py:365
  33.6 7.1 %collective-permute-start.5 = (f32[5,16,128]{2,1,0:T(8,128)S(1)}, f32[5,16,128]{2,1,0:T(8,128)S(1)}, u32[]{:S(2)}, u32[]{:S(2)}) collective-permute-start(f32[5,16,128]{2,1,0:T(8,128)S(1)} %get-tuple-element.25), channel_id=1, source_target_pairs={{0,2},{1,3},{2,4},{3,5},{4,6},{5,7},{6,8},{7,9},{8,10},{9,11},{10,... | collective-permute-start | bytes 122888 | tf_op jit(solution)/shard_map/ppermute | solution.py:365
  41.7 20.5 %collective-permute-start.6 = (f32[480,128]{1,0:T(8,128)S(1)}, f32[480,128]{1,0:T(8,128)S(1)}, u32[]{:S(2)}, u32[]{:S(2)}) collective-permute-start(f32[480,128]{1,0:T(8,128)S(1)} %get-tuple-element.28), channel_id=1, source_target_pairs={{0,896},{128,0},{256,128},{384,256},{512,384},{640,512},{768,640},... | collective-permute-start | bytes 737288 | tf_op jit(solution)/shard_map/ppermute | solution.py:365
  47.9 14.3 %collective-permute-start.7 = (f32[400,128]{1,0:T(8,128)S(1)}, f32[400,128]{1,0:T(8,128)S(1)}, u32[]{:S(2)}, u32[]{:S(2)}) collective-permute-start(f32[400,128]{1,0:T(8,128)S(1)} %get-tuple-element.29), channel_id=1, source_target_pairs={{0,128},{128,256},{256,384},{384,512},{512,640},{640,768},{768,896... | collective-permute-start | bytes 614408 | tf_op jit(solution)/shard_map/ppermute | solution.py:365
  49.8 8.3 %collective-permute-start.8 = (f32[40,128]{1,0:T(8,128)S(1)}, f32[40,128]{1,0:T(8,128)S(1)}, u32[]{:S(2)}, u32[]{:S(2)}) collective-permute-start(f32[40,128]{1,0:T(8,128)S(1)} %get-tuple-element.30), channel_id=1, source_target_pairs={{0,768},{128,896},{256,0},{384,128},{512,256},{640,384},{768,512},... | collective-permute-start | bytes 61448 | tf_op jit(solution)/shard_map/ppermute | solution.py:365
  54.4 2.2 %copy-start.2 = (s32[1,1,80,1]{2,3,1,0:T(1,128)S(1)}, s32[1,1,80,1]{2,3,1,0:T(1,128)}, u32[]{:S(2)}) copy-start(s32[1,1,80,1]{2,3,1,0:T(1,128)} %param.6) | copy-start | bytes 964
  54.4 7.8 %collective-permute-start.9 = (f32[40,128]{1,0:T(8,128)S(1)}, f32[40,128]{1,0:T(8,128)S(1)}, u32[]{:S(2)}, u32[]{:S(2)}) collective-permute-start(f32[40,128]{1,0:T(8,128)S(1)} %get-tuple-element.31), channel_id=1, source_target_pairs={{0,256},{128,384},{256,512},{384,640},{512,768},{640,896},{768,0},... | collective-permute-start | bytes 61448 | tf_op jit(solution)/shard_map/ppermute | solution.py:365
  64.2 38.4 %all-to-all-start = ((f32[64,32,128]{2,1,0:T(8,128)}), f32[64,32,128]{2,1,0:T(8,128)S(1)}, u32[]{:S(2)}, u32[]{:S(2)}) async-start(f32[64,32,128]{2,1,0:T(8,128)} %bitcast.6), calls=%async_computation | async-start | bytes 2097152 | tf_op jit(solution)/shard_map/all_to_all | solution.py:430
  89.1 0.7 copy-start.3

commit v3 on v2

--- a/solution.py
+++ b/solution.py
@@ -112,21 +112,24 @@
     return upper, (x - upper.astype(jnp.float32)).astype(jnp.bfloat16)
 
 
-def share_y_kernel(fields, send, to_low, to_high, cells, matrix, sems):
-    copies = [
-        pltpu.make_async_copy(fields, cells, sems.at[0]),
-        pltpu.make_async_copy(send, matrix, sems.at[1]),
-    ]
+def share_y_kernel(fields, send, maps, to_low, to_high, cells, held, matrix, sems):
+    copies = [pltpu.make_async_copy(send, matrix, sems.at[F]), pltpu.make_async_copy(maps, held, sems.at[F + 1])]
+    for f in range(F):
+        rows = pl.ds(f * 256, 256)
+        copies.append(pltpu.make_async_copy(fields.at[rows], cells.at[rows], sems.at[f]))
     for copy in copies:
         copy.start()
-    for copy in copies:
-        copy.wait()
-    cells_hi, cells_lo = halves(cells[...])
+    copies[0].wait()
     send_hi, send_lo = matrix[:32], matrix[32:]
     dims = ((1,), (1,))
-    shares = dot(send_hi, cells_hi, dims) + dot(send_hi, cells_lo, dims) + dot(send_lo, cells_hi, dims)
-    to_low[...] = shares[:16]
-    to_high[...] = shares[16:]
+    for f in range(F):
+        rows = slice(f * 256, f * 256 + 256)
+        copies[2 + f].wait()
+        cells_hi, cells_lo = halves(cells[rows])
+        shares = dot(send_hi, cells_hi, dims) + dot(send_hi, cells_lo, dims) + dot(send_lo, cells_hi, dims)
+        to_low[:, rows] = shares[:16]
+        to_high[:, rows] = shares[16:]
+    copies[1].wait()
 
 
 def slots_kernel(writers, targets, counts):
@@ -180,19 +183,22 @@
     return near_low, near_high, lanes.pack_third([third[-6], third[-5]]), lanes.pack_third([third[8], third[9], third[10]])
 
 
-def share_z_kernel(
-    fields, maps, from_low, from_high, fine, coarse, to_low, to_high, to_low_far, to_high_far, work
-):
+def own_y_kernel(fields, maps, own):
     cells_hi, cells_lo = halves(fields[...])
     dims = ((1,), (0,))
+    own_hi, own_lo = maps[:128], maps[128:256]
+    own[...] = dot(cells_hi, own_hi, dims) + dot(cells_lo, own_hi, dims) + dot(cells_hi, own_lo, dims)
+
+
+def share_z_kernel(
+    own, maps, from_low, from_high, fine, coarse, to_low, to_high, to_low_far, to_high_far, work
+):
     low_hi, low_lo = halves(from_high[...])
     high_hi, high_lo = halves(from_low[...])
     turned = ((0,), (0,))
-    own_hi, own_lo, place_low, place_high = maps[:128], maps[128:256], maps[256:272], maps[272:]
+    place_low, place_high = maps[256:272], maps[272:]
     work[...] = (
-        dot(cells_hi, own_hi, dims)
-        + dot(cells_lo, own_hi, dims)
-        + dot(cells_hi, own_lo, dims)
+        own[...]
         + dot(low_hi, place_low, turned)
         + dot(low_lo, place_low, turned)
         + dot(high_hi, place_high, turned)
@@ -378,14 +384,15 @@
     maps = jnp.asarray(np.concatenate([*split(own), place.astype(ml_dtypes.bfloat16)]))
     cells = fields.reshape(ROWS, LN)
 
-    to_low, to_high = call(
+    to_low, to_high, cells, maps = call(
         share_y_kernel,
-        [f32(16, ROWS)] * 2,
-        [cells, send],
-        [pltpu.VMEM((ROWS, LN), jnp.float32), pltpu.VMEM((64, LN), jnp.bfloat16), pltpu.SemaphoreType.DMA((2,))],
-        [HB, HB],
-        grant=60 << 20,
-    )
+        [f32(16, ROWS), f32(16, ROWS), f32(ROWS, LN), jax.ShapeDtypeStruct(maps.shape, maps.dtype)],
+        [pltpu.with_memory_space_constraint(a, pltpu.HBM) for a in (cells, send, maps)],
+        [pltpu.VMEM((64, LN), jnp.bfloat16), pltpu.SemaphoreType.DMA((F + 2,))],
+        [HB, HB, HB],
+        grant=32 << 20,
+    )
+    (own,) = call(own_y_kernel, [f32(ROWS, 2 * LN)], [cells, maps], flops=1 << 30)
     from_high = shift(to_low, "gy", -1)
     from_low = shift(to_high, "gy", 1)
 
@@ -401,7 +408,7 @@
     fine, coarse, to_low, to_high, to_low_far, to_high_far = call(
         share_z_kernel,
         [f32(ROWS, LN), f32(ROWS // 2, LN), f32(F, 8, 16, LN), f32(F, 7, 16, LN), f32(F, 16, LN), f32(F, 16, LN)],
-        [cells, maps, from_low, from_high],
+        [own, maps, from_low, from_high],
         [pltpu.VMEM((ROWS, 2 * LN), jnp.float32)],
     )
     from_high = shift(to_low, "gz", -1)

time: 104 us -> 103 us (level)
  local copies, waits for them, and re-layouts: 2.95 us -> 1.35 us
    unnamed x11 -> x7, local copies, waits for them, and re-layouts: 1.73 us -> 0.13 us
    pallas_call x5 -> x6, Pallas kernels: 8.74 us -> 8.82 us  [call(): pl.pallas_call(kernel, out_shape=list(outs), in_specs=specs or [VM] * len...]
  transfers between devices with their start and end apart: 11 -> 11, of which waited for: 5 -> 4; matrix products, arithmetic and copies ran while one was open for 1% -> 1% of each run, Pallas kernels for 1% -> 2%
where the time goes in v3:
time: 103 us; the launch traced here: 102 us
  starting transfers between devices  52.9 us (51%)
  waiting for transfers between devices  23.1 us (22%)
  blocking collectives  14.2 us (14%)
  Pallas kernels  8.82 us (9%)
  local copies, waits for them, and re-layouts  1.35 us (1%)
    ppermute x10, starting transfers between devices, shift(): lax.ppermute(array, axis, [(i, (i + by) % count) for i in range(count)])  42.3 us
    all_gather x1, blocking collectives, body(): band = lax.all_gather(band, 'gz', axis=0, tiled=True)  14.2 us
    all_to_all x1, waiting for transfers between devices, body(): lax.all_to_all(outbox.reshape(64, 32, LN), ('gx', 'gy'), split_axis=0, co...  12.5 us
    ppermute x10, waiting for transfers between devices, shift(): lax.ppermute(array, axis, [(i, (i + by) % count) for i in range(count)])  10.6 us
    all_to_all x1, starting transfers between devices, body(): lax.all_to_all(outbox.reshape(64, 32, LN), ('gx', 'gy'), split_axis=0, co...  10.6 us
    pallas_call x6, Pallas kernels, call(): pl.pallas_call(kernel, out_shape=list(outs), in_specs=specs or [VM] * len...  8.82 us
  transfers between devices with their start and end apart: 11, of which 4 were waited for; matrix products, arithmetic and copies ran while one was open for 1% of the time, Pallas kernels for 2%

profile of v3, /device:TPU:2, one launch (start us, length us, event | category | flops | bytes accessed | tf_op | source)
XLA Modules:
  0.0 102.2 jit_solution(765631505670071553)
XLA Ops:
  0.6 2.2 %shard_map.69 = (f32[16,1280]{1,0:T(8,128)S(1)}, f32[16,1280]{1,0:T(8,128)S(1)}, f32[1280,128]{1,0:T(8,128)S(1)}, bf16[288,256]{1,0:T(8,128)(2,1)S(1)}) custom-call(f32[1280,128]{1,0:T(8,128)} %bitcast.14, bf16[64,128]{1,0:T(8,128)(2,1)} %constant.6.clone.send, bf16[288,256]{1,0:T(8,128)(2,1)} %constant.7.clone.maps), custom_call_target="tpu_custom_call" | custom-call | flops 1048576 | bytes 2097152 | tf_op jit(solution)/shard_map/pallas_call | solution.py:358
  2.8 3.4 %collective-permute-start = (f32[16,1280]{1,0:T(8,128)S(1)}, f32[16,1280]{1,0:T(8,128)S(1)}, u32[]{:S(2)}, u32[]{:S(2)}) collective-permute-start(f32[16,1280]{1,0:T(8,128)S(1)} %get-tuple-element.22), channel_id=1, source_target_pairs={{0,16},{16,32},{32,48},{48,64},{64,80},{80,96},{96,112},{112,0},{1... | collective-permute-start | bytes 245768 | tf_op jit(solution)/shard_map/ppermute | solution.py:371
  6.2 13.6 %collective-permute-start.1 = (f32[16,1280]{1,0:T(8,128)S(1)}, f32[16,1280]{1,0:T(8,128)S(1)}, u32[]{:S(2)}, u32[]{:S(2)}) collective-permute-start(f32[16,1280]{1,0:T(8,128)S(1)} %get-tuple-element.23), channel_id=1, source_target_pairs={{0,112},{16,0},{32,16},{48,32},{64,48},{80,64},{96,80},{112,96},{1... | collective-permute-start | bytes 245768 | tf_op jit(solution)/shard_map/ppermute | solution.py:371
  19.8 0.7 shard_map.70.own
  20.5 0.0 copy-start
  20.5 0.0 collective-permute-done.from_low
  20.5 1.3 %collective-permute-done.1.from_high = f32[16,1280]{1,0:T(8,128)S(1)} collective-permute-done((f32[16,1280]{1,0:T(8,128)S(1)}, f32[16,1280]{1,0:T(8,128)S(1)}, u32[]{:S(2)}, u32[]{:S(2)}) %collective-permute-start.1) | collective-permute-done | bytes 81952 | tf_op jit(solution)/shard_map/ppermute | solution.py:371
  21.9 1.5 %shard_map.71 = (f32[1280,128]{1,0:T(8,128)S(1)}, f32[640,128]{1,0:T(8,128)S(1)}, f32[5,8,16,128]{3,2,1,0:T(8,128)S(1)}, f32[5,7,16,128]{3,2,1,0:T(8,128)S(1)}, ...) custom-call(f32[1280,256]{1,0:T(8,128)S(1)} %shard_map.70.own, bf16[288,256]{1,0:T(8,128)(2,1)S(1)} %get-tuple-element.21.maps, ...), custom_call_target="tpu_custom_call" | custom-call | flops 1048576 | bytes 3448832 | tf_op jit(solution)/shard_map/pallas_call | solution.py:358
  23.4 4.1 %collective-permute-start.2 = (f32[5,8,16,128]{3,2,1,0:T(8,128)S(1)}, f32[5,8,16,128]{3,2,1,0:T(8,128)S(1)}, u32[]{:S(2)}, u32[]{:S(2)}) collective-permute-start(f32[5,8,16,128]{3,2,1,0:T(8,128)S(1)} %get-tuple-element.26), channel_id=1, source_target_pairs={{0,15},{1,0},{2,1},{3,2},{4,3},{5,4},{6,5},{7,6},{8,7},{9,8},{10,9... | collective-permute-start | bytes 983048 | tf_op jit(solution)/shard_map/ppermute | solution.py:371
  27.5 0.0 collective-permute-start.3
  27.5 4.4 %collective-permute-start.4 = (f32[5,16,128]{2,1,0:T(8,128)S(1)}, f32[5,16,128]{2,1,0:T(8,128)S(1)}, u32[]{:S(2)}, u32[]{:S(2)}) collective-permute-start(f32[5,16,128]{2,1,0:T(8,128)S(1)} %get-tuple-element.28), channel_id=1, source_target_pairs={{0,14},{1,15},{2,0},{3,1},{4,2},{5,3},{6,4},{7,5},{8,6},{9,7},{10,... | collective-permute-start | bytes 122888 | tf_op jit(solution)/shard_map/ppermute | solution.py:371
  31.9 1.9 %collective-permute-start.5 = (f32[5,16,128]{2,1,0:T(8,128)S(1)}, f32[5,16,128]{2,1,0:T(8,128)S(1)}, u32[]{:S(2)}, u32[]{:S(2)}) collective-permute-start(f32[5,16,128]{2,1,0:T(8,128)S(1)} %get-tuple-element.29), channel_id=1, source_target_pairs={{0,2},{1,3},{2,4},{3,5},{4,6},{5,7},{6,8},{7,9},{8,10},{9,11},{10,... | collective-permute-start | bytes 122888 | tf_op jit(solution)/shard_map/ppermute | solution.py:371
  33.8 0.0 collective-permute-done.4.from_high_far
  33.8 5.2 %collective-permute-done.5.from_low_far = f32[5,16,128]{2,1,0:T(8,128)S(1)} collective-permute-done((f32[5,16,128]{2,1,0:T(8,128)S(1)}, f32[5,16,128]{2,1,0:T(8,128)S(1)}, u32[]{:S(2)}, u32[]{:S(2)}) %collective-permute-start.5) | collective-permute-done | bytes 40992 | tf_op jit(solution)/shard_map/ppermute | solution.py:371
  39.0 0.0 collective-permute-done.3.from_low
  39.1 0.0 collective-permute-done.2.from_high
  39.1 1.0 shard_map.72
  40.0 6.2 %collective-permute-start.6 = (f32[480,128]{1,0:T(8,128)S(1)}, f32[480,128]{1,0:T(8,128)S(1)}, u32[]{:S(2)}, u32[]{:S(2)}) collective-permute-start(f32[480,128]{1,0:T(8,128)S(1)} %get-tuple-element.32), channel_id=1, source_target_pairs={{0,896},{128,0},{256,128},{384,256},{512,384},{640,512},{768,640},... | collective-permute-start | bytes 737288 | tf_op jit(solution)/shard_map/ppermute | solution.py:371
  46.2 1.9 %collective-permute-start.7 = (f32[400,128]{1,0:T(8,128)S(1)}, f32[400,128]{1,0:T(8,128)S(1)}, u32[]{:S(2)}, u32[]{:S(2)}) collective-permute-start(f32[400,128]{1,0:T(8,128)S(1)} %get-tuple-element.33), channel_id=1, source_target_pairs={{0,128},{128,256},{256,384},{384,512},{512,640},{640,768},{768,896... | collective-permute-start | bytes 614408 | tf_op jit(solution)/shard_map/ppermute | solution.py:371
  48.1 4.6 %collective-permute-start.8 = (f32[40,128]{1,0:T(8,128)S(1)}, f32[40,128]{1,0:T(8,128)S(1)}, u32[]{:S(2)}, u32[]{:S(2)}) collective-permute-start(f32[40,128]{1,0:T(8,128)S(1)} %get-tuple-element.34), channel_id=1, source_target_pairs={{0,768},{128,896},{256,0},{384,128},{512,256},{640,384},{768,512},... | collective-permute-start | bytes 61448 | tf_op jit(solution)/shard_map/ppermute | solution.py:371
  52.7 2.2 %collective-permute-start.9 = (f32[40,128]{1,0:T(8,128)S(1)}, f32[40,128]{1,0:T(8,128)S(1)}, u32[]{:S(2)}, u32[]{:S(2)}) collective-permute-start(f32[40,128]{1,0:T(8,128)S(1)} %get-tuple-element.35), channel_id=1, source_target_pairs={{0,256},{128,384},{256,512},{384,640},{512,768},{640,896},{768,0},... | collective-permute-start | bytes 61448 | tf_op jit(solution)/shard_map/ppermute | solution.py:371
  54.9 0.0 copy-done
  54.9 1.5 %shard_map.68.targets = s32[80]{0:T(128)S(1)} custom-call(s32[80]{0:T(128)S(1)} %bitcast.13), custom_call_target="tpu_custom_call" | custom-call | flops 1073741824 | bytes 640 | tf_op jit(solution)/shard_map/pallas_call | solution.py:358
  56.4 0.0 collective-permute-done.8.from_high_far
  56.5 4.0 %collective-permute-done.9.from_low_far = f32[40,128]{1,0:T(8,128)S(1)} collective-permute-done((f32[40,128]{1,0:T(8,128)S(1)}, f32[40,128]{1,0:T(8,128)S(1)}, u32[]{:S(2)}, u32[]{:S(2)}) %collective-permute-start.9) | collective-permute-done | bytes 20512 | tf_op jit(solution)/shard_map/ppermute | solution.py:371
  60.5 0.0 collective-permute-done.7.from_low
  60.5 0.0 collective-permute-done.6.from_high
  60.5 2.0 %shard_map.73 = (f32[2048,128]{1,0:T(8,128)}, f32[2,40,16]{2,1,0:T(8,128)S(1)}) custom-call(s32[80]{0:T(128)S(1)} %shard_map.68.targets, f32[16,80,128]{2,1,0:T(8,128)S(1)} %get-tuple-element.30.fine, f32[8,40,128]{2,1,0:T(8,128)S(1)} %get-tuple-element.31.coarse, f32[480,128]{1,0:T(8,128)S(1)} %collective-permute-done.6.from_high, ...), custom_call_target="tpu_custom_call" | custom-call | flops 1048576 | bytes 2364736 | tf_op jit(solution)/shard_map/pallas_call | solution.py:358
  62.5 0.0 copy-start.1
  62.5 10.6 %all-to-all-start = ((f32[64,32,128]{2,1,0:T(8,128)}), f32[64,32,128]{2,1,0:T(8,128)S(1)}, u32[]{:S(2)}, u32[]{:S(2)}) async-start(f32[64,32,128]{2,1,0:T(8,128)} %bitcast.6), calls=%async_computation | async-start | bytes 2097152 | tf_op jit(solution)/shard_map/all_to_all | solution.py:437
  73.1 0.1 slice.3
  73.2 0.1 reshape.32
  73.3 14.2 %all-gather = f32[16,2,160]{2,1,0:T(2,128)S(1)} all-gather(f32[1,2,160]{2,1,0:T(2,128)S(1)} %reshape.32), channel_id=1, replica_groups=mesh['gx'=8,'gy'=8,'gz'=16] {'gz'}, dimensions={0}, use_global_device_ids=true | all-gather | bytes 21760 | tf_op jit(solution)/shard_map/all_gather | solution.py:440
  87.6 0.0 copy-done.1
  87.6 1.0 fusion
  88.5 12.5 %all-to-all-done = f32[64,32,128]{2,1,0:T(8,128)S(1)} async-done(((f32[64,32,128]{2,1,0:T(8,128)}), f32[64,32,128]{2,1,0:T(8,128)S(1)}, u32[]{:S(2)}, u32[]{:S(2)}) %all-to-all-start) | async-done | bytes 1048608 | tf_op jit(solution)/shard_map/all_to_all | solution.py:437
  101.0 1.1 %reshape.31 = f32[128,2048]{1,0:T(8,128)} reshape(f32[64,32,128]{2,1,0:T(8,128)S(1)} %all-to-all-done) | data formatting | bytes 2097152 | tf_op jit(solution)/shard_map/reshape | solution.py:444
  (2 shorter events, 0.0 us)
Async XLA Ops:
  2.8 17.7 %collective-permute-start = (f32[16,1280]{1,0:T(8,128)S(1)}, f32[16,1280]{1,0:T(8,128)S(1)}, u32[]{:S(2)}, u32[]{:S(2)}) collective-permute-start(f32[16,1280]{1,0:T(8,128)S(1)} %get-tuple-element.22), channel_id=1, source_target_pairs={{0,16},{16,32},{32,48},{48,64},{64,80},{80,96},{96,112},{112,0},{1... | collective-permute-start | bytes 245768 | tf_op jit(solution)/shard_map/ppermute | solution.py:371
  6.2 15.7 %collective-permute-start.1 = (f32[16,1280]{1,0:T(8,128)S(1)}, f32[16,1280]{1,0:T(8,128)S(1)}, u32[]{:S(2)}, u32[]{:S(2)}) collective-permute-start(f32[16,1280]{1,0:T(8,128)S(1)} %get-tuple-element.23), channel_id=1, source_target_pairs={{0,112},{16,0},{32,16},{48,32},{64,48},{80,64},{96,80},{112,96},{1... | collective-permute-start | bytes 245768 | tf_op jit(solution)/shard_map/ppermute | solution.py:371
  20.5 34.4 %copy-start = (s32[1,1,80,1]{2,3,1,0:T(1,128)S(1)}, s32[1,1,80,1]{2,3,1,0:T(1,128)}, u32[]{:S(2)}) copy-start(s32[1,1,80,1]{2,3,1,0:T(1,128)} %param.6) | copy-start | bytes 964
  23.4 15.7 %collective-permute-start.2 = (f32[5,8,16,128]{3,2,1,0:T(8,128)S(1)}, f32[5,8,16,128]{3,2,1,0:T(8,128)S(1)}, u32[]{:S(2)}, u32[]{:S(2)}) collective-permute-start(f32[5,8,16,128]{3,2,1,0:T(8,128)S(1)} %get-tuple-element.26), channel_id=1, source_target_pairs={{0,15},{1,0},{2,1},{3,2},{4,3},{5,4},{6,5},{7,6},{8,7},{9,8},{10,9... | collective-permute-start | bytes 983048 | tf_op jit(solution)/shard_map/ppermute | solution.py:371
  27.5 11.6 %collective-permute-start.3 = (f32[5,7,16,128]{3,2,1,0:T(8,128)S(1)}, f32[5,7,16,128]{3,2,1,0:T(8,128)S(1)}, u32[]{:S(2)}, u32[]{:S(2)}) collective-permute-start(f32[5,7,16,128]{3,2,1,0:T(8,128)S(1)} %get-tuple-element.27), channel_id=1, source_target_pairs={{0,1},{1,2},{2,3},{3,4},{4,5},{5,6},{6,7},{7,8},{8,9},{9,10},{10,1... | collective-permute-start | bytes 860168 | tf_op jit(solution)/shard_map/ppermute | solution.py:371
  27.5 6.3 %collective-permute-start.4 = (f32[5,16,128]{2,1,0:T(8,128)S(1)}, f32[5,16,128]{2,1,0:T(8,128)S(1)}, u32[]{:S(2)}, u32[]{:S(2)}) collective-permute-start(f32[5,16,128]{2,1,0:T(8,128)S(1)} %get-tuple-element.28), channel_id=1, source_target_pairs={{0,14},{1,15},{2,0},{3,1},{4,2},{5,3},{6,4},{7,5},{8,6},{9,7},{10,... | collective-permute-start | bytes 122888 | tf_op jit(solution)/shard_map/ppermute | solution.py:371
  31.9 7.1 %collective-permute-start.5 = (f32[5,16,128]{2,1,0:T(8,128)S(1)}, f32[5,16,128]{2,1,0:T(8,128)S(1)}, u32[]{:S(2)}, u32[]{:S(2)}) collective-permute-start(f32[5,16,128]{2,1,0:T(8,128)S(1)} %get-tuple-element.29), channel_id=1, source_target_pairs={{0,2},{1,3},{2,4},{3,5},{4,6},{5,7},{6,8},{7,9},{8,10},{9,11},{10,... | collective-permute-start | bytes 122888 | tf_op jit(solution)/shard_map/ppermute | solution.py:371
  40.0 20.5 %collective-permute-start.6 = (f32[480,128]{1,0:T(8,128)S(1)}, f32[480,128]{1,0:T(8,128)S(1)}, u32[]{:S(2)}, u32[]{:S(2)}) collective-permute-start(f32[480,128]{1,0:T(8,128)S(1)} %get-tuple-element.32), channel_id=1, source_target_pairs={{0,896},{128,0},{256,128},{384,256},{512,384},{640,512},{768,640},... | collective-permute-start | bytes 737288 | tf_op jit(solution)/shard_map/ppermute | solution.py:371
  46.2 14.3 %collective-permute-start.7 = (f32[400,128]{1,0:T(8,128)S(1)}, f32[400,128]{1,0:T(8,128)S(1)}, u32[]{:S(2)}, u32[]{:S(2)}) collective-permute-start(f32[400,128]{1,0:T(8,128)S(1)} %get-tuple-element.33), channel_id=1, source_target_pairs={{0,128},{128,256},{256,384},{384,512},{512,640},{640,768},{768,896... | collective-permute-start | bytes 614408 | tf_op jit(solution)/shard_map/ppermute | solution.py:371
  48.1 8.3 %collective-permute-start.8 = (f32[40,128]{1,0:T(8,128)S(1)}, f32[40,128]{1,0:T(8,128)S(1)}, u32[]{:S(2)}, u32[]{:S(2)}) collective-permute-start(f32[40,128]{1,0:T(8,128)S(1)} %get-tuple-element.34), channel_id=1, source_target_pairs={{0,768},{128,896},{256,0},{384,128},{512,256},{640,384},{768,512},... | collective-permute-start | bytes 61448 | tf_op jit(solution)/shard_map/ppermute | solution.py:371
  52.7 7.8 %collective-permute-start.9 = (f32[40,128]{1,0:T(8,128)S(1)}, f32[40,128]{1,0:T(8,128)S(1)}, u32[]{:S(2)}, u32[]{:S(2)}) collective-permute-start(f32[40,128]{1,0:T(8,128)S(1)} %get-tuple-element.35), channel_id=1, source_target_pairs={{0,256},{128,384},{256,512},{384,640},{512,768},{640,896},{768,0},... | collective-permute-start | bytes 61448 | tf_op jit(solution)/shard_map/ppermute | solution.py:371
  62.5 25.1 %copy-start.1 = (f32[32,32]{1,0:T(8,128)S(1)}, f32[32,32]{1,0:T(8,128)}, u32[]{:S(2)}) copy-start(f32[32,32]{1,0:T(8,128)} %constant.8.clone) | copy-start | bytes 12292
  62.5 38.5 %all-to-all-start = ((f32[64,32,128]{2,1,0:T(8,128)}), f32[64,32,128]{2,1,0:T(8,128)S(1)}, u32[]{:S(2)}, u32[]{:S(2)}) async-start(f32[64,32,128]{2,1,0:T(8,128)} %bitcast.6), calls=%async_computation | async-start | bytes 2097152 | tf_op jit(solution)/shard_map/all_to_all | solution.py:437

commit v4 on v3

--- a/solution.py
+++ b/solution.py
@@ -132,16 +132,6 @@
     copies[1].wait()
 
 
-def slots_kernel(writers, targets, counts):
-    for i in range(64):
-        counts[i] = 0
-    for t in range(TILES):
-        writer = writers[t]
-        slot = counts[writer]
-        counts[writer] = slot + 1
-        targets[t] = writer * 2 + slot
-
-
 def fine_shares(values):
     return lift(values)
 
@@ -247,16 +237,30 @@
     return rows
 
 
-def share_x_kernel(
-    fine, coarse, from_high, from_low, from_high_far, from_low_far,
-    own_fine, own_coarse, to_low, to_high, to_low_far, to_high_far, work, work_coarse,
-):
-    lanes = Lanes()
+def fine_x_kernel(fine, from_high, from_low, own_fine, to_low, to_high, work):
     for f in range(F):
         at = f * 256
         work[at : at + 48] = fine[at : at + 48] + from_low[f, :3].reshape(48, LN)
         work[at + 48 : at + 192] = fine[at + 48 : at + 192]
         work[at + 192 : at + 256] = fine[at + 192 : at + 256] + from_high[f, :4].reshape(64, LN)
+    for g in range(10):
+        rows = slice(g * 8, g * 8 + 8)
+        done = fine_shares({x: work[pl.ds(g * 128 + x, 8, stride=16), :] for x in range(NB)})
+        for x in range(NB):
+            own_fine[x, rows] = done[x]
+        for i in range(4):
+            to_low[i * 80 + g * 8 : i * 80 + g * 8 + 8] = done[i - 4]
+        for i in range(3):
+            to_high[i * 80 + g * 8 : i * 80 + g * 8 + 8] = done[16 + i]
+
+
+def coarse_x_kernel(
+    coarse, from_high, from_low, from_high_far, from_low_far, held_low, held_high,
+    own_coarse, to_low, to_high, to_low_far, to_high_far, work_coarse,
+):
+    del held_low, held_high
+    lanes = Lanes()
+    for f in range(F):
         for half in (0, 8):
             rows = slice(half, half + 8)
             at = [f * 128 + z * 16 + half for z in range(8)]
@@ -270,15 +274,6 @@
             )
             for z in range(8):
                 work_coarse[at[z] : at[z] + 8] = added[z]
-    for g in range(10):
-        rows = slice(g * 8, g * 8 + 8)
-        done = fine_shares({x: work[pl.ds(g * 128 + x, 8, stride=16), :] for x in range(NB)})
-        for x in range(NB):
-            own_fine[x, rows] = done[x]
-        for i in range(4):
-            to_low[i * 80 + g * 8 : i * 80 + g * 8 + 8] = done[i - 4]
-        for i in range(3):
-            to_high[i * 80 + g * 8 : i * 80 + g * 8 + 8] = done[16 + i]
     for g in range(5):
         rows = slice(g * 8, g * 8 + 8)
         second, third = coarse_shares({x: work_coarse[pl.ds(g * 128 + x, 8, stride=16), :] for x in range(NB)})
@@ -292,14 +287,33 @@
         to_high_far[rows] = far_high
 
 
+def tiles_kernel(writers, fine, from_high, from_low, targets, tiles, counts):
+    for i in range(64):
+        counts[i] = 0
+    for t in range(TILES):
+        writer = writers[t]
+        slot = counts[writer]
+        counts[writer] = slot + 1
+        targets[t] = writer * 2 + slot
+    for g in range(10):
+        rows = slice(g * 8, g * 8 + 8)
+        for x in range(NB):
+            row = fine[x, rows]
+            if x < 3:
+                row = row + from_low[x * 80 + g * 8 : x * 80 + g * 8 + 8]
+            if x >= 12:
+                i = x - 12
+                row = row + from_high[i * 80 + g * 8 : i * 80 + g * 8 + 8]
+            tiles[pl.ds(g * 128 + x, 8, stride=16), :] = row
+
+
 def route_kernel(
-    targets, fine, coarse, from_high, from_low, from_high_far, from_low_far, outbox, low_band, tiles, spread
+    targets, tiles, coarse, from_high, from_low, from_high_far, from_low_far, outbox, low_band, spread
 ):
     shape = (8, LN)
     lanes = Lanes()
-    lane = lanes.lane
     even_row = lax.broadcasted_iota(jnp.int32, shape, 0) % 2 == 0
-    replaced = (lane % 4 == 0) & even_row
+    replaced = (lanes.lane % 4 == 0) & even_row
     merged = lanes.second & even_row
     picked = (LN, 16)
     pick = lax.broadcasted_iota(jnp.int32, picked, 0) == 8 * lax.broadcasted_iota(jnp.int32, picked, 1) + 1
@@ -324,24 +338,17 @@
             row = added[x]
             if x % 2 == 0:
                 row = jnp.where(replaced, lanes.roll(row, -1), row)
-            spread[pl.ds(x * 80 + g * 16, 8, stride=2), :] = row
-            spread[pl.ds(x * 80 + g * 16 + 1, 8, stride=2), :] = row
-    for g in range(10):
-        rows = slice(g * 8, g * 8 + 8)
-        for x in range(NB):
-            row = fine[x, rows]
-            if x < 3:
-                row = row + from_low[x * 80 + g * 8 : x * 80 + g * 8 + 8]
-            if x >= 12:
-                i = x - 12
-                row = row + from_high[i * 80 + g * 8 : i * 80 + g * 8 + 8]
-            if x % 2 == 0:
-                row = jnp.where(merged, spread[x // 2 * 80 + g * 8 : x // 2 * 80 + g * 8 + 8], row)
-            tiles[pl.ds(g * 128 + x, 8, stride=16), :] = row
-
+            for odd in range(2):
+                spread[pl.ds(g * 128 + 2 * x + odd, 8, stride=16), :] = row
     for t in range(TILES):
         to = pl.multiple_of(targets[t] * 16, 16)
-        outbox[pl.ds(to, 16), :] = tiles[t * 16 : t * 16 + 16]
+        f, z = t // NB, t % NB
+        for half in (0, 8):
+            row = tiles[t * 16 + half : t * 16 + half + 8]
+            if z % 2 == 0:
+                at = (f * 8 + z // 2) * 16 + half
+                row = jnp.where(merged, spread[at : at + 8], row)
+            outbox[pl.ds(to + half, 8), :] = row
 
 
 VM = pl.BlockSpec(memory_space=pltpu.VMEM)
@@ -353,7 +360,7 @@
     return jax.ShapeDtypeStruct(shape, jnp.float32)
 
 
-def call(kernel, outs, ins, scratch=(), specs=None, out_specs=None, flops=1 << 20, grant=32 << 20):
+def call(kernel, outs, ins, scratch=(), specs=None, out_specs=None, flops=1 << 20, grant=32 << 20, aliases=None):
     moved = sum(4 * int(np.prod(a.shape)) for a in list(outs) + list(ins))
     return pl.pallas_call(
         kernel,
@@ -361,6 +368,7 @@
         in_specs=specs or [VM] * len(ins),
         out_specs=out_specs or [VM] * len(outs),
         scratch_shapes=list(scratch),
+        input_output_aliases=aliases or {},
         compiler_params=pltpu.CompilerParams(vmem_limit_bytes=grant),
         cost_estimate=pl.CostEstimate(flops=flops, bytes_accessed=moved, transcendentals=0),
     )(*ins)
@@ -396,15 +404,6 @@
     from_high = shift(to_low, "gy", -1)
     from_low = shift(to_high, "gy", 1)
 
-    (targets,) = call(
-        slots_kernel,
-        [jax.ShapeDtypeStruct((TILES,), jnp.int32)],
-        [tile_writer.reshape(TILES)],
-        [pltpu.SMEM((64,), jnp.int32)],
-        [SM],
-        [SM],
-        flops=1 << 30,
-    )
     fine, coarse, to_low, to_high, to_low_far, to_high_far = call(
         share_z_kernel,
         [f32(ROWS, LN), f32(ROWS // 2, LN), f32(F, 8, 16, LN), f32(F, 7, 16, LN), f32(F, 16, LN), f32(F, 16, LN)],
@@ -416,22 +415,39 @@
     from_high_far = shift(to_low_far, "gz", -2)
     from_low_far = shift(to_high_far, "gz", 2)
 
-    fine, coarse, to_low, to_high, to_low_far, to_high_far = call(
-        share_x_kernel,
-        [f32(16, 80, LN), f32(8, 40, LN), f32(480, LN), f32(400, LN), f32(40, LN), f32(40, LN)],
-        [fine, coarse, from_high, from_low, from_high_far, from_low_far],
-        [pltpu.VMEM((ROWS, LN), jnp.float32), pltpu.VMEM((ROWS // 2, LN), jnp.float32)],
+    fine, to_low, to_high = call(
+        fine_x_kernel,
+        [f32(16, 80, LN), f32(480, LN), f32(400, LN)],
+        [fine, from_high, from_low],
+        [pltpu.VMEM((ROWS, LN), jnp.float32)],
+        flops=1 << 30,
+    )
+    coarse, to_low, to_high, to_low_far, to_high_far = call(
+        coarse_x_kernel,
+        [f32(8, 40, LN), f32(480, LN), f32(400, LN), f32(40, LN), f32(40, LN)],
+        [coarse, from_high, from_low, from_high_far, from_low_far, to_low, to_high],
+        [pltpu.VMEM((ROWS // 2, LN), jnp.float32)],
+        aliases={5: 1, 6: 2},
     )
     from_high = shift(to_low, "gx", -1)
     from_low = shift(to_high, "gx", 1)
     from_high_far = shift(to_low_far, "gx", -2)
     from_low_far = shift(to_high_far, "gx", 2)
 
+    targets, tiles = call(
+        tiles_kernel,
+        [jax.ShapeDtypeStruct((TILES,), jnp.int32), f32(ROWS, LN)],
+        [tile_writer.reshape(TILES), fine, from_high, from_low],
+        [pltpu.SMEM((64,), jnp.int32)],
+        [SM, VM, VM, VM],
+        [SM, VM],
+        flops=1 << 30,
+    )
     outbox, low_band = call(
         route_kernel,
         [f32(2048, LN), f32(2, 40, 16)],
-        [targets, fine, coarse, from_high, from_low, from_high_far, from_low_far],
-        [pltpu.VMEM((ROWS, LN), jnp.float32), pltpu.VMEM((640, LN), jnp.float32)],
+        [targets, tiles, coarse, from_high, from_low, from_high_far, from_low_far],
+        [pltpu.VMEM((640, LN), jnp.float32)],
         [SM] + [VM] * 6,
     )
     inbox = lax.all_to_all(outbox.reshape(64, 32, LN), ("gx", "gy"), split_axis=0, concat_axis=0, tiled=True)

time: 103 us -> 102 us (level)
    pallas_call x6 -> x7, Pallas kernels: 8.82 us -> 8.85 us  [call(): pl.pallas_call(kernel, out_shape=list(outs), in_specs=specs or [VM] * len...]
  transfers between devices with their start and end apart: 11 -> 11, of which waited for: 4 -> 6; matrix products, arithmetic and copies ran while one was open for 1% -> 1% of each run, Pallas kernels for 2% -> 3%
where the time goes in v4:
time: 102 us
  starting transfers between devices  52.9 us (52%)
  waiting for transfers between devices  22.5 us (22%)
  blocking collectives  14.2 us (14%)
  Pallas kernels  8.85 us (9%)
  local copies, waits for them, and re-layouts  1.35 us (1%)
    ppermute x10, starting transfers between devices, shift(): lax.ppermute(array, axis, [(i, (i + by) % count) for i in range(count)])  42.3 us
    all_gather x1, blocking collectives, body(): band = lax.all_gather(band, 'gz', axis=0, tiled=True)  14.2 us
    all_to_all x1, waiting for transfers between devices, body(): lax.all_to_all(outbox.reshape(64, 32, LN), ('gx', 'gy'), split_axis=0, co...  12.5 us
    all_to_all x1, starting transfers between devices, body(): lax.all_to_all(outbox.reshape(64, 32, LN), ('gx', 'gy'), split_axis=0, co...  10.6 us
    ppermute x10, waiting for transfers between devices, shift(): lax.ppermute(array, axis, [(i, (i + by) % count) for i in range(count)])  10 us
    pallas_call x7, Pallas kernels, call(): pl.pallas_call(kernel, out_shape=list(outs), in_specs=specs or [VM] * len...  8.85 us
  transfers between devices with their start and end apart: 11, of which 6 were waited for; matrix products, arithmetic and copies ran while one was open for 1% of the time, Pallas kernels for 3%

profile of v4, /device:TPU:2, one launch (start us, length us, event | category | flops | bytes accessed | tf_op | source)
XLA Modules:
  0.0 101.6 jit_solution(17598808203942030582)
XLA Ops:
  0.6 2.2 %shard_map.68 = (f32[16,1280]{1,0:T(8,128)S(1)}, f32[16,1280]{1,0:T(8,128)S(1)}, f32[1280,128]{1,0:T(8,128)S(1)}, bf16[288,256]{1,0:T(8,128)(2,1)S(1)}) custom-call(f32[1280,128]{1,0:T(8,128)} %bitcast.14, bf16[64,128]{1,0:T(8,128)(2,1)} %constant.6.clone.send, bf16[288,256]{1,0:T(8,128)(2,1)} %constant.7.clone.maps), custom_call_target="tpu_custom_call" | custom-call | flops 1048576 | bytes 2097152 | tf_op jit(solution)/shard_map/pallas_call | solution.py:365
  2.8 3.4 %collective-permute-start = (f32[16,1280]{1,0:T(8,128)S(1)}, f32[16,1280]{1,0:T(8,128)S(1)}, u32[]{:S(2)}, u32[]{:S(2)}) collective-permute-start(f32[16,1280]{1,0:T(8,128)S(1)} %get-tuple-element.26), channel_id=1, source_target_pairs={{0,16},{16,32},{32,48},{48,64},{64,80},{80,96},{96,112},{112,0},{1... | collective-permute-start | bytes 245768 | tf_op jit(solution)/shard_map/ppermute | solution.py:379
  6.2 13.6 %collective-permute-start.1 = (f32[16,1280]{1,0:T(8,128)S(1)}, f32[16,1280]{1,0:T(8,128)S(1)}, u32[]{:S(2)}, u32[]{:S(2)}) collective-permute-start(f32[16,1280]{1,0:T(8,128)S(1)} %get-tuple-element.27), channel_id=1, source_target_pairs={{0,112},{16,0},{32,16},{48,32},{64,48},{80,64},{96,80},{112,96},{1... | collective-permute-start | bytes 245768 | tf_op jit(solution)/shard_map/ppermute | solution.py:379
  19.8 0.7 shard_map.69.own
  20.5 0.0 collective-permute-done.from_low
  20.5 1.4 %collective-permute-done.1.from_high = f32[16,1280]{1,0:T(8,128)S(1)} collective-permute-done((f32[16,1280]{1,0:T(8,128)S(1)}, f32[16,1280]{1,0:T(8,128)S(1)}, u32[]{:S(2)}, u32[]{:S(2)}) %collective-permute-start.1) | collective-permute-done | bytes 81952 | tf_op jit(solution)/shard_map/ppermute | solution.py:379
  21.9 1.5 %shard_map.70 = (f32[1280,128]{1,0:T(8,128)S(1)}, f32[640,128]{1,0:T(8,128)S(1)}, f32[5,8,16,128]{3,2,1,0:T(8,128)S(1)}, f32[5,7,16,128]{3,2,1,0:T(8,128)S(1)}, ...) custom-call(f32[1280,256]{1,0:T(8,128)S(1)} %shard_map.69.own, bf16[288,256]{1,0:T(8,128)(2,1)S(1)} %get-tuple-element.25.maps, ...), custom_call_target="tpu_custom_call" | custom-call | flops 1048576 | bytes 3448832 | tf_op jit(solution)/shard_map/pallas_call | solution.py:365
  23.4 4.1 %collective-permute-start.2 = (f32[5,8,16,128]{3,2,1,0:T(8,128)S(1)}, f32[5,8,16,128]{3,2,1,0:T(8,128)S(1)}, u32[]{:S(2)}, u32[]{:S(2)}) collective-permute-start(f32[5,8,16,128]{3,2,1,0:T(8,128)S(1)} %get-tuple-element.29), channel_id=1, source_target_pairs={{0,15},{1,0},{2,1},{3,2},{4,3},{5,4},{6,5},{7,6},{8,7},{9,8},{10,9... | collective-permute-start | bytes 983048 | tf_op jit(solution)/shard_map/ppermute | solution.py:379
  27.5 0.0 collective-permute-start.3
  27.5 4.4 %collective-permute-start.4 = (f32[5,16,128]{2,1,0:T(8,128)S(1)}, f32[5,16,128]{2,1,0:T(8,128)S(1)}, u32[]{:S(2)}, u32[]{:S(2)}) collective-permute-start(f32[5,16,128]{2,1,0:T(8,128)S(1)} %get-tuple-element.33), channel_id=1, source_target_pairs={{0,14},{1,15},{2,0},{3,1},{4,2},{5,3},{6,4},{7,5},{8,6},{9,7},{10,... | collective-permute-start | bytes 122888 | tf_op jit(solution)/shard_map/ppermute | solution.py:379
  31.9 1.9 %collective-permute-start.5 = (f32[5,16,128]{2,1,0:T(8,128)S(1)}, f32[5,16,128]{2,1,0:T(8,128)S(1)}, u32[]{:S(2)}, u32[]{:S(2)}) collective-permute-start(f32[5,16,128]{2,1,0:T(8,128)S(1)} %get-tuple-element.34), channel_id=1, source_target_pairs={{0,2},{1,3},{2,4},{3,5},{4,6},{5,7},{6,8},{7,9},{8,10},{9,11},{10,... | collective-permute-start | bytes 122888 | tf_op jit(solution)/shard_map/ppermute | solution.py:379
  33.8 0.9 collective-permute-done.3.from_low
  34.8 0.0 collective-permute-done.2.from_high
  34.8 0.4 shard_map.71
  35.2 0.0 copy-start
  35.2 0.0 collective-permute-done.4.from_high_far
  35.2 3.8 %collective-permute-done.5.from_low_far = f32[5,16,128]{2,1,0:T(8,128)S(1)} collective-permute-done((f32[5,16,128]{2,1,0:T(8,128)S(1)}, f32[5,16,128]{2,1,0:T(8,128)S(1)}, u32[]{:S(2)}, u32[]{:S(2)}) %collective-permute-start.5) | collective-permute-done | bytes 40992 | tf_op jit(solution)/shard_map/ppermute | solution.py:379
  39.0 0.5 shard_map.72
  39.6 6.2 %collective-permute-start.6 = (f32[480,128]{1,0:T(8,128)S(1)}, f32[480,128]{1,0:T(8,128)S(1)}, u32[]{:S(2)}, u32[]{:S(2)}) collective-permute-start(f32[480,128]{1,0:T(8,128)S(1)} %get-tuple-element.37), channel_id=1, source_target_pairs={{0,896},{128,0},{256,128},{384,256},{512,384},{640,512},{768,640},... | collective-permute-start | bytes 737288 | tf_op jit(solution)/shard_map/ppermute | solution.py:379
  45.8 1.9 %collective-permute-start.7 = (f32[400,128]{1,0:T(8,128)S(1)}, f32[400,128]{1,0:T(8,128)S(1)}, u32[]{:S(2)}, u32[]{:S(2)}) collective-permute-start(f32[400,128]{1,0:T(8,128)S(1)} %get-tuple-element.38), channel_id=1, source_target_pairs={{0,128},{128,256},{256,384},{384,512},{512,640},{640,768},{768,896... | collective-permute-start | bytes 614408 | tf_op jit(solution)/shard_map/ppermute | solution.py:379
  47.7 4.6 %collective-permute-start.8 = (f32[40,128]{1,0:T(8,128)S(1)}, f32[40,128]{1,0:T(8,128)S(1)}, u32[]{:S(2)}, u32[]{:S(2)}) collective-permute-start(f32[40,128]{1,0:T(8,128)S(1)} %get-tuple-element.42), channel_id=1, source_target_pairs={{0,768},{128,896},{256,0},{384,128},{512,256},{640,384},{768,512},... | collective-permute-start | bytes 61448 | tf_op jit(solution)/shard_map/ppermute | solution.py:379
  52.3 2.2 %collective-permute-start.9 = (f32[40,128]{1,0:T(8,128)S(1)}, f32[40,128]{1,0:T(8,128)S(1)}, u32[]{:S(2)}, u32[]{:S(2)}) collective-permute-start(f32[40,128]{1,0:T(8,128)S(1)} %get-tuple-element.43), channel_id=1, source_target_pairs={{0,256},{128,384},{256,512},{384,640},{512,768},{640,896},{768,0},... | collective-permute-start | bytes 61448 | tf_op jit(solution)/shard_map/ppermute | solution.py:379
  54.4 0.9 collective-permute-done.7.from_low
  55.4 0.0 collective-permute-done.6.from_high
  55.4 0.0 copy-done
  55.4 1.7 %shard_map.73 = (s32[80]{0:T(128)S(1)}, f32[1280,128]{1,0:T(8,128)S(1)}) custom-call(s32[80]{0:T(128)S(1)} %bitcast.13, f32[16,80,128]{2,1,0:T(8,128)S(1)} %get-tuple-element.31.fine, f32[480,128]{1,0:T(8,128)S(1)} %collective-permute-done.6.from_high, f32[400,128]{1,0:T(8,128)S(1)} %collective-permute-done.7.from_low), custom_call_target="tpu_custom_call" | custom-call | flops 1073741824 | bytes 1761920 | tf_op jit(solution)/shard_map/pallas_call | solution.py:365
  57.1 0.0 collective-permute-done.8.from_high_far
  57.1 3.0 %collective-permute-done.9.from_low_far = f32[40,128]{1,0:T(8,128)S(1)} collective-permute-done((f32[40,128]{1,0:T(8,128)S(1)}, f32[40,128]{1,0:T(8,128)S(1)}, u32[]{:S(2)}, u32[]{:S(2)}) %collective-permute-start.9) | collective-permute-done | bytes 20512 | tf_op jit(solution)/shard_map/ppermute | solution.py:379
  60.1 1.9 %shard_map.74 = (f32[2048,128]{1,0:T(8,128)}, f32[2,40,16]{2,1,0:T(8,128)S(1)}) custom-call(s32[80]{0:T(128)S(1)} %get-tuple-element.39.targets, f32[1280,128]{1,0:T(8,128)S(1)} %get-tuple-element.40.tiles, f32[8,40,128]{2,1,0:T(8,128)S(1)} %get-tuple-element.41.coarse, f32[480,128]{1,0:T(8,128)S(1)} %collective-permute-done.6.from_high, ...), custom_call_target="tpu_custom_call" | custom-call | flops 1048576 | bytes 2364736 | tf_op jit(solution)/shard_map/pallas_call | solution.py:365
  61.9 0.0 copy-start.1
  61.9 10.6 %all-to-all-start = ((f32[64,32,128]{2,1,0:T(8,128)}), f32[64,32,128]{2,1,0:T(8,128)S(1)}, u32[]{:S(2)}, u32[]{:S(2)}) async-start(f32[64,32,128]{2,1,0:T(8,128)} %bitcast.6), calls=%async_computation | async-start | bytes 2097152 | tf_op jit(solution)/shard_map/all_to_all | solution.py:453
  72.5 0.1 slice.3
  72.6 0.1 reshape.32
  72.7 14.2 %all-gather = f32[16,2,160]{2,1,0:T(2,128)S(1)} all-gather(f32[1,2,160]{2,1,0:T(2,128)S(1)} %reshape.32), channel_id=1, replica_groups=mesh['gx'=8,'gy'=8,'gz'=16] {'gz'}, dimensions={0}, use_global_device_ids=true | all-gather | bytes 21760 | tf_op jit(solution)/shard_map/all_gather | solution.py:456
  87.0 0.0 copy-done.1
  87.0 1.0 fusion
  88.0 12.5 %all-to-all-done = f32[64,32,128]{2,1,0:T(8,128)S(1)} async-done(((f32[64,32,128]{2,1,0:T(8,128)}), f32[64,32,128]{2,1,0:T(8,128)S(1)}, u32[]{:S(2)}, u32[]{:S(2)}) %all-to-all-start) | async-done | bytes 1048608 | tf_op jit(solution)/shard_map/all_to_all | solution.py:453
  100.5 1.1 %reshape.31 = f32[128,2048]{1,0:T(8,128)} reshape(f32[64,32,128]{2,1,0:T(8,128)S(1)} %all-to-all-done) | data formatting | bytes 2097152 | tf_op jit(solution)/shard_map/reshape | solution.py:460
  (2 shorter events, 0.0 us)
Async XLA Ops:
  2.8 17.7 %collective-permute-start = (f32[16,1280]{1,0:T(8,128)S(1)}, f32[16,1280]{1,0:T(8,128)S(1)}, u32[]{:S(2)}, u32[]{:S(2)}) collective-permute-start(f32[16,1280]{1,0:T(8,128)S(1)} %get-tuple-element.26), channel_id=1, source_target_pairs={{0,16},{16,32},{32,48},{48,64},{64,80},{80,96},{96,112},{112,0},{1... | collective-permute-start | bytes 245768 | tf_op jit(solution)/shard_map/ppermute | solution.py:379
  6.2 15.7 %collective-permute-start.1 = (f32[16,1280]{1,0:T(8,128)S(1)}, f32[16,1280]{1,0:T(8,128)S(1)}, u32[]{:S(2)}, u32[]{:S(2)}) collective-permute-start(f32[16,1280]{1,0:T(8,128)S(1)} %get-tuple-element.27), channel_id=1, source_target_pairs={{0,112},{16,0},{32,16},{48,32},{64,48},{80,64},{96,80},{112,96},{1... | collective-permute-start | bytes 245768 | tf_op jit(solution)/shard_map/ppermute | solution.py:379
  23.4 11.4 %collective-permute-start.2 = (f32[5,8,16,128]{3,2,1,0:T(8,128)S(1)}, f32[5,8,16,128]{3,2,1,0:T(8,128)S(1)}, u32[]{:S(2)}, u32[]{:S(2)}) collective-permute-start(f32[5,8,16,128]{3,2,1,0:T(8,128)S(1)} %get-tuple-element.29), channel_id=1, source_target_pairs={{0,15},{1,0},{2,1},{3,2},{4,3},{5,4},{6,5},{7,6},{8,7},{9,8},{10,9... | collective-permute-start | bytes 983048 | tf_op jit(solution)/shard_map/ppermute | solution.py:379
  27.5 7.3 %collective-permute-start.3 = (f32[5,7,16,128]{3,2,1,0:T(8,128)S(1)}, f32[5,7,16,128]{3,2,1,0:T(8,128)S(1)}, u32[]{:S(2)}, u32[]{:S(2)}) collective-permute-start(f32[5,7,16,128]{3,2,1,0:T(8,128)S(1)} %get-tuple-element.30), channel_id=1, source_target_pairs={{0,1},{1,2},{2,3},{3,4},{4,5},{5,6},{6,7},{7,8},{8,9},{9,10},{10,1... | collective-permute-start | bytes 860168 | tf_op jit(solution)/shard_map/ppermute | solution.py:379
  27.5 7.7 %collective-permute-start.4 = (f32[5,16,128]{2,1,0:T(8,128)S(1)}, f32[5,16,128]{2,1,0:T(8,128)S(1)}, u32[]{:S(2)}, u32[]{:S(2)}) collective-permute-start(f32[5,16,128]{2,1,0:T(8,128)S(1)} %get-tuple-element.33), channel_id=1, source_target_pairs={{0,14},{1,15},{2,0},{3,1},{4,2},{5,3},{6,4},{7,5},{8,6},{9,7},{10,... | collective-permute-start | bytes 122888 | tf_op jit(solution)/shard_map/ppermute | solution.py:379
  31.9 7.1 %collective-permute-start.5 = (f32[5,16,128]{2,1,0:T(8,128)S(1)}, f32[5,16,128]{2,1,0:T(8,128)S(1)}, u32[]{:S(2)}, u32[]{:S(2)}) collective-permute-start(f32[5,16,128]{2,1,0:T(8,128)S(1)} %get-tuple-element.34), channel_id=1, source_target_pairs={{0,2},{1,3},{2,4},{3,5},{4,6},{5,7},{6,8},{7,9},{8,10},{9,11},{10,... | collective-permute-start | bytes 122888 | tf_op jit(solution)/shard_map/ppermute | solution.py:379
  35.2 20.2 %copy-start = (s32[1,1,80,1]{2,3,1,0:T(1,128)S(1)}, s32[1,1,80,1]{2,3,1,0:T(1,128)}, u32[]{:S(2)}) copy-start(s32[1,1,80,1]{2,3,1,0:T(1,128)} %param.6) | copy-start | bytes 964
  39.6 15.8 %collective-permute-start.6 = (f32[480,128]{1,0:T(8,128)S(1)}, f32[480,128]{1,0:T(8,128)S(1)}, u32[]{:S(2)}, u32[]{:S(2)}) collective-permute-start(f32[480,128]{1,0:T(8,128)S(1)} %get-tuple-element.37), channel_id=1, source_target_pairs={{0,896},{128,0},{256,128},{384,256},{512,384},{640,512},{768,640},... | collective-permute-start | bytes 737288 | tf_op jit(solution)/shard_map/ppermute | solution.py:379
  45.8 9.6 %collective-permute-start.7 = (f32[400,128]{1,0:T(8,128)S(1)}, f32[400,128]{1,0:T(8,128)S(1)}, u32[]{:S(2)}, u32[]{:S(2)}) collective-permute-start(f32[400,128]{1,0:T(8,128)S(1)} %get-tuple-element.38), channel_id=1, source_target_pairs={{0,128},{128,256},{256,384},{384,512},{512,640},{640,768},{768,896... | collective-permute-start | bytes 614408 | tf_op jit(solution)/shard_map/ppermute | solution.py:379
  47.7 9.4 %collective-permute-start.8 = (f32[40,128]{1,0:T(8,128)S(1)}, f32[40,128]{1,0:T(8,128)S(1)}, u32[]{:S(2)}, u32[]{:S(2)}) collective-permute-start(f32[40,128]{1,0:T(8,128)S(1)} %get-tuple-element.42), channel_id=1, source_target_pairs={{0,768},{128,896},{256,0},{384,128},{512,256},{640,384},{768,512},... | collective-permute-start | bytes 61448 | tf_op jit(solution)/shard_map/ppermute | solution.py:379
  52.3 7.8 %collective-permute-start.9 = (f32[40,128]{1,0:T(8,128)S(1)}, f32[40,128]{1,0:T(8,128)S(1)}, u32[]{:S(2)}, u32[]{:S(2)}) collective-permute-start(f32[40,128]{1,0:T(8,128)S(1)} %get-tuple-element.43), channel_id=1, source_target_pairs={{0,256},{128,384},{256,512},{384,640},{512,768},{640,896},{768,0},... | collective-permute-start | bytes 61448 | tf_op jit(solution)/shard_map/ppermute | solution.py:379
  61.9 25.1 %copy-start.1 = (f32[32,32]{1,0:T(8,128)S(1)}, f32[32,32]{1,0:T(8,128)}, u32[]{:S(2)}) copy-start(f32[32,32]{1,0:T(8,128)} %constant.8.clone) | copy-start | bytes 12292
  61.9 38.5 %all-to-all-start = ((f32[64,32,128]{2,1,0:T(8,128)}), f32[64,32,128]{2,1,0:T(8,128)S(1)}, u32[]{:S(2)}, u32[]{:S(2)}) async-start(f32[64,32,128]{2,1,0:T(8,128)} %bitcast.6), calls=%async_computation | async-start | bytes 2097152 | tf_op jit(solution)/shard_map/all_to_all | solution.py:453

commit v5 on v4

--- a/solution.py
+++ b/solution.py
@@ -113,23 +113,25 @@
 
 
 def share_y_kernel(fields, send, maps, to_low, to_high, cells, held, matrix, sems):
-    copies = [pltpu.make_async_copy(send, matrix, sems.at[F]), pltpu.make_async_copy(maps, held, sems.at[F + 1])]
+    copies = [pltpu.make_async_copy(send, matrix, sems.at[F])]
     for f in range(F):
         rows = pl.ds(f * 256, 256)
         copies.append(pltpu.make_async_copy(fields.at[rows], cells.at[rows], sems.at[f]))
+    copies.append(pltpu.make_async_copy(maps, held, sems.at[F + 1]))
     for copy in copies:
         copy.start()
     copies[0].wait()
-    send_hi, send_lo = matrix[:32], matrix[32:]
+    both, send_hi = matrix[...], matrix[:32]
     dims = ((1,), (1,))
     for f in range(F):
         rows = slice(f * 256, f * 256 + 256)
-        copies[2 + f].wait()
+        copies[1 + f].wait()
         cells_hi, cells_lo = halves(cells[rows])
-        shares = dot(send_hi, cells_hi, dims) + dot(send_hi, cells_lo, dims) + dot(send_lo, cells_hi, dims)
+        upper = dot(both, cells_hi, dims)
+        shares = upper[:32] + dot(send_hi, cells_lo, dims) + upper[32:]
         to_low[:, rows] = shares[:16]
         to_high[:, rows] = shares[16:]
-    copies[1].wait()
+    copies[F + 1].wait()
 
 
 def fine_shares(values):
@@ -173,11 +175,17 @@
     return near_low, near_high, lanes.pack_third([third[-6], third[-5]]), lanes.pack_third([third[8], third[9], third[10]])
 
 
-def own_y_kernel(fields, maps, own):
+def own_y_kernel(fields, maps, own, outbox, zeros, sems):
+    zeros[...] = jnp.zeros_like(zeros)
+    copies = [pltpu.make_async_copy(zeros, outbox.at[pl.ds(i * 512, 512)], sems.at[i]) for i in range(4)]
+    for copy in copies:
+        copy.start()
     cells_hi, cells_lo = halves(fields[...])
     dims = ((1,), (0,))
     own_hi, own_lo = maps[:128], maps[128:256]
     own[...] = dot(cells_hi, own_hi, dims) + dot(cells_lo, own_hi, dims) + dot(cells_hi, own_lo, dims)
+    for copy in copies:
+        copy.wait()
 
 
 def share_z_kernel(
@@ -287,7 +295,17 @@
         to_high_far[rows] = far_high
 
 
-def tiles_kernel(writers, fine, from_high, from_low, targets, tiles, counts):
+def tile_copies(targets, tiles, outbox, sems, first):
+    copies = []
+    for i in range(TILES // 2):
+        t = 2 * i + first
+        to = pl.multiple_of(targets[t] * 16, 16)
+        copies.append(pltpu.make_async_copy(tiles.at[pl.ds(t * 16, 16)], outbox.at[pl.ds(to, 16)], sems.at[i]))
+    return copies
+
+
+def tiles_kernel(writers, fine, from_high, from_low, cleared, targets, tiles, outbox, counts, sems):
+    del cleared
     for i in range(64):
         counts[i] = 0
     for t in range(TILES):
@@ -305,11 +323,19 @@
                 i = x - 12
                 row = row + from_high[i * 80 + g * 8 : i * 80 + g * 8 + 8]
             tiles[pl.ds(g * 128 + x, 8, stride=16), :] = row
+    copies = tile_copies(targets, tiles, outbox, sems, 1)
+    for copy in copies:
+        copy.start()
+    for copy in copies:
+        copy.wait()
 
 
 def route_kernel(
-    targets, tiles, coarse, from_high, from_low, from_high_far, from_low_far, outbox, low_band, spread
+    targets, tiles, coarse, from_high, from_low, from_high_far, from_low_far, filled,
+    outbox, low_band, spread, whole, sems,
 ):
+    del filled
+    copies = tile_copies(targets, whole, outbox, sems, 0)
     shape = (8, LN)
     lanes = Lanes()
     even_row = lax.broadcasted_iota(jnp.int32, shape, 0) % 2 == 0
@@ -318,7 +344,6 @@
     picked = (LN, 16)
     pick = lax.broadcasted_iota(jnp.int32, picked, 0) == 8 * lax.broadcasted_iota(jnp.int32, picked, 1) + 1
     pick = jnp.where(pick, jnp.ones(picked, jnp.float32), jnp.zeros(picked, jnp.float32)).astype(jnp.bfloat16)
-    outbox[...] = jnp.zeros_like(outbox)
     for g in range(5):
         rows = slice(g * 8, g * 8 + 8)
         added = add_coarse(
@@ -329,26 +354,26 @@
             from_low_far[rows],
             lanes,
         )
-        for i, x in ((0, 0), (1, 4)):
-            upper, lower = halves(added[x])
-            rest = (added[x] - upper.astype(jnp.float32) - lower.astype(jnp.float32)).astype(jnp.bfloat16)
-            dims = ((1,), (0,))
-            low_band[i, rows] = dot(upper, pick, dims) + dot(lower, pick, dims) + dot(rest, pick, dims)
         for x in range(8):
             row = added[x]
             if x % 2 == 0:
                 row = jnp.where(replaced, lanes.roll(row, -1), row)
             for odd in range(2):
                 spread[pl.ds(g * 128 + 2 * x + odd, 8, stride=16), :] = row
-    for t in range(TILES):
-        to = pl.multiple_of(targets[t] * 16, 16)
-        f, z = t // NB, t % NB
-        for half in (0, 8):
-            row = tiles[t * 16 + half : t * 16 + half + 8]
-            if z % 2 == 0:
-                at = (f * 8 + z // 2) * 16 + half
-                row = jnp.where(merged, spread[at : at + 8], row)
-            outbox[pl.ds(to + half, 8), :] = row
+        for z in range(0, NB, 2):
+            t = g * NB + z
+            for half in (0, 8):
+                at = (g * 8 + z // 2) * 16 + half
+                here = slice(t * 16 + half, t * 16 + half + 8)
+                whole[here] = jnp.where(merged, spread[at : at + 8], tiles[here])
+            copies[t // 2].start()
+        for i, x in ((0, 0), (1, 4)):
+            upper, lower = halves(added[x])
+            rest = (added[x] - upper.astype(jnp.float32) - lower.astype(jnp.float32)).astype(jnp.bfloat16)
+            dims = ((1,), (0,))
+            low_band[i, rows] = dot(upper, pick, dims) + dot(lower, pick, dims) + dot(rest, pick, dims)
+    for copy in copies:
+        copy.wait()
 
 
 VM = pl.BlockSpec(memory_space=pltpu.VMEM)
@@ -400,7 +425,14 @@
         [HB, HB, HB],
         grant=32 << 20,
     )
-    (own,) = call(own_y_kernel, [f32(ROWS, 2 * LN)], [cells, maps], flops=1 << 30)
+    own, outbox = call(
+        own_y_kernel,
+        [f32(ROWS, 2 * LN), f32(2048, LN)],
+        [cells, maps],
+        [pltpu.VMEM((512, LN), jnp.float32), pltpu.SemaphoreType.DMA((4,))],
+        out_specs=[VM, HB],
+        flops=1 << 30,
+    )
     from_high = shift(to_low, "gy", -1)
     from_low = shift(to_high, "gy", 1)
 
@@ -434,21 +466,24 @@
     from_high_far = shift(to_low_far, "gx", -2)
     from_low_far = shift(to_high_far, "gx", 2)
 
-    targets, tiles = call(
+    targets, tiles, outbox = call(
         tiles_kernel,
-        [jax.ShapeDtypeStruct((TILES,), jnp.int32), f32(ROWS, LN)],
-        [tile_writer.reshape(TILES), fine, from_high, from_low],
-        [pltpu.SMEM((64,), jnp.int32)],
-        [SM, VM, VM, VM],
-        [SM, VM],
+        [jax.ShapeDtypeStruct((TILES,), jnp.int32), f32(ROWS, LN), f32(2048, LN)],
+        [tile_writer.reshape(TILES), fine, from_high, from_low, outbox],
+        [pltpu.SMEM((64,), jnp.int32), pltpu.SemaphoreType.DMA((TILES // 2,))],
+        [SM, VM, VM, VM, HB],
+        [SM, VM, HB],
         flops=1 << 30,
+        aliases={4: 2},
     )
     outbox, low_band = call(
         route_kernel,
         [f32(2048, LN), f32(2, 40, 16)],
-        [targets, tiles, coarse, from_high, from_low, from_high_far, from_low_far],
-        [pltpu.VMEM((640, LN), jnp.float32)],
-        [SM] + [VM] * 6,
+        [targets, tiles, coarse, from_high, from_low, from_high_far, from_low_far, outbox],
+        [pltpu.VMEM((640, LN), jnp.float32), pltpu.VMEM((ROWS, LN), jnp.float32), pltpu.SemaphoreType.DMA((TILES // 2,))],
+        [SM] + [VM] * 6 + [HB],
+        [HB, VM],
+        aliases={7: 0},
     )
     inbox = lax.all_to_all(outbox.reshape(64, 32, LN), ("gx", "gy"), split_axis=0, concat_axis=0, tiled=True)
 

time: 102 us -> 102 us (level)
  waiting for transfers between devices: 22.5 us -> 20.6 us
  Pallas kernels: 8.85 us -> 10.5 us
    ppermute x10, waiting for transfers between devices: 10 us -> 8.13 us  [shift(): lax.ppermute(array, axis, [(i, (i + by) % count) for i in range(count)])]
    pallas_call x7, Pallas kernels: 8.85 us -> 10.5 us  [call(): pl.pallas_call(kernel, out_shape=list(outs), in_specs=specs or [VM] * len...]
  transfers between devices with their start and end apart: 11 -> 11, of which waited for: 6 -> 6; matrix products, arithmetic and copies ran while one was open for 1% -> 1% of each run, Pallas kernels for 3% -> 5%
where the time goes in v5:
time: 102 us; the launch traced here: 101 us
  starting transfers between devices  52.7 us (52%)
  waiting for transfers between devices  20.6 us (20%)
  blocking collectives  14.2 us (14%)
  Pallas kernels  10.5 us (10%)
  local copies, waits for them, and re-layouts  1.35 us (1%)
    ppermute x10, starting transfers between devices, shift(): lax.ppermute(array, axis, [(i, (i + by) % count) for i in range(count)])  42.3 us
    all_gather x1, blocking collectives, body(): band = lax.all_gather(band, 'gz', axis=0, tiled=True)  14.2 us
    all_to_all x1, waiting for transfers between devices, body(): lax.all_to_all(outbox.reshape(64, 32, LN), ('gx', 'gy'), split_axis=0, co...  12.5 us
    pallas_call x7, Pallas kernels, call(): pl.pallas_call(kernel, out_shape=list(outs), in_specs=specs or [VM] * len...  10.5 us
    all_to_all x1, starting transfers between devices, body(): lax.all_to_all(outbox.reshape(64, 32, LN), ('gx', 'gy'), split_axis=0, co...  10.5 us
    ppermute x10, waiting for transfers between devices, shift(): lax.ppermute(array, axis, [(i, (i + by) % count) for i in range(count)])  8.13 us
  transfers between devices with their start and end apart: 11, of which 6 were waited for; matrix products, arithmetic and copies ran while one was open for 1% of the time, Pallas kernels for 5%

profile of v5, /device:TPU:2, one launch (start us, length us, event | category | flops | bytes accessed | tf_op | source)
XLA Modules:
  0.0 101.2 jit_solution(12386327538276961899)
XLA Ops:
  0.6 1.9 %shard_map.68 = (f32[16,1280]{1,0:T(8,128)S(1)}, f32[16,1280]{1,0:T(8,128)S(1)}, f32[1280,128]{1,0:T(8,128)S(1)}, bf16[288,256]{1,0:T(8,128)(2,1)S(1)}) custom-call(f32[1280,128]{1,0:T(8,128)} %bitcast.14, bf16[64,128]{1,0:T(8,128)(2,1)} %constant.6.clone.send, bf16[288,256]{1,0:T(8,128)(2,1)} %constant.7.clone.maps), custom_call_target="tpu_custom_call" | custom-call | flops 1048576 | bytes 2097152 | tf_op jit(solution)/shard_map/pallas_call | solution.py:390
  2.6 3.4 %collective-permute-start = (f32[16,1280]{1,0:T(8,128)S(1)}, f32[16,1280]{1,0:T(8,128)S(1)}, u32[]{:S(2)}, u32[]{:S(2)}) collective-permute-start(f32[16,1280]{1,0:T(8,128)S(1)} %get-tuple-element.30), channel_id=1, source_target_pairs={{0,16},{16,32},{32,48},{48,64},{64,80},{80,96},{96,112},{112,0},{1... | collective-permute-start | bytes 245768 | tf_op jit(solution)/shard_map/ppermute | solution.py:404
  6.0 13.6 %collective-permute-start.1 = (f32[16,1280]{1,0:T(8,128)S(1)}, f32[16,1280]{1,0:T(8,128)S(1)}, u32[]{:S(2)}, u32[]{:S(2)}) collective-permute-start(f32[16,1280]{1,0:T(8,128)S(1)} %get-tuple-element.31), channel_id=1, source_target_pairs={{0,112},{16,0},{32,16},{48,32},{64,48},{80,64},{96,80},{112,96},{1... | collective-permute-start | bytes 245768 | tf_op jit(solution)/shard_map/ppermute | solution.py:404
  19.6 1.6 %shard_map.69 = (f32[1280,256]{1,0:T(8,128)S(1)}, f32[2048,128]{1,0:T(8,128)}) custom-call(f32[1280,128]{1,0:T(8,128)S(1)} %get-tuple-element.27.fields, bf16[288,256]{1,0:T(8,128)(2,1)S(1)} %get-tuple-element.28.maps), custom_call_target="tpu_custom_call" | custom-call | flops 1073741824 | bytes 3309568 | tf_op jit(solution)/shard_map/pallas_call | solution.py:390
  21.2 0.0 collective-permute-done.from_low
  21.2 0.4 collective-permute-done.1.from_high
  21.6 1.5 %shard_map.70 = (f32[1280,128]{1,0:T(8,128)S(1)}, f32[640,128]{1,0:T(8,128)S(1)}, f32[5,8,16,128]{3,2,1,0:T(8,128)S(1)}, f32[5,7,16,128]{3,2,1,0:T(8,128)S(1)}, ...) custom-call(f32[1280,256]{1,0:T(8,128)S(1)} %get-tuple-element.29.own, bf16[288,256]{1,0:T(8,128)(2,1)S(1)} %get-tuple-element.28.maps, ...), custom_call_target="tpu_custom_call" | custom-call | flops 1048576 | bytes 3448832 | tf_op jit(solution)/shard_map/pallas_call | solution.py:390
  23.2 4.1 %collective-permute-start.2 = (f32[5,8,16,128]{3,2,1,0:T(8,128)S(1)}, f32[5,8,16,128]{3,2,1,0:T(8,128)S(1)}, u32[]{:S(2)}, u32[]{:S(2)}) collective-permute-start(f32[5,8,16,128]{3,2,1,0:T(8,128)S(1)} %get-tuple-element.33), channel_id=1, source_target_pairs={{0,15},{1,0},{2,1},{3,2},{4,3},{5,4},{6,5},{7,6},{8,7},{9,8},{10,9... | collective-permute-start | bytes 983048 | tf_op jit(solution)/shard_map/ppermute | solution.py:404
  27.3 0.0 collective-permute-start.3
  27.3 4.4 %collective-permute-start.4 = (f32[5,16,128]{2,1,0:T(8,128)S(1)}, f32[5,16,128]{2,1,0:T(8,128)S(1)}, u32[]{:S(2)}, u32[]{:S(2)}) collective-permute-start(f32[5,16,128]{2,1,0:T(8,128)S(1)} %get-tuple-element.37), channel_id=1, source_target_pairs={{0,14},{1,15},{2,0},{3,1},{4,2},{5,3},{6,4},{7,5},{8,6},{9,7},{10,... | collective-permute-start | bytes 122888 | tf_op jit(solution)/shard_map/ppermute | solution.py:404
  31.7 1.9 %collective-permute-start.5 = (f32[5,16,128]{2,1,0:T(8,128)S(1)}, f32[5,16,128]{2,1,0:T(8,128)S(1)}, u32[]{:S(2)}, u32[]{:S(2)}) collective-permute-start(f32[5,16,128]{2,1,0:T(8,128)S(1)} %get-tuple-element.38), channel_id=1, source_target_pairs={{0,2},{1,3},{2,4},{3,5},{4,6},{5,7},{6,8},{7,9},{8,10},{9,11},{10,... | collective-permute-start | bytes 122888 | tf_op jit(solution)/shard_map/ppermute | solution.py:404
  33.6 0.9 collective-permute-done.3.from_low
  34.5 0.0 collective-permute-done.2.from_high
  34.5 0.4 shard_map.71
  35.0 0.0 copy-start
  35.0 0.0 collective-permute-done.4.from_high_far
  35.0 3.8 %collective-permute-done.5.from_low_far = f32[5,16,128]{2,1,0:T(8,128)S(1)} collective-permute-done((f32[5,16,128]{2,1,0:T(8,128)S(1)}, f32[5,16,128]{2,1,0:T(8,128)S(1)}, u32[]{:S(2)}, u32[]{:S(2)}) %collective-permute-start.5) | collective-permute-done | bytes 40992 | tf_op jit(solution)/shard_map/ppermute | solution.py:404
  38.8 0.5 shard_map.72
  39.3 6.2 %collective-permute-start.6 = (f32[480,128]{1,0:T(8,128)S(1)}, f32[480,128]{1,0:T(8,128)S(1)}, u32[]{:S(2)}, u32[]{:S(2)}) collective-permute-start(f32[480,128]{1,0:T(8,128)S(1)} %get-tuple-element.41), channel_id=1, source_target_pairs={{0,896},{128,0},{256,128},{384,256},{512,384},{640,512},{768,640},... | collective-permute-start | bytes 737288 | tf_op jit(solution)/shard_map/ppermute | solution.py:404
  45.5 1.9 %collective-permute-start.7 = (f32[400,128]{1,0:T(8,128)S(1)}, f32[400,128]{1,0:T(8,128)S(1)}, u32[]{:S(2)}, u32[]{:S(2)}) collective-permute-start(f32[400,128]{1,0:T(8,128)S(1)} %get-tuple-element.42), channel_id=1, source_target_pairs={{0,128},{128,256},{256,384},{384,512},{512,640},{640,768},{768,896... | collective-permute-start | bytes 614408 | tf_op jit(solution)/shard_map/ppermute | solution.py:404
  47.5 4.6 %collective-permute-start.8 = (f32[40,128]{1,0:T(8,128)S(1)}, f32[40,128]{1,0:T(8,128)S(1)}, u32[]{:S(2)}, u32[]{:S(2)}) collective-permute-start(f32[40,128]{1,0:T(8,128)S(1)} %get-tuple-element.47), channel_id=1, source_target_pairs={{0,768},{128,896},{256,0},{384,128},{512,256},{640,384},{768,512},... | collective-permute-start | bytes 61448 | tf_op jit(solution)/shard_map/ppermute | solution.py:404
  52.1 2.1 %collective-permute-start.9 = (f32[40,128]{1,0:T(8,128)S(1)}, f32[40,128]{1,0:T(8,128)S(1)}, u32[]{:S(2)}, u32[]{:S(2)}) collective-permute-start(f32[40,128]{1,0:T(8,128)S(1)} %get-tuple-element.48), channel_id=1, source_target_pairs={{0,256},{128,384},{256,512},{384,640},{512,768},{640,896},{768,0},... | collective-permute-start | bytes 61448 | tf_op jit(solution)/shard_map/ppermute | solution.py:404
  54.2 0.9 collective-permute-done.7.from_low
  55.1 0.0 collective-permute-done.6.from_high
  55.1 0.0 copy-done
  55.1 2.7 %shard_map.73 = (s32[80]{0:T(128)S(1)}, f32[1280,128]{1,0:T(8,128)S(1)}, f32[2048,128]{1,0:T(8,128)}) custom-call(s32[80]{0:T(128)S(1)} %bitcast.13, f32[16,80,128]{2,1,0:T(8,128)S(1)} %get-tuple-element.35.fine, f32[480,128]{1,0:T(8,128)S(1)} %collective-permute-done.6.from_high, ...), custom_call_target="tpu_custom_call", output_to_operand_aliasing={{2}: (4, {})} | custom-call | flops 1073741824 | bytes 3859072 | tf_op jit(solution)/shard_map/pallas_call | solution.py:390
  57.8 0.0 collective-permute-done.8.from_high_far
  57.8 2.0 %collective-permute-done.9.from_low_far = f32[40,128]{1,0:T(8,128)S(1)} collective-permute-done((f32[40,128]{1,0:T(8,128)S(1)}, f32[40,128]{1,0:T(8,128)S(1)}, u32[]{:S(2)}, u32[]{:S(2)}) %collective-permute-start.9) | collective-permute-done | bytes 20512 | tf_op jit(solution)/shard_map/ppermute | solution.py:404
  59.8 1.8 %shard_map.74 = (f32[2048,128]{1,0:T(8,128)}, f32[2,40,16]{2,1,0:T(8,128)S(1)}) custom-call(s32[80]{0:T(128)S(1)} %get-tuple-element.44.targets, f32[1280,128]{1,0:T(8,128)S(1)} %get-tuple-element.45.tiles, f32[8,40,128]{2,1,0:T(8,128)S(1)} %get-tuple-element.46.coarse, ...), custom_call_target="tpu_custom_call", output_to_operand_aliasing={{0}: (7, {})} | custom-call | flops 1048576 | bytes 3413312 | tf_op jit(solution)/shard_map/pallas_call | solution.py:390
  61.7 0.0 copy-start.1
  61.7 10.5 %all-to-all-start = ((f32[64,32,128]{2,1,0:T(8,128)}), f32[64,32,128]{2,1,0:T(8,128)S(1)}, u32[]{:S(2)}, u32[]{:S(2)}) async-start(f32[64,32,128]{2,1,0:T(8,128)} %bitcast.6), calls=%async_computation | async-start | bytes 2097152 | tf_op jit(solution)/shard_map/all_to_all | solution.py:488
  72.1 0.1 slice.3
  72.3 0.1 reshape.32
  72.3 14.2 %all-gather = f32[16,2,160]{2,1,0:T(2,128)S(1)} all-gather(f32[1,2,160]{2,1,0:T(2,128)S(1)} %reshape.32), channel_id=1, replica_groups=mesh['gx'=8,'gy'=8,'gz'=16] {'gz'}, dimensions={0}, use_global_device_ids=true | all-gather | bytes 21760 | tf_op jit(solution)/shard_map/all_gather | solution.py:491
  86.6 0.0 copy-done.1
  86.6 1.0 fusion
  87.6 12.5 %all-to-all-done = f32[64,32,128]{2,1,0:T(8,128)S(1)} async-done(((f32[64,32,128]{2,1,0:T(8,128)}), f32[64,32,128]{2,1,0:T(8,128)S(1)}, u32[]{:S(2)}, u32[]{:S(2)}) %all-to-all-start) | async-done | bytes 1048608 | tf_op jit(solution)/shard_map/all_to_all | solution.py:488
  100.1 1.1 %reshape.31 = f32[128,2048]{1,0:T(8,128)} reshape(f32[64,32,128]{2,1,0:T(8,128)S(1)} %all-to-all-done) | data formatting | bytes 2097152 | tf_op jit(solution)/shard_map/reshape | solution.py:495
  (2 shorter events, 0.0 us)
Async XLA Ops:
  2.6 18.6 %collective-permute-start = (f32[16,1280]{1,0:T(8,128)S(1)}, f32[16,1280]{1,0:T(8,128)S(1)}, u32[]{:S(2)}, u32[]{:S(2)}) collective-permute-start(f32[16,1280]{1,0:T(8,128)S(1)} %get-tuple-element.30), channel_id=1, source_target_pairs={{0,16},{16,32},{32,48},{48,64},{64,80},{80,96},{96,112},{112,0},{1... | collective-permute-start | bytes 245768 | tf_op jit(solution)/shard_map/ppermute | solution.py:404
  6.0 15.7 %collective-permute-start.1 = (f32[16,1280]{1,0:T(8,128)S(1)}, f32[16,1280]{1,0:T(8,128)S(1)}, u32[]{:S(2)}, u32[]{:S(2)}) collective-permute-start(f32[16,1280]{1,0:T(8,128)S(1)} %get-tuple-element.31), channel_id=1, source_target_pairs={{0,112},{16,0},{32,16},{48,32},{64,48},{80,64},{96,80},{112,96},{1... | collective-permute-start | bytes 245768 | tf_op jit(solution)/shard_map/ppermute | solution.py:404
  23.2 11.4 %collective-permute-start.2 = (f32[5,8,16,128]{3,2,1,0:T(8,128)S(1)}, f32[5,8,16,128]{3,2,1,0:T(8,128)S(1)}, u32[]{:S(2)}, u32[]{:S(2)}) collective-permute-start(f32[5,8,16,128]{3,2,1,0:T(8,128)S(1)} %get-tuple-element.33), channel_id=1, source_target_pairs={{0,15},{1,0},{2,1},{3,2},{4,3},{5,4},{6,5},{7,6},{8,7},{9,8},{10,9... | collective-permute-start | bytes 983048 | tf_op jit(solution)/shard_map/ppermute | solution.py:404
  27.3 7.3 %collective-permute-start.3 = (f32[5,7,16,128]{3,2,1,0:T(8,128)S(1)}, f32[5,7,16,128]{3,2,1,0:T(8,128)S(1)}, u32[]{:S(2)}, u32[]{:S(2)}) collective-permute-start(f32[5,7,16,128]{3,2,1,0:T(8,128)S(1)} %get-tuple-element.34), channel_id=1, source_target_pairs={{0,1},{1,2},{2,3},{3,4},{4,5},{5,6},{6,7},{7,8},{8,9},{9,10},{10,1... | collective-permute-start | bytes 860168 | tf_op jit(solution)/shard_map/ppermute | solution.py:404
  27.3 7.7 %collective-permute-start.4 = (f32[5,16,128]{2,1,0:T(8,128)S(1)}, f32[5,16,128]{2,1,0:T(8,128)S(1)}, u32[]{:S(2)}, u32[]{:S(2)}) collective-permute-start(f32[5,16,128]{2,1,0:T(8,128)S(1)} %get-tuple-element.37), channel_id=1, source_target_pairs={{0,14},{1,15},{2,0},{3,1},{4,2},{5,3},{6,4},{7,5},{8,6},{9,7},{10,... | collective-permute-start | bytes 122888 | tf_op jit(solution)/shard_map/ppermute | solution.py:404
  31.7 7.2 %collective-permute-start.5 = (f32[5,16,128]{2,1,0:T(8,128)S(1)}, f32[5,16,128]{2,1,0:T(8,128)S(1)}, u32[]{:S(2)}, u32[]{:S(2)}) collective-permute-start(f32[5,16,128]{2,1,0:T(8,128)S(1)} %get-tuple-element.38), channel_id=1, source_target_pairs={{0,2},{1,3},{2,4},{3,5},{4,6},{5,7},{6,8},{7,9},{8,10},{9,11},{10,... | collective-permute-start | bytes 122888 | tf_op jit(solution)/shard_map/ppermute | solution.py:404
  35.0 20.2 %copy-start = (s32[1,1,80,1]{2,3,1,0:T(1,128)S(1)}, s32[1,1,80,1]{2,3,1,0:T(1,128)}, u32[]{:S(2)}) copy-start(s32[1,1,80,1]{2,3,1,0:T(1,128)} %param.6) | copy-start | bytes 964
  39.3 15.8 %collective-permute-start.6 = (f32[480,128]{1,0:T(8,128)S(1)}, f32[480,128]{1,0:T(8,128)S(1)}, u32[]{:S(2)}, u32[]{:S(2)}) collective-permute-start(f32[480,128]{1,0:T(8,128)S(1)} %get-tuple-element.41), channel_id=1, source_target_pairs={{0,896},{128,0},{256,128},{384,256},{512,384},{640,512},{768,640},... | collective-permute-start | bytes 737288 | tf_op jit(solution)/shard_map/ppermute | solution.py:404
  45.5 9.6 %collective-permute-start.7 = (f32[400,128]{1,0:T(8,128)S(1)}, f32[400,128]{1,0:T(8,128)S(1)}, u32[]{:S(2)}, u32[]{:S(2)}) collective-permute-start(f32[400,128]{1,0:T(8,128)S(1)} %get-tuple-element.42), channel_id=1, source_target_pairs={{0,128},{128,256},{256,384},{384,512},{512,640},{640,768},{768,896... | collective-permute-start | bytes 614408 | tf_op jit(solution)/shard_map/ppermute | solution.py:404
  47.5 10.4 %collective-permute-start.8 = (f32[40,128]{1,0:T(8,128)S(1)}, f32[40,128]{1,0:T(8,128)S(1)}, u32[]{:S(2)}, u32[]{:S(2)}) collective-permute-start(f32[40,128]{1,0:T(8,128)S(1)} %get-tuple-element.47), channel_id=1, source_target_pairs={{0,768},{128,896},{256,0},{384,128},{512,256},{640,384},{768,512},... | collective-permute-start | bytes 61448 | tf_op jit(solution)/shard_map/ppermute | solution.py:404
  52.1 7.8 %collective-permute-start.9 = (f32[40,128]{1,0:T(8,128)S(1)}, f32[40,128]{1,0:T(8,128)S(1)}, u32[]{:S(2)}, u32[]{:S(2)}) collective-permute-start(f32[40,128]{1,0:T(8,128)S(1)} %get-tuple-element.48), channel_id=1, source_target_pairs={{0,256},{128,384},{256,512},{384,640},{512,768},{640,896},{768,0},... | collective-permute-start | bytes 61448 | tf_op jit(solution)/shard_map/ppermute | solution.py:404
  61.7 24.9 %copy-start.1 = (f32[32,32]{1,0:T(8,128)S(1)}, f32[32,32]{1,0:T(8,128)}, u32[]{:S(2)}) copy-start(f32[32,32]{1,0:T(8,128)} %constant.8.clone) | copy-start | bytes 12292
  61.7 38.4 %all-to-all-start = ((f32[64,32,128]{2,1,0:T(8,128)}), f32[64,32,128]{2,1,0:T(8,128)S(1)}, u32[]{:S(2)}, u32[]{:S(2)}) async-start(f32[64,32,128]{2,1,0:T(8,128)} %bitcast.6), calls=%async_computation | async-start | bytes 2097152 | tf_op jit(solution)/shard_map/all_to_all | solution.py:488

commit v6 on v5

--- a/solution.py
+++ b/solution.py
@@ -112,12 +112,13 @@
     return upper, (x - upper.astype(jnp.float32)).astype(jnp.bfloat16)
 
 
-def share_y_kernel(fields, send, maps, to_low, to_high, cells, held, matrix, sems):
+def share_y_kernel(fields, send, maps, writers, to_low, to_high, cells, held, held_writers, matrix, sems):
     copies = [pltpu.make_async_copy(send, matrix, sems.at[F])]
     for f in range(F):
         rows = pl.ds(f * 256, 256)
         copies.append(pltpu.make_async_copy(fields.at[rows], cells.at[rows], sems.at[f]))
     copies.append(pltpu.make_async_copy(maps, held, sems.at[F + 1]))
+    copies.append(pltpu.make_async_copy(writers, held_writers, sems.at[F + 2]))
     for copy in copies:
         copy.start()
     copies[0].wait()
@@ -132,6 +133,7 @@
         to_low[:, rows] = shares[:16]
         to_high[:, rows] = shares[16:]
     copies[F + 1].wait()
+    copies[F + 2].wait()
 
 
 def fine_shares(values):
@@ -175,7 +177,18 @@
     return near_low, near_high, lanes.pack_third([third[-6], third[-5]]), lanes.pack_third([third[8], third[9], third[10]])
 
 
-def own_y_kernel(fields, maps, own, outbox, zeros, sems):
+def slots_of(row):
+    shape = (TILES, TILES)
+    wide = jnp.broadcast_to(row, shape)
+    other = lax.broadcasted_iota(jnp.int32, shape, 0)
+    tile = lax.broadcasted_iota(jnp.int32, shape, 1)
+    zero = jnp.zeros(shape, jnp.float32)
+    column = jnp.sum(jnp.where(other == tile, wide, zero), axis=1, keepdims=True)
+    equal = jnp.where((wide == column) & (other < tile), zero + 1, zero)
+    return row * 2 + jnp.sum(equal, axis=0, keepdims=True)
+
+
+def own_y_kernel(writers, fields, maps, own, outbox, targets, zeros, sems):
     zeros[...] = jnp.zeros_like(zeros)
     copies = [pltpu.make_async_copy(zeros, outbox.at[pl.ds(i * 512, 512)], sems.at[i]) for i in range(4)]
     for copy in copies:
@@ -184,6 +197,7 @@
     dims = ((1,), (0,))
     own_hi, own_lo = maps[:128], maps[128:256]
     own[...] = dot(cells_hi, own_hi, dims) + dot(cells_lo, own_hi, dims) + dot(cells_hi, own_lo, dims)
+    targets[...] = slots_of(writers[...].astype(jnp.float32)).astype(jnp.int32)
     for copy in copies:
         copy.wait()
 
@@ -304,15 +318,8 @@
     return copies
 
 
-def tiles_kernel(writers, fine, from_high, from_low, cleared, targets, tiles, outbox, counts, sems):
+def tiles_kernel(targets, fine, from_high, from_low, cleared, tiles, outbox, sems):
     del cleared
-    for i in range(64):
-        counts[i] = 0
-    for t in range(TILES):
-        writer = writers[t]
-        slot = counts[writer]
-        counts[writer] = slot + 1
-        targets[t] = writer * 2 + slot
     for g in range(10):
         rows = slice(g * 8, g * 8 + 8)
         for x in range(NB):
@@ -332,7 +339,7 @@
 
 def route_kernel(
     targets, tiles, coarse, from_high, from_low, from_high_far, from_low_far, filled,
-    outbox, low_band, spread, whole, sems,
+    outbox, low_rows, spread, whole, sems,
 ):
     del filled
     copies = tile_copies(targets, whole, outbox, sems, 0)
@@ -341,9 +348,6 @@
     even_row = lax.broadcasted_iota(jnp.int32, shape, 0) % 2 == 0
     replaced = (lanes.lane % 4 == 0) & even_row
     merged = lanes.second & even_row
-    picked = (LN, 16)
-    pick = lax.broadcasted_iota(jnp.int32, picked, 0) == 8 * lax.broadcasted_iota(jnp.int32, picked, 1) + 1
-    pick = jnp.where(pick, jnp.ones(picked, jnp.float32), jnp.zeros(picked, jnp.float32)).astype(jnp.bfloat16)
     for g in range(5):
         rows = slice(g * 8, g * 8 + 8)
         added = add_coarse(
@@ -367,13 +371,20 @@
                 here = slice(t * 16 + half, t * 16 + half + 8)
                 whole[here] = jnp.where(merged, spread[at : at + 8], tiles[here])
             copies[t // 2].start()
-        for i, x in ((0, 0), (1, 4)):
-            upper, lower = halves(added[x])
-            rest = (added[x] - upper.astype(jnp.float32) - lower.astype(jnp.float32)).astype(jnp.bfloat16)
-            dims = ((1,), (0,))
-            low_band[i, rows] = dot(upper, pick, dims) + dot(lower, pick, dims) + dot(rest, pick, dims)
+        low_rows[g * 8 : g * 8 + 8] = added[0]
+        low_rows[40 + g * 8 : 40 + g * 8 + 8] = added[4]
     for copy in copies:
         copy.wait()
+
+
+def pick_kernel(rows, low_band):
+    picked = (LN, 16)
+    pick = lax.broadcasted_iota(jnp.int32, picked, 0) == 8 * lax.broadcasted_iota(jnp.int32, picked, 1) + 1
+    pick = jnp.where(pick, jnp.ones(picked, jnp.float32), jnp.zeros(picked, jnp.float32)).astype(jnp.bfloat16)
+    upper, lower = halves(rows[...])
+    rest = (rows[...] - upper.astype(jnp.float32) - lower.astype(jnp.float32)).astype(jnp.bfloat16)
+    dims = ((1,), (0,))
+    low_band[...] = dot(upper, pick, dims) + dot(lower, pick, dims) + dot(rest, pick, dims)
 
 
 VM = pl.BlockSpec(memory_space=pltpu.VMEM)
@@ -416,21 +427,22 @@
     send = jnp.asarray(np.concatenate(split(send)))
     maps = jnp.asarray(np.concatenate([*split(own), place.astype(ml_dtypes.bfloat16)]))
     cells = fields.reshape(ROWS, LN)
-
-    to_low, to_high, cells, maps = call(
+    writers = tile_writer.reshape(1, TILES)
+
+    to_low, to_high, cells, maps, writers = call(
         share_y_kernel,
-        [f32(16, ROWS), f32(16, ROWS), f32(ROWS, LN), jax.ShapeDtypeStruct(maps.shape, maps.dtype)],
-        [pltpu.with_memory_space_constraint(a, pltpu.HBM) for a in (cells, send, maps)],
-        [pltpu.VMEM((64, LN), jnp.bfloat16), pltpu.SemaphoreType.DMA((F + 2,))],
-        [HB, HB, HB],
+        [f32(16, ROWS), f32(16, ROWS), f32(ROWS, LN)] + [jax.ShapeDtypeStruct(a.shape, a.dtype) for a in (maps, writers)],
+        [pltpu.with_memory_space_constraint(a, pltpu.HBM) for a in (cells, send, maps, writers)],
+        [pltpu.VMEM((64, LN), jnp.bfloat16), pltpu.SemaphoreType.DMA((F + 3,))],
+        [HB, HB, HB, HB],
         grant=32 << 20,
     )
-    own, outbox = call(
+    own, outbox, targets = call(
         own_y_kernel,
-        [f32(ROWS, 2 * LN), f32(2048, LN)],
-        [cells, maps],
+        [f32(ROWS, 2 * LN), f32(2048, LN), jax.ShapeDtypeStruct((1, TILES), jnp.int32)],
+        [writers, cells, maps],
         [pltpu.VMEM((512, LN), jnp.float32), pltpu.SemaphoreType.DMA((4,))],
-        out_specs=[VM, HB],
+        out_specs=[VM, HB, VM],
         flops=1 << 30,
     )
     from_high = shift(to_low, "gy", -1)
@@ -466,19 +478,20 @@
     from_high_far = shift(to_low_far, "gx", -2)
     from_low_far = shift(to_high_far, "gx", 2)
 
-    targets, tiles, outbox = call(
+    targets = targets.reshape(TILES)
+    tiles, outbox = call(
         tiles_kernel,
-        [jax.ShapeDtypeStruct((TILES,), jnp.int32), f32(ROWS, LN), f32(2048, LN)],
-        [tile_writer.reshape(TILES), fine, from_high, from_low, outbox],
-        [pltpu.SMEM((64,), jnp.int32), pltpu.SemaphoreType.DMA((TILES // 2,))],
+        [f32(ROWS, LN), f32(2048, LN)],
+        [targets, fine, from_high, from_low, outbox],
+        [pltpu.SemaphoreType.DMA((TILES // 2,))],
         [SM, VM, VM, VM, HB],
-        [SM, VM, HB],
+        [VM, HB],
         flops=1 << 30,
-        aliases={4: 2},
-    )
-    outbox, low_band = call(
+        aliases={4: 1},
+    )
+    outbox, low_rows = call(
         route_kernel,
-        [f32(2048, LN), f32(2, 40, 16)],
+        [f32(2048, LN), f32(80, LN)],
         [targets, tiles, coarse, from_high, from_low, from_high_far, from_low_far, outbox],
         [pltpu.VMEM((640, LN), jnp.float32), pltpu.VMEM((ROWS, LN), jnp.float32), pltpu.SemaphoreType.DMA((TILES // 2,))],
         [SM] + [VM] * 6 + [HB],
@@ -487,6 +500,7 @@
     )
     inbox = lax.all_to_all(outbox.reshape(64, 32, LN), ("gx", "gy"), split_axis=0, concat_axis=0, tiled=True)
 
+    (low_band,) = call(pick_kernel, [f32(80, 16)], [low_rows])
     band = low_band.reshape(2, F, 8, 16)[:, :, ::4].transpose(2, 1, 0, 3).reshape(2, F * 32)
     band = lax.all_gather(band, "gz", axis=0, tiled=True)
     turn = jnp.asarray(coarse_matrix(band.shape[0]))

time: 102 us -> 102 us (level)
    pallas_call x7 -> x8, Pallas kernels: 10.5 us -> 9.8 us  [call(): pl.pallas_call(kernel, out_shape=list(outs), in_specs=specs or [VM] * len...]
  transfers between devices with their start and end apart: 11 -> 11, of which waited for: 6 -> 6; matrix products, arithmetic and copies ran while one was open for 1% -> 1% of each run, Pallas kernels for 5% -> 4%
where the time goes in v6:
time: 102 us; the launch traced here: 101 us
  starting transfers between devices  52.7 us (52%)
  waiting for transfers between devices  21.3 us (21%)
  blocking collectives  14.2 us (14%)
  Pallas kernels  9.8 us (10%)
  local copies, waits for them, and re-layouts  1.34 us (1%)
    ppermute x10, starting transfers between devices, shift(): lax.ppermute(array, axis, [(i, (i + by) % count) for i in range(count)])  42.3 us
    all_gather x1, blocking collectives, body(): band = lax.all_gather(band, 'gz', axis=0, tiled=True)  14.2 us
    all_to_all x1, waiting for transfers between devices, body(): lax.all_to_all(outbox.reshape(64, 32, LN), ('gx', 'gy'), split_axis=0, co...  12.3 us
    all_to_all x1, starting transfers between devices, body(): lax.all_to_all(outbox.reshape(64, 32, LN), ('gx', 'gy'), split_axis=0, co...  10.5 us
    pallas_call x8, Pallas kernels, call(): pl.pallas_call(kernel, out_shape=list(outs), in_specs=specs or [VM] * len...  9.8 us
    ppermute x10, waiting for transfers between devices, shift(): lax.ppermute(array, axis, [(i, (i + by) % count) for i in range(count)])  8.99 us
  transfers between devices with their start and end apart: 11, of which 6 were waited for; matrix products, arithmetic and copies ran while one was open for 1% of the time, Pallas kernels for 4%

profile of v6, /device:TPU:2, one launch (start us, length us, event | category | flops | bytes accessed | tf_op | source)
XLA Modules:
  0.0 101.2 jit_solution(476098163081570225)
XLA Ops:
  0.6 1.9 %shard_map.68 = (f32[16,1280]{1,0:T(8,128)S(1)}, f32[16,1280]{1,0:T(8,128)S(1)}, f32[1280,128]{1,0:T(8,128)S(1)}, bf16[288,256]{1,0:T(8,128)(2,1)S(1)}, s32[1,80]{1,0:T(1,128)S(1)}) custom-call(f32[1280,128]{1,0:T(8,128)} %bitcast.16, bf16[64,128]{1,0:T(8,128)(2,1)} %constant.6.clone.send, bf16[288,256]{1,0:T(8,128)(2,1)} %constant.7.clone.maps, ...), custom_call_target="tpu_custom_call" | custom-call | flops 1048576 | bytes 2097792 | tf_op jit(solution)/shard_map/pallas_call | solution.py:401
  2.6 3.4 %collective-permute-start = (f32[16,1280]{1,0:T(8,128)S(1)}, f32[16,1280]{1,0:T(8,128)S(1)}, u32[]{:S(2)}, u32[]{:S(2)}) collective-permute-start(f32[16,1280]{1,0:T(8,128)S(1)} %get-tuple-element.33), channel_id=1, source_target_pairs={{0,16},{16,32},{32,48},{48,64},{64,80},{80,96},{96,112},{112,0},{1... | collective-permute-start | bytes 245768 | tf_op jit(solution)/shard_map/ppermute | solution.py:415
  6.0 13.6 %collective-permute-start.1 = (f32[16,1280]{1,0:T(8,128)S(1)}, f32[16,1280]{1,0:T(8,128)S(1)}, u32[]{:S(2)}, u32[]{:S(2)}) collective-permute-start(f32[16,1280]{1,0:T(8,128)S(1)} %get-tuple-element.34), channel_id=1, source_target_pairs={{0,112},{16,0},{32,16},{48,32},{64,48},{80,64},{96,80},{112,96},{1... | collective-permute-start | bytes 245768 | tf_op jit(solution)/shard_map/ppermute | solution.py:415
  19.6 1.6 %shard_map.69 = (f32[1280,256]{1,0:T(8,128)S(1)}, f32[2048,128]{1,0:T(8,128)}, s32[1,80]{1,0:T(1,128)S(1)}) custom-call(s32[1,80]{1,0:T(1,128)S(1)} %get-tuple-element.28.writers, f32[1280,128]{1,0:T(8,128)S(1)} %get-tuple-element.29.fields, bf16[288,256]{1,0:T(8,128)(2,1)S(1)} %get-tuple-element.30.maps), custom_call_target="tpu_custom_call" | custom-call | flops 1073741824 | bytes 3310208 | tf_op jit(solution)/shard_map/pallas_call | solution.py:401
  21.2 0.0 collective-permute-done.from_low
  21.2 0.4 collective-permute-done.1.from_high
  21.6 1.5 %shard_map.70 = (f32[1280,128]{1,0:T(8,128)S(1)}, f32[640,128]{1,0:T(8,128)S(1)}, f32[5,8,16,128]{3,2,1,0:T(8,128)S(1)}, f32[5,7,16,128]{3,2,1,0:T(8,128)S(1)}, ...) custom-call(f32[1280,256]{1,0:T(8,128)S(1)} %get-tuple-element.32.own, bf16[288,256]{1,0:T(8,128)(2,1)S(1)} %get-tuple-element.30.maps, ...), custom_call_target="tpu_custom_call" | custom-call | flops 1048576 | bytes 3448832 | tf_op jit(solution)/shard_map/pallas_call | solution.py:401
  23.2 4.1 %collective-permute-start.2 = (f32[5,8,16,128]{3,2,1,0:T(8,128)S(1)}, f32[5,8,16,128]{3,2,1,0:T(8,128)S(1)}, u32[]{:S(2)}, u32[]{:S(2)}) collective-permute-start(f32[5,8,16,128]{3,2,1,0:T(8,128)S(1)} %get-tuple-element.36), channel_id=1, source_target_pairs={{0,15},{1,0},{2,1},{3,2},{4,3},{5,4},{6,5},{7,6},{8,7},{9,8},{10,9... | collective-permute-start | bytes 983048 | tf_op jit(solution)/shard_map/ppermute | solution.py:415
  27.3 0.0 collective-permute-start.3
  27.3 4.4 %collective-permute-start.4 = (f32[5,16,128]{2,1,0:T(8,128)S(1)}, f32[5,16,128]{2,1,0:T(8,128)S(1)}, u32[]{:S(2)}, u32[]{:S(2)}) collective-permute-start(f32[5,16,128]{2,1,0:T(8,128)S(1)} %get-tuple-element.40), channel_id=1, source_target_pairs={{0,14},{1,15},{2,0},{3,1},{4,2},{5,3},{6,4},{7,5},{8,6},{9,7},{10,... | collective-permute-start | bytes 122888 | tf_op jit(solution)/shard_map/ppermute | solution.py:415
  31.7 1.9 %collective-permute-start.5 = (f32[5,16,128]{2,1,0:T(8,128)S(1)}, f32[5,16,128]{2,1,0:T(8,128)S(1)}, u32[]{:S(2)}, u32[]{:S(2)}) collective-permute-start(f32[5,16,128]{2,1,0:T(8,128)S(1)} %get-tuple-element.41), channel_id=1, source_target_pairs={{0,2},{1,3},{2,4},{3,5},{4,6},{5,7},{6,8},{7,9},{8,10},{9,11},{10,... | collective-permute-start | bytes 122888 | tf_op jit(solution)/shard_map/ppermute | solution.py:415
  33.6 0.9 collective-permute-done.3.from_low
  34.5 0.0 collective-permute-done.2.from_high
  34.5 0.4 shard_map.71
  35.0 0.0 collective-permute-done.4.from_high_far
  35.0 3.8 %collective-permute-done.5.from_low_far = f32[5,16,128]{2,1,0:T(8,128)S(1)} collective-permute-done((f32[5,16,128]{2,1,0:T(8,128)S(1)}, f32[5,16,128]{2,1,0:T(8,128)S(1)}, u32[]{:S(2)}, u32[]{:S(2)}) %collective-permute-start.5) | collective-permute-done | bytes 40992 | tf_op jit(solution)/shard_map/ppermute | solution.py:415
  38.8 0.5 shard_map.72
  39.4 6.2 %collective-permute-start.6 = (f32[480,128]{1,0:T(8,128)S(1)}, f32[480,128]{1,0:T(8,128)S(1)}, u32[]{:S(2)}, u32[]{:S(2)}) collective-permute-start(f32[480,128]{1,0:T(8,128)S(1)} %get-tuple-element.44), channel_id=1, source_target_pairs={{0,896},{128,0},{256,128},{384,256},{512,384},{640,512},{768,640},... | collective-permute-start | bytes 737288 | tf_op jit(solution)/shard_map/ppermute | solution.py:415
  45.5 1.9 %collective-permute-start.7 = (f32[400,128]{1,0:T(8,128)S(1)}, f32[400,128]{1,0:T(8,128)S(1)}, u32[]{:S(2)}, u32[]{:S(2)}) collective-permute-start(f32[400,128]{1,0:T(8,128)S(1)} %get-tuple-element.45), channel_id=1, source_target_pairs={{0,128},{128,256},{256,384},{384,512},{512,640},{640,768},{768,896... | collective-permute-start | bytes 614408 | tf_op jit(solution)/shard_map/ppermute | solution.py:415
  47.5 4.6 %collective-permute-start.8 = (f32[40,128]{1,0:T(8,128)S(1)}, f32[40,128]{1,0:T(8,128)S(1)}, u32[]{:S(2)}, u32[]{:S(2)}) collective-permute-start(f32[40,128]{1,0:T(8,128)S(1)} %get-tuple-element.49), channel_id=1, source_target_pairs={{0,768},{128,896},{256,0},{384,128},{512,256},{640,384},{768,512},... | collective-permute-start | bytes 61448 | tf_op jit(solution)/shard_map/ppermute | solution.py:415
  52.1 2.1 %collective-permute-start.9 = (f32[40,128]{1,0:T(8,128)S(1)}, f32[40,128]{1,0:T(8,128)S(1)}, u32[]{:S(2)}, u32[]{:S(2)}) collective-permute-start(f32[40,128]{1,0:T(8,128)S(1)} %get-tuple-element.50), channel_id=1, source_target_pairs={{0,256},{128,384},{256,512},{384,640},{512,768},{640,896},{768,0},... | collective-permute-start | bytes 61448 | tf_op jit(solution)/shard_map/ppermute | solution.py:415
  54.2 0.9 collective-permute-done.7.from_low
  55.1 0.0 collective-permute-done.6.from_high
  55.2 1.8 %shard_map.73 = (f32[1280,128]{1,0:T(8,128)S(1)}, f32[2048,128]{1,0:T(8,128)}) custom-call(s32[80]{0:T(128)S(1)} %bitcast.14, f32[16,80,128]{2,1,0:T(8,128)S(1)} %get-tuple-element.38.fine, f32[480,128]{1,0:T(8,128)S(1)} %collective-permute-done.6.from_high, f32[400,128]{1,0:T(8,128)S(1)} %collective-permute-done.7.from_low, ...), custom_call_target="tpu_custom_call", output_to_operand_aliasing={{1}: (4, {})} | custom-call | flops 1073741824 | bytes 3858752 | tf_op jit(solution)/shard_map/pallas_call | solution.py:401
  57.0 0.0 collective-permute-done.8.from_high_far
  57.0 2.8 %collective-permute-done.9.from_low_far = f32[40,128]{1,0:T(8,128)S(1)} collective-permute-done((f32[40,128]{1,0:T(8,128)S(1)}, f32[40,128]{1,0:T(8,128)S(1)}, u32[]{:S(2)}, u32[]{:S(2)}) %collective-permute-start.9) | collective-permute-done | bytes 20512 | tf_op jit(solution)/shard_map/ppermute | solution.py:415
  59.9 1.8 %shard_map.74 = (f32[2048,128]{1,0:T(8,128)}, f32[80,128]{1,0:T(8,128)S(1)}) custom-call(s32[80]{0:T(128)S(1)} %bitcast.15, f32[1280,128]{1,0:T(8,128)S(1)} %get-tuple-element.47.tiles, f32[8,40,128]{2,1,0:T(8,128)S(1)} %get-tuple-element.48.coarse, f32[480,128]{1,0:T(8,128)S(1)} %collective-permute-done.6.from_high, ...), custom_call_target="tpu_custom_call", output_to_operand_aliasing={{0}: (7, {})} | custom-call | flops 1048576 | bytes 3449152 | tf_op jit(solution)/shard_map/pallas_call | solution.py:401
  61.7 0.0 copy-start
  61.7 10.5 %all-to-all-start = ((f32[64,32,128]{2,1,0:T(8,128)}), f32[64,32,128]{2,1,0:T(8,128)S(1)}, u32[]{:S(2)}, u32[]{:S(2)}) async-start(f32[64,32,128]{2,1,0:T(8,128)} %bitcast.7), calls=%async_computation | async-start | bytes 2097152 | tf_op jit(solution)/shard_map/all_to_all | solution.py:501
  72.2 0.2 shard_map.75
  72.3 0.1 slice.3
  72.5 0.1 reshape.36
  72.5 14.2 %all-gather = f32[16,2,160]{2,1,0:T(2,128)S(1)} all-gather(f32[1,2,160]{2,1,0:T(2,128)S(1)} %reshape.36), channel_id=1, replica_groups=mesh['gx'=8,'gy'=8,'gz'=16] {'gz'}, dimensions={0}, use_global_device_ids=true | all-gather | bytes 21760 | tf_op jit(solution)/shard_map/all_gather | solution.py:505
  86.8 0.0 copy-done
  86.8 1.0 fusion
  87.8 12.3 %all-to-all-done = f32[64,32,128]{2,1,0:T(8,128)S(1)} async-done(((f32[64,32,128]{2,1,0:T(8,128)}), f32[64,32,128]{2,1,0:T(8,128)S(1)}, u32[]{:S(2)}, u32[]{:S(2)}) %all-to-all-start) | async-done | bytes 1048608 | tf_op jit(solution)/shard_map/all_to_all | solution.py:501
  100.1 1.1 %reshape.35 = f32[128,2048]{1,0:T(8,128)} reshape(f32[64,32,128]{2,1,0:T(8,128)S(1)} %all-to-all-done) | data formatting | bytes 2097152 | tf_op jit(solution)/shard_map/reshape | solution.py:509
  (2 shorter events, 0.0 us)
Async XLA Ops:
  2.6 18.6 %collective-permute-start = (f32[16,1280]{1,0:T(8,128)S(1)}, f32[16,1280]{1,0:T(8,128)S(1)}, u32[]{:S(2)}, u32[]{:S(2)}) collective-permute-start(f32[16,1280]{1,0:T(8,128)S(1)} %get-tuple-element.33), channel_id=1, source_target_pairs={{0,16},{16,32},{32,48},{48,64},{64,80},{80,96},{96,112},{112,0},{1... | collective-permute-start | bytes 245768 | tf_op jit(solution)/shard_map/ppermute | solution.py:415
  6.0 15.7 %collective-permute-start.1 = (f32[16,1280]{1,0:T(8,128)S(1)}, f32[16,1280]{1,0:T(8,128)S(1)}, u32[]{:S(2)}, u32[]{:S(2)}) collective-permute-start(f32[16,1280]{1,0:T(8,128)S(1)} %get-tuple-element.34), channel_id=1, source_target_pairs={{0,112},{16,0},{32,16},{48,32},{64,48},{80,64},{96,80},{112,96},{1... | collective-permute-start | bytes 245768 | tf_op jit(solution)/shard_map/ppermute | solution.py:415
  23.2 11.4 %collective-permute-start.2 = (f32[5,8,16,128]{3,2,1,0:T(8,128)S(1)}, f32[5,8,16,128]{3,2,1,0:T(8,128)S(1)}, u32[]{:S(2)}, u32[]{:S(2)}) collective-permute-start(f32[5,8,16,128]{3,2,1,0:T(8,128)S(1)} %get-tuple-element.36), channel_id=1, source_target_pairs={{0,15},{1,0},{2,1},{3,2},{4,3},{5,4},{6,5},{7,6},{8,7},{9,8},{10,9... | collective-permute-start | bytes 983048 | tf_op jit(solution)/shard_map/ppermute | solution.py:415
  27.3 7.3 %collective-permute-start.3 = (f32[5,7,16,128]{3,2,1,0:T(8,128)S(1)}, f32[5,7,16,128]{3,2,1,0:T(8,128)S(1)}, u32[]{:S(2)}, u32[]{:S(2)}) collective-permute-start(f32[5,7,16,128]{3,2,1,0:T(8,128)S(1)} %get-tuple-element.37), channel_id=1, source_target_pairs={{0,1},{1,2},{2,3},{3,4},{4,5},{5,6},{6,7},{7,8},{8,9},{9,10},{10,1... | collective-permute-start | bytes 860168 | tf_op jit(solution)/shard_map/ppermute | solution.py:415
  27.3 7.7 %collective-permute-start.4 = (f32[5,16,128]{2,1,0:T(8,128)S(1)}, f32[5,16,128]{2,1,0:T(8,128)S(1)}, u32[]{:S(2)}, u32[]{:S(2)}) collective-permute-start(f32[5,16,128]{2,1,0:T(8,128)S(1)} %get-tuple-element.40), channel_id=1, source_target_pairs={{0,14},{1,15},{2,0},{3,1},{4,2},{5,3},{6,4},{7,5},{8,6},{9,7},{10,... | collective-permute-start | bytes 122888 | tf_op jit(solution)/shard_map/ppermute | solution.py:415
  31.7 7.2 %collective-permute-start.5 = (f32[5,16,128]{2,1,0:T(8,128)S(1)}, f32[5,16,128]{2,1,0:T(8,128)S(1)}, u32[]{:S(2)}, u32[]{:S(2)}) collective-permute-start(f32[5,16,128]{2,1,0:T(8,128)S(1)} %get-tuple-element.41), channel_id=1, source_target_pairs={{0,2},{1,3},{2,4},{3,5},{4,6},{5,7},{6,8},{7,9},{8,10},{9,11},{10,... | collective-permute-start | bytes 122888 | tf_op jit(solution)/shard_map/ppermute | solution.py:415
  39.4 15.8 %collective-permute-start.6 = (f32[480,128]{1,0:T(8,128)S(1)}, f32[480,128]{1,0:T(8,128)S(1)}, u32[]{:S(2)}, u32[]{:S(2)}) collective-permute-start(f32[480,128]{1,0:T(8,128)S(1)} %get-tuple-element.44), channel_id=1, source_target_pairs={{0,896},{128,0},{256,128},{384,256},{512,384},{640,512},{768,640},... | collective-permute-start | bytes 737288 | tf_op jit(solution)/shard_map/ppermute | solution.py:415
  45.5 9.6 %collective-permute-start.7 = (f32[400,128]{1,0:T(8,128)S(1)}, f32[400,128]{1,0:T(8,128)S(1)}, u32[]{:S(2)}, u32[]{:S(2)}) collective-permute-start(f32[400,128]{1,0:T(8,128)S(1)} %get-tuple-element.45), channel_id=1, source_target_pairs={{0,128},{128,256},{256,384},{384,512},{512,640},{640,768},{768,896... | collective-permute-start | bytes 614408 | tf_op jit(solution)/shard_map/ppermute | solution.py:415
  47.5 9.5 %collective-permute-start.8 = (f32[40,128]{1,0:T(8,128)S(1)}, f32[40,128]{1,0:T(8,128)S(1)}, u32[]{:S(2)}, u32[]{:S(2)}) collective-permute-start(f32[40,128]{1,0:T(8,128)S(1)} %get-tuple-element.49), channel_id=1, source_target_pairs={{0,768},{128,896},{256,0},{384,128},{512,256},{640,384},{768,512},... | collective-permute-start | bytes 61448 | tf_op jit(solution)/shard_map/ppermute | solution.py:415
  52.1 7.8 %collective-permute-start.9 = (f32[40,128]{1,0:T(8,128)S(1)}, f32[40,128]{1,0:T(8,128)S(1)}, u32[]{:S(2)}, u32[]{:S(2)}) collective-permute-start(f32[40,128]{1,0:T(8,128)S(1)} %get-tuple-element.50), channel_id=1, source_target_pairs={{0,256},{128,384},{256,512},{384,640},{512,768},{640,896},{768,0},... | collective-permute-start | bytes 61448 | tf_op jit(solution)/shard_map/ppermute | solution.py:415
  61.7 25.1 %copy-start = (f32[32,32]{1,0:T(8,128)S(1)}, f32[32,32]{1,0:T(8,128)}, u32[]{:S(2)}) copy-start(f32[32,32]{1,0:T(8,128)} %constant.8.clone) | copy-start | bytes 12292
  61.7 38.4 %all-to-all-start = ((f32[64,32,128]{2,1,0:T(8,128)}), f32[64,32,128]{2,1,0:T(8,128)S(1)}, u32[]{:S(2)}, u32[]{:S(2)}) async-start(f32[64,32,128]{2,1,0:T(8,128)} %bitcast.7), calls=%async_computation | async-start | bytes 2097152 | tf_op jit(solution)/shard_map/all_to_all | solution.py:501

commit v7 on v6

--- a/solution.py
+++ b/solution.py
@@ -188,18 +188,12 @@
     return row * 2 + jnp.sum(equal, axis=0, keepdims=True)
 
 
-def own_y_kernel(writers, fields, maps, own, outbox, targets, zeros, sems):
-    zeros[...] = jnp.zeros_like(zeros)
-    copies = [pltpu.make_async_copy(zeros, outbox.at[pl.ds(i * 512, 512)], sems.at[i]) for i in range(4)]
-    for copy in copies:
-        copy.start()
+def own_y_kernel(writers, fields, maps, own, targets):
     cells_hi, cells_lo = halves(fields[...])
     dims = ((1,), (0,))
     own_hi, own_lo = maps[:128], maps[128:256]
     own[...] = dot(cells_hi, own_hi, dims) + dot(cells_lo, own_hi, dims) + dot(cells_hi, own_lo, dims)
     targets[...] = slots_of(writers[...].astype(jnp.float32)).astype(jnp.int32)
-    for copy in copies:
-        copy.wait()
 
 
 def share_z_kernel(
@@ -309,17 +303,8 @@
         to_high_far[rows] = far_high
 
 
-def tile_copies(targets, tiles, outbox, sems, first):
-    copies = []
-    for i in range(TILES // 2):
-        t = 2 * i + first
-        to = pl.multiple_of(targets[t] * 16, 16)
-        copies.append(pltpu.make_async_copy(tiles.at[pl.ds(t * 16, 16)], outbox.at[pl.ds(to, 16)], sems.at[i]))
-    return copies
-
-
-def tiles_kernel(targets, fine, from_high, from_low, cleared, tiles, outbox, sems):
-    del cleared
+def tiles_kernel(targets, fine, from_high, from_low, tiles, outbox):
+    outbox[...] = jnp.zeros_like(outbox)
     for g in range(10):
         rows = slice(g * 8, g * 8 + 8)
         for x in range(NB):
@@ -330,19 +315,16 @@
                 i = x - 12
                 row = row + from_high[i * 80 + g * 8 : i * 80 + g * 8 + 8]
             tiles[pl.ds(g * 128 + x, 8, stride=16), :] = row
-    copies = tile_copies(targets, tiles, outbox, sems, 1)
-    for copy in copies:
-        copy.start()
-    for copy in copies:
-        copy.wait()
+    for t in range(1, TILES, 2):
+        to = pl.multiple_of(targets[t] * 16, 16)
+        outbox[pl.ds(to, 16), :] = tiles[t * 16 : t * 16 + 16]
 
 
 def route_kernel(
     targets, tiles, coarse, from_high, from_low, from_high_far, from_low_far, filled,
-    outbox, low_rows, spread, whole, sems,
+    outbox, filling, low_rows, spread, sems,
 ):
     del filled
-    copies = tile_copies(targets, whole, outbox, sems, 0)
     shape = (8, LN)
     lanes = Lanes()
     even_row = lax.broadcasted_iota(jnp.int32, shape, 0) % 2 == 0
@@ -366,13 +348,19 @@
                 spread[pl.ds(g * 128 + 2 * x + odd, 8, stride=16), :] = row
         for z in range(0, NB, 2):
             t = g * NB + z
+            to = pl.multiple_of(targets[t] * 16, 16)
             for half in (0, 8):
                 at = (g * 8 + z // 2) * 16 + half
-                here = slice(t * 16 + half, t * 16 + half + 8)
-                whole[here] = jnp.where(merged, spread[at : at + 8], tiles[here])
-            copies[t // 2].start()
+                row = jnp.where(merged, spread[at : at + 8], tiles[t * 16 + half : t * 16 + half + 8])
+                filling[pl.ds(to + half, 8), :] = row
         low_rows[g * 8 : g * 8 + 8] = added[0]
         low_rows[40 + g * 8 : 40 + g * 8 + 8] = added[4]
+    copies = []
+    for i in range(4):
+        rows = pl.ds(i * 512, 512)
+        copies.append(pltpu.make_async_copy(filling.at[rows], outbox.at[rows], sems.at[i]))
+    for copy in copies:
+        copy.start()
     for copy in copies:
         copy.wait()
 
@@ -437,12 +425,10 @@
         [HB, HB, HB, HB],
         grant=32 << 20,
     )
-    own, outbox, targets = call(
+    own, targets = call(
         own_y_kernel,
-        [f32(ROWS, 2 * LN), f32(2048, LN), jax.ShapeDtypeStruct((1, TILES), jnp.int32)],
+        [f32(ROWS, 2 * LN), jax.ShapeDtypeStruct((1, TILES), jnp.int32)],
         [writers, cells, maps],
-        [pltpu.VMEM((512, LN), jnp.float32), pltpu.SemaphoreType.DMA((4,))],
-        out_specs=[VM, HB, VM],
         flops=1 << 30,
     )
     from_high = shift(to_low, "gy", -1)
@@ -479,24 +465,21 @@
     from_low_far = shift(to_high_far, "gx", 2)
 
     targets = targets.reshape(TILES)
-    tiles, outbox = call(
+    tiles, filling = call(
         tiles_kernel,
         [f32(ROWS, LN), f32(2048, LN)],
-        [targets, fine, from_high, from_low, outbox],
-        [pltpu.SemaphoreType.DMA((TILES // 2,))],
-        [SM, VM, VM, VM, HB],
-        [VM, HB],
+        [targets, fine, from_high, from_low],
+        specs=[SM, VM, VM, VM],
         flops=1 << 30,
-        aliases={4: 1},
-    )
-    outbox, low_rows = call(
+    )
+    outbox, _, low_rows = call(
         route_kernel,
-        [f32(2048, LN), f32(80, LN)],
-        [targets, tiles, coarse, from_high, from_low, from_high_far, from_low_far, outbox],
-        [pltpu.VMEM((640, LN), jnp.float32), pltpu.VMEM((ROWS, LN), jnp.float32), pltpu.SemaphoreType.DMA((TILES // 2,))],
-        [SM] + [VM] * 6 + [HB],
-        [HB, VM],
-        aliases={7: 0},
+        [f32(2048, LN), f32(2048, LN), f32(80, LN)],
+        [targets, tiles, coarse, from_high, from_low, from_high_far, from_low_far, filling],
+        [pltpu.VMEM((640, LN), jnp.float32), pltpu.SemaphoreType.DMA((4,))],
+        [SM] + [VM] * 7,
+        [HB, VM, VM],
+        aliases={7: 1},
     )
     inbox = lax.all_to_all(outbox.reshape(64, 32, LN), ("gx", "gy"), split_axis=0, concat_axis=0, tiled=True)
 

time: 102 us -> 102 us (level)
  Pallas kernels: 9.8 us -> 7.84 us
  waiting for transfers between devices: 21.3 us -> 23.2 us
    pallas_call x8, Pallas kernels: 9.8 us -> 7.84 us  [call(): pl.pallas_call(kernel, out_shape=list(outs), in_specs=specs or [VM] * len...]
    ppermute x10, waiting for transfers between devices: 8.99 us -> 10.9 us  [shift(): lax.ppermute(array, axis, [(i, (i + by) % count) for i in range(count)])]
  transfers between devices with their start and end apart: 11 -> 11, of which waited for: 6 -> 6; matrix products, arithmetic and copies ran while one was open for 1% -> 1% of each run, Pallas kernels for 4% -> 2%
where the time goes in v7:
time: 102 us; the launch traced here: 101 us
  starting transfers between devices  52.7 us (52%)
  waiting for transfers between devices  23.2 us (23%)
  blocking collectives  14.2 us (14%)
  Pallas kernels  7.84 us (8%)
  local copies, waits for them, and re-layouts  1.34 us (1%)
    ppermute x10, starting transfers between devices, shift(): lax.ppermute(array, axis, [(i, (i + by) % count) for i in range(count)])  42.3 us
    all_gather x1, blocking collectives, body(): band = lax.all_gather(band, 'gz', axis=0, tiled=True)  14.2 us
    all_to_all x1, waiting for transfers between devices, body(): lax.all_to_all(outbox.reshape(64, 32, LN), ('gx', 'gy'), split_axis=0, co...  12.3 us
    ppermute x10, waiting for transfers between devices, shift(): lax.ppermute(array, axis, [(i, (i + by) % count) for i in range(count)])  10.9 us
    all_to_all x1, starting transfers between devices, body(): lax.all_to_all(outbox.reshape(64, 32, LN), ('gx', 'gy'), split_axis=0, co...  10.5 us
    pallas_call x8, Pallas kernels, call(): pl.pallas_call(kernel, out_shape=list(outs), in_specs=specs or [VM] * len...  7.84 us
  transfers between devices with their start and end apart: 11, of which 6 were waited for; matrix products, arithmetic and copies ran while one was open for 1% of the time, Pallas kernels for 2%

profile of v7, /device:TPU:2, one launch (start us, length us, event | category | flops | bytes accessed | tf_op | source)
XLA Modules:
  0.0 101.2 jit_solution(14950671063583887022)
XLA Ops:
  0.6 1.9 %shard_map.68 = (f32[16,1280]{1,0:T(8,128)S(1)}, f32[16,1280]{1,0:T(8,128)S(1)}, f32[1280,128]{1,0:T(8,128)S(1)}, bf16[288,256]{1,0:T(8,128)(2,1)S(1)}, s32[1,80]{1,0:T(1,128)S(1)}) custom-call(f32[1280,128]{1,0:T(8,128)} %bitcast.16, bf16[64,128]{1,0:T(8,128)(2,1)} %constant.6.clone.send, bf16[288,256]{1,0:T(8,128)(2,1)} %constant.7.clone.maps, ...), custom_call_target="tpu_custom_call" | custom-call | flops 1048576 | bytes 2097792 | tf_op jit(solution)/shard_map/pallas_call | solution.py:389
  2.6 3.4 %collective-permute-start = (f32[16,1280]{1,0:T(8,128)S(1)}, f32[16,1280]{1,0:T(8,128)S(1)}, u32[]{:S(2)}, u32[]{:S(2)}) collective-permute-start(f32[16,1280]{1,0:T(8,128)S(1)} %get-tuple-element.32), channel_id=1, source_target_pairs={{0,16},{16,32},{32,48},{48,64},{64,80},{80,96},{96,112},{112,0},{1... | collective-permute-start | bytes 245768 | tf_op jit(solution)/shard_map/ppermute | solution.py:403
  6.0 13.6 %collective-permute-start.1 = (f32[16,1280]{1,0:T(8,128)S(1)}, f32[16,1280]{1,0:T(8,128)S(1)}, u32[]{:S(2)}, u32[]{:S(2)}) collective-permute-start(f32[16,1280]{1,0:T(8,128)S(1)} %get-tuple-element.33), channel_id=1, source_target_pairs={{0,112},{16,0},{32,16},{48,32},{64,48},{80,64},{96,80},{112,96},{1... | collective-permute-start | bytes 245768 | tf_op jit(solution)/shard_map/ppermute | solution.py:403
  19.6 0.7 shard_map.69
  20.3 0.0 collective-permute-done.from_low
  20.3 1.4 %collective-permute-done.1.from_high = f32[16,1280]{1,0:T(8,128)S(1)} collective-permute-done((f32[16,1280]{1,0:T(8,128)S(1)}, f32[16,1280]{1,0:T(8,128)S(1)}, u32[]{:S(2)}, u32[]{:S(2)}) %collective-permute-start.1) | collective-permute-done | bytes 81952 | tf_op jit(solution)/shard_map/ppermute | solution.py:403
  21.6 1.5 %shard_map.70 = (f32[1280,128]{1,0:T(8,128)S(1)}, f32[640,128]{1,0:T(8,128)S(1)}, f32[5,8,16,128]{3,2,1,0:T(8,128)S(1)}, f32[5,7,16,128]{3,2,1,0:T(8,128)S(1)}, ...) custom-call(f32[1280,256]{1,0:T(8,128)S(1)} %get-tuple-element.31.own, bf16[288,256]{1,0:T(8,128)(2,1)S(1)} %get-tuple-element.29.maps, ...), custom_call_target="tpu_custom_call" | custom-call | flops 1048576 | bytes 3448832 | tf_op jit(solution)/shard_map/pallas_call | solution.py:389
  23.2 4.1 %collective-permute-start.2 = (f32[5,8,16,128]{3,2,1,0:T(8,128)S(1)}, f32[5,8,16,128]{3,2,1,0:T(8,128)S(1)}, u32[]{:S(2)}, u32[]{:S(2)}) collective-permute-start(f32[5,8,16,128]{3,2,1,0:T(8,128)S(1)} %get-tuple-element.35), channel_id=1, source_target_pairs={{0,15},{1,0},{2,1},{3,2},{4,3},{5,4},{6,5},{7,6},{8,7},{9,8},{10,9... | collective-permute-start | bytes 983048 | tf_op jit(solution)/shard_map/ppermute | solution.py:403
  27.3 0.0 collective-permute-start.3
  27.3 4.4 %collective-permute-start.4 = (f32[5,16,128]{2,1,0:T(8,128)S(1)}, f32[5,16,128]{2,1,0:T(8,128)S(1)}, u32[]{:S(2)}, u32[]{:S(2)}) collective-permute-start(f32[5,16,128]{2,1,0:T(8,128)S(1)} %get-tuple-element.39), channel_id=1, source_target_pairs={{0,14},{1,15},{2,0},{3,1},{4,2},{5,3},{6,4},{7,5},{8,6},{9,7},{10,... | collective-permute-start | bytes 122888 | tf_op jit(solution)/shard_map/ppermute | solution.py:403
  31.7 1.9 %collective-permute-start.5 = (f32[5,16,128]{2,1,0:T(8,128)S(1)}, f32[5,16,128]{2,1,0:T(8,128)S(1)}, u32[]{:S(2)}, u32[]{:S(2)}) collective-permute-start(f32[5,16,128]{2,1,0:T(8,128)S(1)} %get-tuple-element.40), channel_id=1, source_target_pairs={{0,2},{1,3},{2,4},{3,5},{4,6},{5,7},{6,8},{7,9},{8,10},{9,11},{10,... | collective-permute-start | bytes 122888 | tf_op jit(solution)/shard_map/ppermute | solution.py:403
  33.6 0.9 collective-permute-done.3.from_low
  34.5 0.0 collective-permute-done.2.from_high
  34.6 0.4 shard_map.71
  35.0 0.0 collective-permute-done.4.from_high_far
  35.0 3.8 %collective-permute-done.5.from_low_far = f32[5,16,128]{2,1,0:T(8,128)S(1)} collective-permute-done((f32[5,16,128]{2,1,0:T(8,128)S(1)}, f32[5,16,128]{2,1,0:T(8,128)S(1)}, u32[]{:S(2)}, u32[]{:S(2)}) %collective-permute-start.5) | collective-permute-done | bytes 40992 | tf_op jit(solution)/shard_map/ppermute | solution.py:403
  38.8 0.5 shard_map.72
  39.4 6.2 %collective-permute-start.6 = (f32[480,128]{1,0:T(8,128)S(1)}, f32[480,128]{1,0:T(8,128)S(1)}, u32[]{:S(2)}, u32[]{:S(2)}) collective-permute-start(f32[480,128]{1,0:T(8,128)S(1)} %get-tuple-element.43), channel_id=1, source_target_pairs={{0,896},{128,0},{256,128},{384,256},{512,384},{640,512},{768,640},... | collective-permute-start | bytes 737288 | tf_op jit(solution)/shard_map/ppermute | solution.py:403
  45.5 1.9 %collective-permute-start.7 = (f32[400,128]{1,0:T(8,128)S(1)}, f32[400,128]{1,0:T(8,128)S(1)}, u32[]{:S(2)}, u32[]{:S(2)}) collective-permute-start(f32[400,128]{1,0:T(8,128)S(1)} %get-tuple-element.44), channel_id=1, source_target_pairs={{0,128},{128,256},{256,384},{384,512},{512,640},{640,768},{768,896... | collective-permute-start | bytes 614408 | tf_op jit(solution)/shard_map/ppermute | solution.py:403
  47.5 4.6 %collective-permute-start.8 = (f32[40,128]{1,0:T(8,128)S(1)}, f32[40,128]{1,0:T(8,128)S(1)}, u32[]{:S(2)}, u32[]{:S(2)}) collective-permute-start(f32[40,128]{1,0:T(8,128)S(1)} %get-tuple-element.47), channel_id=1, source_target_pairs={{0,768},{128,896},{256,0},{384,128},{512,256},{640,384},{768,512},... | collective-permute-start | bytes 61448 | tf_op jit(solution)/shard_map/ppermute | solution.py:403
  52.1 2.1 %collective-permute-start.9 = (f32[40,128]{1,0:T(8,128)S(1)}, f32[40,128]{1,0:T(8,128)S(1)}, u32[]{:S(2)}, u32[]{:S(2)}) collective-permute-start(f32[40,128]{1,0:T(8,128)S(1)} %get-tuple-element.48), channel_id=1, source_target_pairs={{0,256},{128,384},{256,512},{384,640},{512,768},{640,896},{768,0},... | collective-permute-start | bytes 61448 | tf_op jit(solution)/shard_map/ppermute | solution.py:403
  54.2 0.9 collective-permute-done.7.from_low
  55.1 0.0 collective-permute-done.6.from_high
  55.2 0.8 shard_map.73
  56.0 0.0 collective-permute-done.8.from_high_far
  56.0 3.9 %collective-permute-done.9.from_low_far = f32[40,128]{1,0:T(8,128)S(1)} collective-permute-done((f32[40,128]{1,0:T(8,128)S(1)}, f32[40,128]{1,0:T(8,128)S(1)}, u32[]{:S(2)}, u32[]{:S(2)}) %collective-permute-start.9) | collective-permute-done | bytes 20512 | tf_op jit(solution)/shard_map/ppermute | solution.py:403
  59.9 1.8 %shard_map.74 = (f32[2048,128]{1,0:T(8,128)}, f32[2048,128]{1,0:T(8,128)S(1)}, f32[80,128]{1,0:T(8,128)S(1)}) custom-call(s32[80]{0:T(128)S(1)} %bitcast.15, f32[1280,128]{1,0:T(8,128)S(1)} %get-tuple-element.45.tiles, f32[8,40,128]{2,1,0:T(8,128)S(1)} %get-tuple-element.46.coarse, ...), custom_call_target="tpu_custom_call", output_to_operand_aliasing={{1}: (7, {})} | custom-call | flops 1048576 | bytes 4497728 | tf_op jit(solution)/shard_map/pallas_call | solution.py:389
  61.6 0.0 copy-start
  61.6 10.5 %all-to-all-start = ((f32[64,32,128]{2,1,0:T(8,128)}), f32[64,32,128]{2,1,0:T(8,128)S(1)}, u32[]{:S(2)}, u32[]{:S(2)}) async-start(f32[64,32,128]{2,1,0:T(8,128)} %bitcast.7), calls=%async_computation | async-start | bytes 2097152 | tf_op jit(solution)/shard_map/all_to_all | solution.py:484
  72.1 0.2 shard_map.75
  72.3 0.1 slice.3
  72.4 0.1 reshape.36
  72.5 14.2 %all-gather = f32[16,2,160]{2,1,0:T(2,128)S(1)} all-gather(f32[1,2,160]{2,1,0:T(2,128)S(1)} %reshape.36), channel_id=1, replica_groups=mesh['gx'=8,'gy'=8,'gz'=16] {'gz'}, dimensions={0}, use_global_device_ids=true | all-gather | bytes 21760 | tf_op jit(solution)/shard_map/all_gather | solution.py:488
  86.7 0.0 copy-done
  86.8 1.0 fusion
  87.7 12.3 %all-to-all-done = f32[64,32,128]{2,1,0:T(8,128)S(1)} async-done(((f32[64,32,128]{2,1,0:T(8,128)}), f32[64,32,128]{2,1,0:T(8,128)S(1)}, u32[]{:S(2)}, u32[]{:S(2)}) %all-to-all-start) | async-done | bytes 1048608 | tf_op jit(solution)/shard_map/all_to_all | solution.py:484
  100.0 1.1 %reshape.35 = f32[128,2048]{1,0:T(8,128)} reshape(f32[64,32,128]{2,1,0:T(8,128)S(1)} %all-to-all-done) | data formatting | bytes 2097152 | tf_op jit(solution)/shard_map/reshape | solution.py:492
  (2 shorter events, 0.0 us)
Async XLA Ops:
  2.6 17.7 %collective-permute-start = (f32[16,1280]{1,0:T(8,128)S(1)}, f32[16,1280]{1,0:T(8,128)S(1)}, u32[]{:S(2)}, u32[]{:S(2)}) collective-permute-start(f32[16,1280]{1,0:T(8,128)S(1)} %get-tuple-element.32), channel_id=1, source_target_pairs={{0,16},{16,32},{32,48},{48,64},{64,80},{80,96},{96,112},{112,0},{1... | collective-permute-start | bytes 245768 | tf_op jit(solution)/shard_map/ppermute | solution.py:403
  6.0 15.7 %collective-permute-start.1 = (f32[16,1280]{1,0:T(8,128)S(1)}, f32[16,1280]{1,0:T(8,128)S(1)}, u32[]{:S(2)}, u32[]{:S(2)}) collective-permute-start(f32[16,1280]{1,0:T(8,128)S(1)} %get-tuple-element.33), channel_id=1, source_target_pairs={{0,112},{16,0},{32,16},{48,32},{64,48},{80,64},{96,80},{112,96},{1... | collective-permute-start | bytes 245768 | tf_op jit(solution)/shard_map/ppermute | solution.py:403
  23.2 11.4 %collective-permute-start.2 = (f32[5,8,16,128]{3,2,1,0:T(8,128)S(1)}, f32[5,8,16,128]{3,2,1,0:T(8,128)S(1)}, u32[]{:S(2)}, u32[]{:S(2)}) collective-permute-start(f32[5,8,16,128]{3,2,1,0:T(8,128)S(1)} %get-tuple-element.35), channel_id=1, source_target_pairs={{0,15},{1,0},{2,1},{3,2},{4,3},{5,4},{6,5},{7,6},{8,7},{9,8},{10,9... | collective-permute-start | bytes 983048 | tf_op jit(solution)/shard_map/ppermute | solution.py:403
  27.3 7.3 %collective-permute-start.3 = (f32[5,7,16,128]{3,2,1,0:T(8,128)S(1)}, f32[5,7,16,128]{3,2,1,0:T(8,128)S(1)}, u32[]{:S(2)}, u32[]{:S(2)}) collective-permute-start(f32[5,7,16,128]{3,2,1,0:T(8,128)S(1)} %get-tuple-element.36), channel_id=1, source_target_pairs={{0,1},{1,2},{2,3},{3,4},{4,5},{5,6},{6,7},{7,8},{8,9},{9,10},{10,1... | collective-permute-start | bytes 860168 | tf_op jit(solution)/shard_map/ppermute | solution.py:403
  27.3 7.7 %collective-permute-start.4 = (f32[5,16,128]{2,1,0:T(8,128)S(1)}, f32[5,16,128]{2,1,0:T(8,128)S(1)}, u32[]{:S(2)}, u32[]{:S(2)}) collective-permute-start(f32[5,16,128]{2,1,0:T(8,128)S(1)} %get-tuple-element.39), channel_id=1, source_target_pairs={{0,14},{1,15},{2,0},{3,1},{4,2},{5,3},{6,4},{7,5},{8,6},{9,7},{10,... | collective-permute-start | bytes 122888 | tf_op jit(solution)/shard_map/ppermute | solution.py:403
  31.7 7.2 %collective-permute-start.5 = (f32[5,16,128]{2,1,0:T(8,128)S(1)}, f32[5,16,128]{2,1,0:T(8,128)S(1)}, u32[]{:S(2)}, u32[]{:S(2)}) collective-permute-start(f32[5,16,128]{2,1,0:T(8,128)S(1)} %get-tuple-element.40), channel_id=1, source_target_pairs={{0,2},{1,3},{2,4},{3,5},{4,6},{5,7},{6,8},{7,9},{8,10},{9,11},{10,... | collective-permute-start | bytes 122888 | tf_op jit(solution)/shard_map/ppermute | solution.py:403
  39.4 15.8 %collective-permute-start.6 = (f32[480,128]{1,0:T(8,128)S(1)}, f32[480,128]{1,0:T(8,128)S(1)}, u32[]{:S(2)}, u32[]{:S(2)}) collective-permute-start(f32[480,128]{1,0:T(8,128)S(1)} %get-tuple-element.43), channel_id=1, source_target_pairs={{0,896},{128,0},{256,128},{384,256},{512,384},{640,512},{768,640},... | collective-permute-start | bytes 737288 | tf_op jit(solution)/shard_map/ppermute | solution.py:403
  45.5 9.6 %collective-permute-start.7 = (f32[400,128]{1,0:T(8,128)S(1)}, f32[400,128]{1,0:T(8,128)S(1)}, u32[]{:S(2)}, u32[]{:S(2)}) collective-permute-start(f32[400,128]{1,0:T(8,128)S(1)} %get-tuple-element.44), channel_id=1, source_target_pairs={{0,128},{128,256},{256,384},{384,512},{512,640},{640,768},{768,896... | collective-permute-start | bytes 614408 | tf_op jit(solution)/shard_map/ppermute | solution.py:403
  47.5 8.5 %collective-permute-start.8 = (f32[40,128]{1,0:T(8,128)S(1)}, f32[40,128]{1,0:T(8,128)S(1)}, u32[]{:S(2)}, u32[]{:S(2)}) collective-permute-start(f32[40,128]{1,0:T(8,128)S(1)} %get-tuple-element.47), channel_id=1, source_target_pairs={{0,768},{128,896},{256,0},{384,128},{512,256},{640,384},{768,512},... | collective-permute-start | bytes 61448 | tf_op jit(solution)/shard_map/ppermute | solution.py:403
  52.1 7.8 %collective-permute-start.9 = (f32[40,128]{1,0:T(8,128)S(1)}, f32[40,128]{1,0:T(8,128)S(1)}, u32[]{:S(2)}, u32[]{:S(2)}) collective-permute-start(f32[40,128]{1,0:T(8,128)S(1)} %get-tuple-element.48), channel_id=1, source_target_pairs={{0,256},{128,384},{256,512},{384,640},{512,768},{640,896},{768,0},... | collective-permute-start | bytes 61448 | tf_op jit(solution)/shard_map/ppermute | solution.py:403
  61.6 25.1 %copy-start = (f32[32,32]{1,0:T(8,128)S(1)}, f32[32,32]{1,0:T(8,128)}, u32[]{:S(2)}) copy-start(f32[32,32]{1,0:T(8,128)} %constant.8.clone) | copy-start | bytes 12292
  61.6 38.4 %all-to-all-start = ((f32[64,32,128]{2,1,0:T(8,128)}), f32[64,32,128]{2,1,0:T(8,128)S(1)}, u32[]{:S(2)}, u32[]{:S(2)}) async-start(f32[64,32,128]{2,1,0:T(8,128)} %bitcast.7), calls=%async_computation | async-start | bytes 2097152 | tf_op jit(solution)/shard_map/all_to_all | solution.py:484

commit v8 on v7

--- a/solution.py
+++ b/solution.py
@@ -356,8 +356,8 @@
         low_rows[g * 8 : g * 8 + 8] = added[0]
         low_rows[40 + g * 8 : 40 + g * 8 + 8] = added[4]
     copies = []
-    for i in range(4):
-        rows = pl.ds(i * 512, 512)
+    for i in range(16):
+        rows = pl.ds(i * 128, 128)
         copies.append(pltpu.make_async_copy(filling.at[rows], outbox.at[rows], sems.at[i]))
     for copy in copies:
         copy.start()
@@ -476,7 +476,7 @@
         route_kernel,
         [f32(2048, LN), f32(2048, LN), f32(80, LN)],
         [targets, tiles, coarse, from_high, from_low, from_high_far, from_low_far, filling],
-        [pltpu.VMEM((640, LN), jnp.float32), pltpu.SemaphoreType.DMA((4,))],
+        [pltpu.VMEM((640, LN), jnp.float32), pltpu.SemaphoreType.DMA((16,))],
         [SM] + [VM] * 7,
         [HB, VM, VM],
         aliases={7: 1},

time: 102 us -> 102 us (level)
  no operation moved by 1% of the time
where the time goes in v8:
time: 102 us; the launch traced here: 101 us
  starting transfers between devices  52.7 us (52%)
  waiting for transfers between devices  23.2 us (23%)
  blocking collectives  14.2 us (14%)
  Pallas kernels  7.94 us (8%)
  local copies, waits for them, and re-layouts  1.34 us (1%)
    ppermute x10, starting transfers between devices, shift(): lax.ppermute(array, axis, [(i, (i + by) % count) for i in range(count)])  42.3 us
    all_gather x1, blocking collectives, body(): band = lax.all_gather(band, 'gz', axis=0, tiled=True)  14.2 us
    all_to_all x1, waiting for transfers between devices, body(): lax.all_to_all(outbox.reshape(64, 32, LN), ('gx', 'gy'), split_axis=0, co...  12.3 us
    ppermute x10, waiting for transfers between devices, shift(): lax.ppermute(array, axis, [(i, (i + by) % count) for i in range(count)])  10.9 us
    all_to_all x1, starting transfers between devices, body(): lax.all_to_all(outbox.reshape(64, 32, LN), ('gx', 'gy'), split_axis=0, co...  10.5 us
    pallas_call x8, Pallas kernels, call(): pl.pallas_call(kernel, out_shape=list(outs), in_specs=specs or [VM] * len...  7.94 us
  transfers between devices with their start and end apart: 11, of which 6 were waited for; matrix products, arithmetic and copies ran while one was open for 1% of the time, Pallas kernels for 2%

profile of v8, /device:TPU:2, one launch (start us, length us, event | category | flops | bytes accessed | tf_op | source)
XLA Modules:
  0.0 101.3 jit_solution(10438700668365810756)
XLA Ops:
  0.6 1.9 %shard_map.68 = (f32[16,1280]{1,0:T(8,128)S(1)}, f32[16,1280]{1,0:T(8,128)S(1)}, f32[1280,128]{1,0:T(8,128)S(1)}, bf16[288,256]{1,0:T(8,128)(2,1)S(1)}, s32[1,80]{1,0:T(1,128)S(1)}) custom-call(f32[1280,128]{1,0:T(8,128)} %bitcast.16, bf16[64,128]{1,0:T(8,128)(2,1)} %constant.6.clone.send, bf16[288,256]{1,0:T(8,128)(2,1)} %constant.7.clone.maps, ...), custom_call_target="tpu_custom_call" | custom-call | flops 1048576 | bytes 2097792 | tf_op jit(solution)/shard_map/pallas_call | solution.py:389
  2.6 3.4 %collective-permute-start = (f32[16,1280]{1,0:T(8,128)S(1)}, f32[16,1280]{1,0:T(8,128)S(1)}, u32[]{:S(2)}, u32[]{:S(2)}) collective-permute-start(f32[16,1280]{1,0:T(8,128)S(1)} %get-tuple-element.32), channel_id=1, source_target_pairs={{0,16},{16,32},{32,48},{48,64},{64,80},{80,96},{96,112},{112,0},{1... | collective-permute-start | bytes 245768 | tf_op jit(solution)/shard_map/ppermute | solution.py:403
  6.0 13.6 %collective-permute-start.1 = (f32[16,1280]{1,0:T(8,128)S(1)}, f32[16,1280]{1,0:T(8,128)S(1)}, u32[]{:S(2)}, u32[]{:S(2)}) collective-permute-start(f32[16,1280]{1,0:T(8,128)S(1)} %get-tuple-element.33), channel_id=1, source_target_pairs={{0,112},{16,0},{32,16},{48,32},{64,48},{80,64},{96,80},{112,96},{1... | collective-permute-start | bytes 245768 | tf_op jit(solution)/shard_map/ppermute | solution.py:403
  19.6 0.7 shard_map.69
  20.3 0.0 collective-permute-done.from_low
  20.3 1.4 %collective-permute-done.1.from_high = f32[16,1280]{1,0:T(8,128)S(1)} collective-permute-done((f32[16,1280]{1,0:T(8,128)S(1)}, f32[16,1280]{1,0:T(8,128)S(1)}, u32[]{:S(2)}, u32[]{:S(2)}) %collective-permute-start.1) | collective-permute-done | bytes 81952 | tf_op jit(solution)/shard_map/ppermute | solution.py:403
  21.6 1.5 %shard_map.70 = (f32[1280,128]{1,0:T(8,128)S(1)}, f32[640,128]{1,0:T(8,128)S(1)}, f32[5,8,16,128]{3,2,1,0:T(8,128)S(1)}, f32[5,7,16,128]{3,2,1,0:T(8,128)S(1)}, ...) custom-call(f32[1280,256]{1,0:T(8,128)S(1)} %get-tuple-element.31.own, bf16[288,256]{1,0:T(8,128)(2,1)S(1)} %get-tuple-element.29.maps, ...), custom_call_target="tpu_custom_call" | custom-call | flops 1048576 | bytes 3448832 | tf_op jit(solution)/shard_map/pallas_call | solution.py:389
  23.2 4.1 %collective-permute-start.2 = (f32[5,8,16,128]{3,2,1,0:T(8,128)S(1)}, f32[5,8,16,128]{3,2,1,0:T(8,128)S(1)}, u32[]{:S(2)}, u32[]{:S(2)}) collective-permute-start(f32[5,8,16,128]{3,2,1,0:T(8,128)S(1)} %get-tuple-element.35), channel_id=1, source_target_pairs={{0,15},{1,0},{2,1},{3,2},{4,3},{5,4},{6,5},{7,6},{8,7},{9,8},{10,9... | collective-permute-start | bytes 983048 | tf_op jit(solution)/shard_map/ppermute | solution.py:403
  27.3 0.0 collective-permute-start.3
  27.3 4.4 %collective-permute-start.4 = (f32[5,16,128]{2,1,0:T(8,128)S(1)}, f32[5,16,128]{2,1,0:T(8,128)S(1)}, u32[]{:S(2)}, u32[]{:S(2)}) collective-permute-start(f32[5,16,128]{2,1,0:T(8,128)S(1)} %get-tuple-element.39), channel_id=1, source_target_pairs={{0,14},{1,15},{2,0},{3,1},{4,2},{5,3},{6,4},{7,5},{8,6},{9,7},{10,... | collective-permute-start | bytes 122888 | tf_op jit(solution)/shard_map/ppermute | solution.py:403
  31.7 1.9 %collective-permute-start.5 = (f32[5,16,128]{2,1,0:T(8,128)S(1)}, f32[5,16,128]{2,1,0:T(8,128)S(1)}, u32[]{:S(2)}, u32[]{:S(2)}) collective-permute-start(f32[5,16,128]{2,1,0:T(8,128)S(1)} %get-tuple-element.40), channel_id=1, source_target_pairs={{0,2},{1,3},{2,4},{3,5},{4,6},{5,7},{6,8},{7,9},{8,10},{9,11},{10,... | collective-permute-start | bytes 122888 | tf_op jit(solution)/shard_map/ppermute | solution.py:403
  33.6 0.9 collective-permute-done.3.from_low
  34.5 0.0 collective-permute-done.2.from_high
  34.6 0.4 shard_map.71
  35.0 0.0 collective-permute-done.4.from_high_far
  35.0 3.8 %collective-permute-done.5.from_low_far = f32[5,16,128]{2,1,0:T(8,128)S(1)} collective-permute-done((f32[5,16,128]{2,1,0:T(8,128)S(1)}, f32[5,16,128]{2,1,0:T(8,128)S(1)}, u32[]{:S(2)}, u32[]{:S(2)}) %collective-permute-start.5) | collective-permute-done | bytes 40992 | tf_op jit(solution)/shard_map/ppermute | solution.py:403
  38.8 0.5 shard_map.72
  39.4 6.2 %collective-permute-start.6 = (f32[480,128]{1,0:T(8,128)S(1)}, f32[480,128]{1,0:T(8,128)S(1)}, u32[]{:S(2)}, u32[]{:S(2)}) collective-permute-start(f32[480,128]{1,0:T(8,128)S(1)} %get-tuple-element.43), channel_id=1, source_target_pairs={{0,896},{128,0},{256,128},{384,256},{512,384},{640,512},{768,640},... | collective-permute-start | bytes 737288 | tf_op jit(solution)/shard_map/ppermute | solution.py:403
  45.5 1.9 %collective-permute-start.7 = (f32[400,128]{1,0:T(8,128)S(1)}, f32[400,128]{1,0:T(8,128)S(1)}, u32[]{:S(2)}, u32[]{:S(2)}) collective-permute-start(f32[400,128]{1,0:T(8,128)S(1)} %get-tuple-element.44), channel_id=1, source_target_pairs={{0,128},{128,256},{256,384},{384,512},{512,640},{640,768},{768,896... | collective-permute-start | bytes 614408 | tf_op jit(solution)/shard_map/ppermute | solution.py:403
  47.5 4.6 %collective-permute-start.8 = (f32[40,128]{1,0:T(8,128)S(1)}, f32[40,128]{1,0:T(8,128)S(1)}, u32[]{:S(2)}, u32[]{:S(2)}) collective-permute-start(f32[40,128]{1,0:T(8,128)S(1)} %get-tuple-element.47), channel_id=1, source_target_pairs={{0,768},{128,896},{256,0},{384,128},{512,256},{640,384},{768,512},... | collective-permute-start | bytes 61448 | tf_op jit(solution)/shard_map/ppermute | solution.py:403
  52.1 2.1 %collective-permute-start.9 = (f32[40,128]{1,0:T(8,128)S(1)}, f32[40,128]{1,0:T(8,128)S(1)}, u32[]{:S(2)}, u32[]{:S(2)}) collective-permute-start(f32[40,128]{1,0:T(8,128)S(1)} %get-tuple-element.48), channel_id=1, source_target_pairs={{0,256},{128,384},{256,512},{384,640},{512,768},{640,896},{768,0},... | collective-permute-start | bytes 61448 | tf_op jit(solution)/shard_map/ppermute | solution.py:403
  54.2 0.9 collective-permute-done.7.from_low
  55.1 0.0 collective-permute-done.6.from_high
  55.2 0.8 shard_map.73
  56.0 0.0 collective-permute-done.8.from_high_far
  56.0 3.9 %collective-permute-done.9.from_low_far = f32[40,128]{1,0:T(8,128)S(1)} collective-permute-done((f32[40,128]{1,0:T(8,128)S(1)}, f32[40,128]{1,0:T(8,128)S(1)}, u32[]{:S(2)}, u32[]{:S(2)}) %collective-permute-start.9) | collective-permute-done | bytes 20512 | tf_op jit(solution)/shard_map/ppermute | solution.py:403
  59.9 1.9 %shard_map.74 = (f32[2048,128]{1,0:T(8,128)}, f32[2048,128]{1,0:T(8,128)S(1)}, f32[80,128]{1,0:T(8,128)S(1)}) custom-call(s32[80]{0:T(128)S(1)} %bitcast.15, f32[1280,128]{1,0:T(8,128)S(1)} %get-tuple-element.45.tiles, f32[8,40,128]{2,1,0:T(8,128)S(1)} %get-tuple-element.46.coarse, ...), custom_call_target="tpu_custom_call", output_to_operand_aliasing={{1}: (7, {})} | custom-call | flops 1048576 | bytes 4497728 | tf_op jit(solution)/shard_map/pallas_call | solution.py:389
  61.7 0.0 copy-start
  61.7 10.5 %all-to-all-start = ((f32[64,32,128]{2,1,0:T(8,128)}), f32[64,32,128]{2,1,0:T(8,128)S(1)}, u32[]{:S(2)}, u32[]{:S(2)}) async-start(f32[64,32,128]{2,1,0:T(8,128)} %bitcast.7), calls=%async_computation | async-start | bytes 2097152 | tf_op jit(solution)/shard_map/all_to_all | solution.py:484
  72.2 0.2 shard_map.75
  72.4 0.1 slice.3
  72.5 0.1 reshape.36
  72.6 14.2 %all-gather = f32[16,2,160]{2,1,0:T(2,128)S(1)} all-gather(f32[1,2,160]{2,1,0:T(2,128)S(1)} %reshape.36), channel_id=1, replica_groups=mesh['gx'=8,'gy'=8,'gz'=16] {'gz'}, dimensions={0}, use_global_device_ids=true | all-gather | bytes 21760 | tf_op jit(solution)/shard_map/all_gather | solution.py:488
  86.8 0.0 copy-done
  86.9 1.0 fusion
  87.8 12.3 %all-to-all-done = f32[64,32,128]{2,1,0:T(8,128)S(1)} async-done(((f32[64,32,128]{2,1,0:T(8,128)}), f32[64,32,128]{2,1,0:T(8,128)S(1)}, u32[]{:S(2)}, u32[]{:S(2)}) %all-to-all-start) | async-done | bytes 1048608 | tf_op jit(solution)/shard_map/all_to_all | solution.py:484
  100.1 1.1 %reshape.35 = f32[128,2048]{1,0:T(8,128)} reshape(f32[64,32,128]{2,1,0:T(8,128)S(1)} %all-to-all-done) | data formatting | bytes 2097152 | tf_op jit(solution)/shard_map/reshape | solution.py:492
  (2 shorter events, 0.0 us)
Async XLA Ops:
  2.6 17.7 %collective-permute-start = (f32[16,1280]{1,0:T(8,128)S(1)}, f32[16,1280]{1,0:T(8,128)S(1)}, u32[]{:S(2)}, u32[]{:S(2)}) collective-permute-start(f32[16,1280]{1,0:T(8,128)S(1)} %get-tuple-element.32), channel_id=1, source_target_pairs={{0,16},{16,32},{32,48},{48,64},{64,80},{80,96},{96,112},{112,0},{1... | collective-permute-start | bytes 245768 | tf_op jit(solution)/shard_map/ppermute | solution.py:403
  6.0 15.7 %collective-permute-start.1 = (f32[16,1280]{1,0:T(8,128)S(1)}, f32[16,1280]{1,0:T(8,128)S(1)}, u32[]{:S(2)}, u32[]{:S(2)}) collective-permute-start(f32[16,1280]{1,0:T(8,128)S(1)} %get-tuple-element.33), channel_id=1, source_target_pairs={{0,112},{16,0},{32,16},{48,32},{64,48},{80,64},{96,80},{112,96},{1... | collective-permute-start | bytes 245768 | tf_op jit(solution)/shard_map/ppermute | solution.py:403
  23.2 11.4 %collective-permute-start.2 = (f32[5,8,16,128]{3,2,1,0:T(8,128)S(1)}, f32[5,8,16,128]{3,2,1,0:T(8,128)S(1)}, u32[]{:S(2)}, u32[]{:S(2)}) collective-permute-start(f32[5,8,16,128]{3,2,1,0:T(8,128)S(1)} %get-tuple-element.35), channel_id=1, source_target_pairs={{0,15},{1,0},{2,1},{3,2},{4,3},{5,4},{6,5},{7,6},{8,7},{9,8},{10,9... | collective-permute-start | bytes 983048 | tf_op jit(solution)/shard_map/ppermute | solution.py:403
  27.3 7.3 %collective-permute-start.3 = (f32[5,7,16,128]{3,2,1,0:T(8,128)S(1)}, f32[5,7,16,128]{3,2,1,0:T(8,128)S(1)}, u32[]{:S(2)}, u32[]{:S(2)}) collective-permute-start(f32[5,7,16,128]{3,2,1,0:T(8,128)S(1)} %get-tuple-element.36), channel_id=1, source_target_pairs={{0,1},{1,2},{2,3},{3,4},{4,5},{5,6},{6,7},{7,8},{8,9},{9,10},{10,1... | collective-permute-start | bytes 860168 | tf_op jit(solution)/shard_map/ppermute | solution.py:403
  27.3 7.7 %collective-permute-start.4 = (f32[5,16,128]{2,1,0:T(8,128)S(1)}, f32[5,16,128]{2,1,0:T(8,128)S(1)}, u32[]{:S(2)}, u32[]{:S(2)}) collective-permute-start(f32[5,16,128]{2,1,0:T(8,128)S(1)} %get-tuple-element.39), channel_id=1, source_target_pairs={{0,14},{1,15},{2,0},{3,1},{4,2},{5,3},{6,4},{7,5},{8,6},{9,7},{10,... | collective-permute-start | bytes 122888 | tf_op jit(solution)/shard_map/ppermute | solution.py:403
  31.7 7.2 %collective-permute-start.5 = (f32[5,16,128]{2,1,0:T(8,128)S(1)}, f32[5,16,128]{2,1,0:T(8,128)S(1)}, u32[]{:S(2)}, u32[]{:S(2)}) collective-permute-start(f32[5,16,128]{2,1,0:T(8,128)S(1)} %get-tuple-element.40), channel_id=1, source_target_pairs={{0,2},{1,3},{2,4},{3,5},{4,6},{5,7},{6,8},{7,9},{8,10},{9,11},{10,... | collective-permute-start | bytes 122888 | tf_op jit(solution)/shard_map/ppermute | solution.py:403
  39.4 15.8 %collective-permute-start.6 = (f32[480,128]{1,0:T(8,128)S(1)}, f32[480,128]{1,0:T(8,128)S(1)}, u32[]{:S(2)}, u32[]{:S(2)}) collective-permute-start(f32[480,128]{1,0:T(8,128)S(1)} %get-tuple-element.43), channel_id=1, source_target_pairs={{0,896},{128,0},{256,128},{384,256},{512,384},{640,512},{768,640},... | collective-permute-start | bytes 737288 | tf_op jit(solution)/shard_map/ppermute | solution.py:403
  45.5 9.6 %collective-permute-start.7 = (f32[400,128]{1,0:T(8,128)S(1)}, f32[400,128]{1,0:T(8,128)S(1)}, u32[]{:S(2)}, u32[]{:S(2)}) collective-permute-start(f32[400,128]{1,0:T(8,128)S(1)} %get-tuple-element.44), channel_id=1, source_target_pairs={{0,128},{128,256},{256,384},{384,512},{512,640},{640,768},{768,896... | collective-permute-start | bytes 614408 | tf_op jit(solution)/shard_map/ppermute | solution.py:403
  47.5 8.5 %collective-permute-start.8 = (f32[40,128]{1,0:T(8,128)S(1)}, f32[40,128]{1,0:T(8,128)S(1)}, u32[]{:S(2)}, u32[]{:S(2)}) collective-permute-start(f32[40,128]{1,0:T(8,128)S(1)} %get-tuple-element.47), channel_id=1, source_target_pairs={{0,768},{128,896},{256,0},{384,128},{512,256},{640,384},{768,512},... | collective-permute-start | bytes 61448 | tf_op jit(solution)/shard_map/ppermute | solution.py:403
  52.1 7.8 %collective-permute-start.9 = (f32[40,128]{1,0:T(8,128)S(1)}, f32[40,128]{1,0:T(8,128)S(1)}, u32[]{:S(2)}, u32[]{:S(2)}) collective-permute-start(f32[40,128]{1,0:T(8,128)S(1)} %get-tuple-element.48), channel_id=1, source_target_pairs={{0,256},{128,384},{256,512},{384,640},{512,768},{640,896},{768,0},... | collective-permute-start | bytes 61448 | tf_op jit(solution)/shard_map/ppermute | solution.py:403
  61.7 25.1 %copy-start = (f32[32,32]{1,0:T(8,128)S(1)}, f32[32,32]{1,0:T(8,128)}, u32[]{:S(2)}) copy-start(f32[32,32]{1,0:T(8,128)} %constant.8.clone) | copy-start | bytes 12292
  61.7 38.4 %all-to-all-start = ((f32[64,32,128]{2,1,0:T(8,128)}), f32[64,32,128]{2,1,0:T(8,128)S(1)}, u32[]{:S(2)}, u32[]{:S(2)}) async-start(f32[64,32,128]{2,1,0:T(8,128)} %bitcast.7), calls=%async_computation | async-start | bytes 2097152 | tf_op jit(solution)/shard_map/all_to_all | solution.py:484

commit v9 on v7

--- a/solution.py
+++ b/solution.py
@@ -199,17 +199,10 @@
 def share_z_kernel(
     own, maps, from_low, from_high, fine, coarse, to_low, to_high, to_low_far, to_high_far, work
 ):
-    low_hi, low_lo = halves(from_high[...])
-    high_hi, high_lo = halves(from_low[...])
+    shares = halves(jnp.concatenate([from_high[...], from_low[...]]))
+    place = maps[256:]
     turned = ((0,), (0,))
-    place_low, place_high = maps[256:272], maps[272:]
-    work[...] = (
-        own[...]
-        + dot(low_hi, place_low, turned)
-        + dot(low_lo, place_low, turned)
-        + dot(high_hi, place_high, turned)
-        + dot(high_lo, place_high, turned)
-    )
+    work[...] = own[...] + dot(jnp.concatenate(shares), jnp.concatenate([place, place]), turned)
     lanes = Lanes()
     for f in range(F):
         for half in (0, 8):

time: 102 us -> 101 us (level)
  no operation moved by 1% of the time
where the time goes in v9:
time: 101 us
  starting transfers between devices  52.7 us (52%)
  waiting for transfers between devices  23.2 us (23%)
  blocking collectives  14.2 us (14%)
  Pallas kernels  7.41 us (7%)
  local copies, waits for them, and re-layouts  1.34 us (1%)
    ppermute x10, starting transfers between devices, shift(): lax.ppermute(array, axis, [(i, (i + by) % count) for i in range(count)])  42.3 us
    all_gather x1, blocking collectives, body(): band = lax.all_gather(band, 'gz', axis=0, tiled=True)  14.2 us
    all_to_all x1, waiting for transfers between devices, body(): lax.all_to_all(outbox.reshape(64, 32, LN), ('gx', 'gy'), split_axis=0, co...  12.3 us
    ppermute x10, waiting for transfers between devices, shift(): lax.ppermute(array, axis, [(i, (i + by) % count) for i in range(count)])  10.9 us
    all_to_all x1, starting transfers between devices, body(): lax.all_to_all(outbox.reshape(64, 32, LN), ('gx', 'gy'), split_axis=0, co...  10.5 us
    pallas_call x8, Pallas kernels, call(): pl.pallas_call(kernel, out_shape=list(outs), in_specs=specs or [VM] * len...  7.41 us
  transfers between devices with their start and end apart: 11, of which 6 were waited for; matrix products, arithmetic and copies ran while one was open for 1% of the time, Pallas kernels for 2%

profile of v9, /device:TPU:2, one launch (start us, length us, event | category | flops | bytes accessed | tf_op | source)
XLA Modules:
  0.0 100.7 jit_solution(12407870197163981100)
XLA Ops:
  0.6 1.9 %shard_map.68 = (f32[16,1280]{1,0:T(8,128)S(1)}, f32[16,1280]{1,0:T(8,128)S(1)}, f32[1280,128]{1,0:T(8,128)S(1)}, bf16[288,256]{1,0:T(8,128)(2,1)S(1)}, s32[1,80]{1,0:T(1,128)S(1)}) custom-call(f32[1280,128]{1,0:T(8,128)} %bitcast.16, bf16[64,128]{1,0:T(8,128)(2,1)} %constant.6.clone.send, bf16[288,256]{1,0:T(8,128)(2,1)} %constant.7.clone.maps, ...), custom_call_target="tpu_custom_call" | custom-call | flops 1048576 | bytes 2097792 | tf_op jit(solution)/shard_map/pallas_call | solution.py:382
  2.6 3.4 %collective-permute-start = (f32[16,1280]{1,0:T(8,128)S(1)}, f32[16,1280]{1,0:T(8,128)S(1)}, u32[]{:S(2)}, u32[]{:S(2)}) collective-permute-start(f32[16,1280]{1,0:T(8,128)S(1)} %get-tuple-element.32), channel_id=1, source_target_pairs={{0,16},{16,32},{32,48},{48,64},{64,80},{80,96},{96,112},{112,0},{1... | collective-permute-start | bytes 245768 | tf_op jit(solution)/shard_map/ppermute | solution.py:396
  6.0 13.6 %collective-permute-start.1 = (f32[16,1280]{1,0:T(8,128)S(1)}, f32[16,1280]{1,0:T(8,128)S(1)}, u32[]{:S(2)}, u32[]{:S(2)}) collective-permute-start(f32[16,1280]{1,0:T(8,128)S(1)} %get-tuple-element.33), channel_id=1, source_target_pairs={{0,112},{16,0},{32,16},{48,32},{64,48},{80,64},{96,80},{112,96},{1... | collective-permute-start | bytes 245768 | tf_op jit(solution)/shard_map/ppermute | solution.py:396
  19.6 0.7 shard_map.69
  20.3 0.0 collective-permute-done.from_low
  20.3 1.4 %collective-permute-done.1.from_high = f32[16,1280]{1,0:T(8,128)S(1)} collective-permute-done((f32[16,1280]{1,0:T(8,128)S(1)}, f32[16,1280]{1,0:T(8,128)S(1)}, u32[]{:S(2)}, u32[]{:S(2)}) %collective-permute-start.1) | collective-permute-done | bytes 81952 | tf_op jit(solution)/shard_map/ppermute | solution.py:396
  21.6 1.1 %shard_map.70 = (f32[1280,128]{1,0:T(8,128)S(1)}, f32[640,128]{1,0:T(8,128)S(1)}, f32[5,8,16,128]{3,2,1,0:T(8,128)S(1)}, f32[5,7,16,128]{3,2,1,0:T(8,128)S(1)}, ...) custom-call(f32[1280,256]{1,0:T(8,128)S(1)} %get-tuple-element.31.own, bf16[288,256]{1,0:T(8,128)(2,1)S(1)} %get-tuple-element.29.maps, ...), custom_call_target="tpu_custom_call" | custom-call | flops 1048576 | bytes 3448832 | tf_op jit(solution)/shard_map/pallas_call | solution.py:382
  22.7 4.1 %collective-permute-start.2 = (f32[5,8,16,128]{3,2,1,0:T(8,128)S(1)}, f32[5,8,16,128]{3,2,1,0:T(8,128)S(1)}, u32[]{:S(2)}, u32[]{:S(2)}) collective-permute-start(f32[5,8,16,128]{3,2,1,0:T(8,128)S(1)} %get-tuple-element.35), channel_id=1, source_target_pairs={{0,15},{1,0},{2,1},{3,2},{4,3},{5,4},{6,5},{7,6},{8,7},{9,8},{10,9... | collective-permute-start | bytes 983048 | tf_op jit(solution)/shard_map/ppermute | solution.py:396
  26.8 0.0 collective-permute-start.3
  26.8 4.4 %collective-permute-start.4 = (f32[5,16,128]{2,1,0:T(8,128)S(1)}, f32[5,16,128]{2,1,0:T(8,128)S(1)}, u32[]{:S(2)}, u32[]{:S(2)}) collective-permute-start(f32[5,16,128]{2,1,0:T(8,128)S(1)} %get-tuple-element.39), channel_id=1, source_target_pairs={{0,14},{1,15},{2,0},{3,1},{4,2},{5,3},{6,4},{7,5},{8,6},{9,7},{10,... | collective-permute-start | bytes 122888 | tf_op jit(solution)/shard_map/ppermute | solution.py:396
  31.2 1.9 %collective-permute-start.5 = (f32[5,16,128]{2,1,0:T(8,128)S(1)}, f32[5,16,128]{2,1,0:T(8,128)S(1)}, u32[]{:S(2)}, u32[]{:S(2)}) collective-permute-start(f32[5,16,128]{2,1,0:T(8,128)S(1)} %get-tuple-element.40), channel_id=1, source_target_pairs={{0,2},{1,3},{2,4},{3,5},{4,6},{5,7},{6,8},{7,9},{8,10},{9,11},{10,... | collective-permute-start | bytes 122888 | tf_op jit(solution)/shard_map/ppermute | solution.py:396
  33.2 0.9 collective-permute-done.3.from_low
  34.1 0.0 collective-permute-done.2.from_high
  34.1 0.4 shard_map.71
  34.5 0.0 collective-permute-done.4.from_high_far
  34.6 3.8 %collective-permute-done.5.from_low_far = f32[5,16,128]{2,1,0:T(8,128)S(1)} collective-permute-done((f32[5,16,128]{2,1,0:T(8,128)S(1)}, f32[5,16,128]{2,1,0:T(8,128)S(1)}, u32[]{:S(2)}, u32[]{:S(2)}) %collective-permute-start.5) | collective-permute-done | bytes 40992 | tf_op jit(solution)/shard_map/ppermute | solution.py:396
  38.4 0.5 shard_map.72
  38.9 6.2 %collective-permute-start.6 = (f32[480,128]{1,0:T(8,128)S(1)}, f32[480,128]{1,0:T(8,128)S(1)}, u32[]{:S(2)}, u32[]{:S(2)}) collective-permute-start(f32[480,128]{1,0:T(8,128)S(1)} %get-tuple-element.43), channel_id=1, source_target_pairs={{0,896},{128,0},{256,128},{384,256},{512,384},{640,512},{768,640},... | collective-permute-start | bytes 737288 | tf_op jit(solution)/shard_map/ppermute | solution.py:396
  45.1 1.9 %collective-permute-start.7 = (f32[400,128]{1,0:T(8,128)S(1)}, f32[400,128]{1,0:T(8,128)S(1)}, u32[]{:S(2)}, u32[]{:S(2)}) collective-permute-start(f32[400,128]{1,0:T(8,128)S(1)} %get-tuple-element.44), channel_id=1, source_target_pairs={{0,128},{128,256},{256,384},{384,512},{512,640},{640,768},{768,896... | collective-permute-start | bytes 614408 | tf_op jit(solution)/shard_map/ppermute | solution.py:396
  47.0 4.6 %collective-permute-start.8 = (f32[40,128]{1,0:T(8,128)S(1)}, f32[40,128]{1,0:T(8,128)S(1)}, u32[]{:S(2)}, u32[]{:S(2)}) collective-permute-start(f32[40,128]{1,0:T(8,128)S(1)} %get-tuple-element.47), channel_id=1, source_target_pairs={{0,768},{128,896},{256,0},{384,128},{512,256},{640,384},{768,512},... | collective-permute-start | bytes 61448 | tf_op jit(solution)/shard_map/ppermute | solution.py:396
  51.6 2.1 %collective-permute-start.9 = (f32[40,128]{1,0:T(8,128)S(1)}, f32[40,128]{1,0:T(8,128)S(1)}, u32[]{:S(2)}, u32[]{:S(2)}) collective-permute-start(f32[40,128]{1,0:T(8,128)S(1)} %get-tuple-element.48), channel_id=1, source_target_pairs={{0,256},{128,384},{256,512},{384,640},{512,768},{640,896},{768,0},... | collective-permute-start | bytes 61448 | tf_op jit(solution)/shard_map/ppermute | solution.py:396
  53.8 0.9 collective-permute-done.7.from_low
  54.7 0.0 collective-permute-done.6.from_high
  54.7 0.8 shard_map.73
  55.6 0.0 collective-permute-done.8.from_high_far
  55.6 3.9 %collective-permute-done.9.from_low_far = f32[40,128]{1,0:T(8,128)S(1)} collective-permute-done((f32[40,128]{1,0:T(8,128)S(1)}, f32[40,128]{1,0:T(8,128)S(1)}, u32[]{:S(2)}, u32[]{:S(2)}) %collective-permute-start.9) | collective-permute-done | bytes 20512 | tf_op jit(solution)/shard_map/ppermute | solution.py:396
  59.4 1.8 %shard_map.74 = (f32[2048,128]{1,0:T(8,128)}, f32[2048,128]{1,0:T(8,128)S(1)}, f32[80,128]{1,0:T(8,128)S(1)}) custom-call(s32[80]{0:T(128)S(1)} %bitcast.15, f32[1280,128]{1,0:T(8,128)S(1)} %get-tuple-element.45.tiles, f32[8,40,128]{2,1,0:T(8,128)S(1)} %get-tuple-element.46.coarse, ...), custom_call_target="tpu_custom_call", output_to_operand_aliasing={{1}: (7, {})} | custom-call | flops 1048576 | bytes 4497728 | tf_op jit(solution)/shard_map/pallas_call | solution.py:382
  61.2 0.0 copy-start
  61.2 10.5 %all-to-all-start = ((f32[64,32,128]{2,1,0:T(8,128)}), f32[64,32,128]{2,1,0:T(8,128)S(1)}, u32[]{:S(2)}, u32[]{:S(2)}) async-start(f32[64,32,128]{2,1,0:T(8,128)} %bitcast.7), calls=%async_computation | async-start | bytes 2097152 | tf_op jit(solution)/shard_map/all_to_all | solution.py:477
  71.7 0.2 shard_map.75
  71.9 0.1 slice.3
  72.0 0.1 reshape.36
  72.1 14.2 %all-gather = f32[16,2,160]{2,1,0:T(2,128)S(1)} all-gather(f32[1,2,160]{2,1,0:T(2,128)S(1)} %reshape.36), channel_id=1, replica_groups=mesh['gx'=8,'gy'=8,'gz'=16] {'gz'}, dimensions={0}, use_global_device_ids=true | all-gather | bytes 21760 | tf_op jit(solution)/shard_map/all_gather | solution.py:481
  86.3 0.0 copy-done
  86.3 1.0 fusion
  87.3 12.3 %all-to-all-done = f32[64,32,128]{2,1,0:T(8,128)S(1)} async-done(((f32[64,32,128]{2,1,0:T(8,128)}), f32[64,32,128]{2,1,0:T(8,128)S(1)}, u32[]{:S(2)}, u32[]{:S(2)}) %all-to-all-start) | async-done | bytes 1048608 | tf_op jit(solution)/shard_map/all_to_all | solution.py:477
  99.6 1.1 %reshape.35 = f32[128,2048]{1,0:T(8,128)} reshape(f32[64,32,128]{2,1,0:T(8,128)S(1)} %all-to-all-done) | data formatting | bytes 2097152 | tf_op jit(solution)/shard_map/reshape | solution.py:485
  (2 shorter events, 0.0 us)
Async XLA Ops:
  2.6 17.7 %collective-permute-start = (f32[16,1280]{1,0:T(8,128)S(1)}, f32[16,1280]{1,0:T(8,128)S(1)}, u32[]{:S(2)}, u32[]{:S(2)}) collective-permute-start(f32[16,1280]{1,0:T(8,128)S(1)} %get-tuple-element.32), channel_id=1, source_target_pairs={{0,16},{16,32},{32,48},{48,64},{64,80},{80,96},{96,112},{112,0},{1... | collective-permute-start | bytes 245768 | tf_op jit(solution)/shard_map/ppermute | solution.py:396
  6.0 15.7 %collective-permute-start.1 = (f32[16,1280]{1,0:T(8,128)S(1)}, f32[16,1280]{1,0:T(8,128)S(1)}, u32[]{:S(2)}, u32[]{:S(2)}) collective-permute-start(f32[16,1280]{1,0:T(8,128)S(1)} %get-tuple-element.33), channel_id=1, source_target_pairs={{0,112},{16,0},{32,16},{48,32},{64,48},{80,64},{96,80},{112,96},{1... | collective-permute-start | bytes 245768 | tf_op jit(solution)/shard_map/ppermute | solution.py:396
  22.7 11.4 %collective-permute-start.2 = (f32[5,8,16,128]{3,2,1,0:T(8,128)S(1)}, f32[5,8,16,128]{3,2,1,0:T(8,128)S(1)}, u32[]{:S(2)}, u32[]{:S(2)}) collective-permute-start(f32[5,8,16,128]{3,2,1,0:T(8,128)S(1)} %get-tuple-element.35), channel_id=1, source_target_pairs={{0,15},{1,0},{2,1},{3,2},{4,3},{5,4},{6,5},{7,6},{8,7},{9,8},{10,9... | collective-permute-start | bytes 983048 | tf_op jit(solution)/shard_map/ppermute | solution.py:396
  26.8 7.3 %collective-permute-start.3 = (f32[5,7,16,128]{3,2,1,0:T(8,128)S(1)}, f32[5,7,16,128]{3,2,1,0:T(8,128)S(1)}, u32[]{:S(2)}, u32[]{:S(2)}) collective-permute-start(f32[5,7,16,128]{3,2,1,0:T(8,128)S(1)} %get-tuple-element.36), channel_id=1, source_target_pairs={{0,1},{1,2},{2,3},{3,4},{4,5},{5,6},{6,7},{7,8},{8,9},{9,10},{10,1... | collective-permute-start | bytes 860168 | tf_op jit(solution)/shard_map/ppermute | solution.py:396
  26.8 7.7 %collective-permute-start.4 = (f32[5,16,128]{2,1,0:T(8,128)S(1)}, f32[5,16,128]{2,1,0:T(8,128)S(1)}, u32[]{:S(2)}, u32[]{:S(2)}) collective-permute-start(f32[5,16,128]{2,1,0:T(8,128)S(1)} %get-tuple-element.39), channel_id=1, source_target_pairs={{0,14},{1,15},{2,0},{3,1},{4,2},{5,3},{6,4},{7,5},{8,6},{9,7},{10,... | collective-permute-start | bytes 122888 | tf_op jit(solution)/shard_map/ppermute | solution.py:396
  31.2 7.2 %collective-permute-start.5 = (f32[5,16,128]{2,1,0:T(8,128)S(1)}, f32[5,16,128]{2,1,0:T(8,128)S(1)}, u32[]{:S(2)}, u32[]{:S(2)}) collective-permute-start(f32[5,16,128]{2,1,0:T(8,128)S(1)} %get-tuple-element.40), channel_id=1, source_target_pairs={{0,2},{1,3},{2,4},{3,5},{4,6},{5,7},{6,8},{7,9},{8,10},{9,11},{10,... | collective-permute-start | bytes 122888 | tf_op jit(solution)/shard_map/ppermute | solution.py:396
  38.9 15.8 %collective-permute-start.6 = (f32[480,128]{1,0:T(8,128)S(1)}, f32[480,128]{1,0:T(8,128)S(1)}, u32[]{:S(2)}, u32[]{:S(2)}) collective-permute-start(f32[480,128]{1,0:T(8,128)S(1)} %get-tuple-element.43), channel_id=1, source_target_pairs={{0,896},{128,0},{256,128},{384,256},{512,384},{640,512},{768,640},... | collective-permute-start | bytes 737288 | tf_op jit(solution)/shard_map/ppermute | solution.py:396
  45.1 9.6 %collective-permute-start.7 = (f32[400,128]{1,0:T(8,128)S(1)}, f32[400,128]{1,0:T(8,128)S(1)}, u32[]{:S(2)}, u32[]{:S(2)}) collective-permute-start(f32[400,128]{1,0:T(8,128)S(1)} %get-tuple-element.44), channel_id=1, source_target_pairs={{0,128},{128,256},{256,384},{384,512},{512,640},{640,768},{768,896... | collective-permute-start | bytes 614408 | tf_op jit(solution)/shard_map/ppermute | solution.py:396
  47.0 8.5 %collective-permute-start.8 = (f32[40,128]{1,0:T(8,128)S(1)}, f32[40,128]{1,0:T(8,128)S(1)}, u32[]{:S(2)}, u32[]{:S(2)}) collective-permute-start(f32[40,128]{1,0:T(8,128)S(1)} %get-tuple-element.47), channel_id=1, source_target_pairs={{0,768},{128,896},{256,0},{384,128},{512,256},{640,384},{768,512},... | collective-permute-start | bytes 61448 | tf_op jit(solution)/shard_map/ppermute | solution.py:396
  51.6 7.8 %collective-permute-start.9 = (f32[40,128]{1,0:T(8,128)S(1)}, f32[40,128]{1,0:T(8,128)S(1)}, u32[]{:S(2)}, u32[]{:S(2)}) collective-permute-start(f32[40,128]{1,0:T(8,128)S(1)} %get-tuple-element.48), channel_id=1, source_target_pairs={{0,256},{128,384},{256,512},{384,640},{512,768},{640,896},{768,0},... | collective-permute-start | bytes 61448 | tf_op jit(solution)/shard_map/ppermute | solution.py:396
  61.2 25.1 %copy-start = (f32[32,32]{1,0:T(8,128)S(1)}, f32[32,32]{1,0:T(8,128)}, u32[]{:S(2)}) copy-start(f32[32,32]{1,0:T(8,128)} %constant.8.clone) | copy-start | bytes 12292
  61.2 38.4 %all-to-all-start = ((f32[64,32,128]{2,1,0:T(8,128)}), f32[64,32,128]{2,1,0:T(8,128)S(1)}, u32[]{:S(2)}, u32[]{:S(2)}) async-start(f32[64,32,128]{2,1,0:T(8,128)} %bitcast.7), calls=%async_computation | async-start | bytes 2097152 | tf_op jit(solution)/shard_map/all_to_all | solution.py:477
